TPU v7x, 256 devices: a whole 4x4x8 slice. The times are simulated.
256 devices in a mesh: branch: 2 (over core), pair: 128 (over y, x, z).
Axes of the slice: x: 4, y: 4, z: 8, core: 2. Of those that a mesh axis runs over, the one named last changes fastest.
Arguments:
- encoder_rows: bfloat16 [256, 196, 1024], P('pair'), may hold values from -6 to 6
- pair_list: int32 [512, 2], P('pair'), may hold values from 0 to 255, as said below
- embed_weight: bfloat16 [1024, 768], P('pair'), may hold values from -0.1875 to 0.1875
- self_qkv: bfloat16 [2, 768, 2304], P('branch'), may hold values from -0.21875 to 0.21875
- self_out: bfloat16 [2, 768, 768], P('branch'), may hold values from -0.21875 to 0.21875
- cross_q: bfloat16 [2, 768, 768], P('branch'), may hold values from -0.21875 to 0.21875
- cross_kv: bfloat16 [2, 768, 1536], P('branch'), may hold values from -0.21875 to 0.21875
- cross_out: bfloat16 [2, 768, 768], P('branch'), may hold values from -0.21875 to 0.21875
Outputs:
- view_sums: float32 [2, 256, 196, 768], P('branch', 'pair')
Inputs may be any that keep to these rules, and one draw needn't show every extreme that they name: `pair_list`: pair p's first image (column 0) is one of the images p // 4 * 2 to p // 4 * 2 + 1, and every image is the first image of some pair. The second image (column 1) differs from the first and is one of the images (p // 4 - 1) * 2 to (p // 4 + 2) * 2 - 1, counted modulo 256; where p % 4 is 0 it is one of the images (p // 4 + 1) * 2 to (p // 4 + 2) * 2 - 1, and where p % 4 is 1 one of the images (p // 4 - 1) * 2 to p // 4 * 2 - 1, both modulo 256.
All inputs are finite; a program needn't handle non-finite values.
Results may differ from a plain program's by a relative error of at most 0.0034.
Values may be sent and summed in bfloat16 or wider, within the bound.
A program may use at most 64 MiB of HBM per device.

v0:
```python
import math

import jax
import jax.numpy as jnp
from jax import lax
from jax.sharding import PartitionSpec as P

HEADS = 12


def padded(x, sides, width):
    for axis, dim in sides:
        peers, length = (lax.axis_size(axis), x.shape[dim])
        up = [(i, (i + 1) % peers) for i in range(peers)]
        down = [(j, i) for i, j in up]
        last = lax.slice_in_dim(x, length - width, length, axis=dim)
        initial = lax.slice_in_dim(x, 0, width, axis=dim)
        before = lax.ppermute(last, axis, up)
        after = lax.ppermute(initial, axis, down)
        x = jnp.concatenate([before, x, after], axis=dim)
    return x


def swapped(value, axis, bit):
    mask = 2**bit
    pairs = [(source, source ^ mask) for source in range(lax.axis_size(axis))]
    return lax.ppermute(value, axis, pairs)


def layer_norm(values):
    values = values.astype(jnp.float32)
    average = jnp.mean(values, axis=-1, keepdims=True)
    centered = values - average
    spread = jnp.mean(centered * centered, axis=-1, keepdims=True)
    return (centered * lax.rsqrt(spread + 1e-06)).astype(jnp.bfloat16)


def project(values, matrix):
    leading = values.shape[:-1]
    flattened = values.reshape(-1, values.shape[-1])
    result = jnp.dot(flattened, matrix, preferred_element_type=jnp.float32)
    return result.reshape(leading + (matrix.shape[-1],))


def attend(queries, keys_in, values_in):
    pair_count, length, model_width = queries.shape
    head_dim = model_width // HEADS
    query_heads = queries.reshape(pair_count, length, HEADS, head_dim)
    key_heads = keys_in.reshape(pair_count, length, HEADS, head_dim)
    value_heads = values_in.reshape(pair_count, length, HEADS, head_dim)
    scores = jnp.einsum(
        "bqhd,bkhd->bhqk", query_heads, key_heads, preferred_element_type=jnp.float32
    ) * (1.0 / math.sqrt(head_dim))
    raised = jnp.exp(scores)
    attn_probs = (raised / jnp.sum(raised, axis=-1, keepdims=True)).astype(jnp.bfloat16)
    mixed_rows = jnp.einsum(
        "bhqk,bkhd->bqhd", attn_probs, value_heads, preferred_element_type=jnp.float32
    )
    return mixed_rows.reshape(pair_count, length, model_width).astype(jnp.bfloat16)


def attention_part(own_rows, partner_rows, w_qkv, w_self, w_query, w_pair, w_cross):
    model_width = own_rows.shape[-1]
    triple = project(layer_norm(own_rows), w_qkv).astype(jnp.bfloat16)
    attended = attend(
        triple[..., :model_width],
        triple[..., model_width : 2 * model_width],
        triple[..., 2 * model_width :],
    )
    stream = own_rows.astype(jnp.float32) + project(attended, w_self)
    query_rows = project(layer_norm(stream), w_query).astype(jnp.bfloat16)
    pair_kv = project(layer_norm(partner_rows), w_pair).astype(jnp.bfloat16)
    crossed = attend(query_rows, pair_kv[..., :model_width], pair_kv[..., model_width:])
    return stream + project(crossed, w_cross)


def select_rows(onehot, window):
    return jnp.dot(onehot.astype(jnp.bfloat16), window, preferred_element_type=jnp.float32).astype(
        jnp.bfloat16
    )


def embed_picked(onehot, window, full_embed, pair_count, tokens_per, enc_width, model_width):
    picked = select_rows(onehot, window).reshape(pair_count * tokens_per, enc_width)
    embedded_rows = jnp.dot(picked, full_embed, preferred_element_type=jnp.float32).astype(
        jnp.bfloat16
    )
    return embedded_rows.reshape(pair_count, tokens_per, model_width)


def body(encoder_rows, pair_list, embed_weight, self_qkv, self_out, cross_q, cross_kv, cross_out):
    img_local = encoder_rows.shape[0]
    tokens_per = encoder_rows.shape[1]
    enc_width = encoder_rows.shape[2]
    pair_count = pair_list.shape[0]
    views_local = self_qkv.shape[0]
    devices = lax.axis_size("pair")
    device_id = lax.axis_index("pair")
    branch_id = lax.axis_index("branch")
    image_total = img_local * devices
    window_start = (device_id - 1) * img_local
    slot_index = jnp.arange(3 * img_local, dtype=jnp.int32)
    other_onehots = []
    local_view = 0
    view_id = branch_id * views_local + local_view
    own_ids = jnp.where(view_id == 0, pair_list[:, 0], pair_list[:, 1])
    other_ids = jnp.where(view_id == 0, pair_list[:, 1], pair_list[:, 0])
    own_place = jnp.mod(own_ids - window_start, image_total)
    other_place = jnp.mod(other_ids - window_start, image_total)
    own_places = [own_place]
    own_onehots = own_place[:, None] == slot_index[None, :]
    other_onehots.append(other_place[:, None] == slot_index[None, :])
    full_embed = lax.all_gather(embed_weight, "pair", axis=0, tiled=True)
    model_width = full_embed.shape[1]
    raw_local = encoder_rows.reshape(img_local, tokens_per * enc_width)
    window = padded(raw_local, (("pair", 0),), img_local)
    own_list = [
        embed_picked(
            own_onehots, window, full_embed, pair_count, tokens_per, enc_width, model_width
        )
    ]
    partner_list = [swapped(own_list[0], "branch", 0)]
    local_view = 0
    decoded = attention_part(
        own_list[local_view],
        partner_list[local_view],
        self_qkv[local_view],
        self_out[local_view],
        cross_q[local_view],
        cross_kv[local_view],
        cross_out[local_view],
    )
    place_onehot = (slot_index[:, None] == own_places[local_view][None, :]).astype(jnp.float32)
    contribution_list = [
        jnp.dot(
            place_onehot,
            decoded.reshape(pair_count, tokens_per * model_width),
            precision=lax.Precision.HIGHEST,
        )
    ]
    contributions = jnp.stack(contribution_list, axis=0)
    rim_rows = jnp.concatenate(
        [contributions[:, :img_local], contributions[:, 2 * img_local :]], axis=1
    )
    extended = padded(rim_rows, (("pair", 1),), img_local)
    image_sums = (
        contributions[:, img_local : 2 * img_local]
        + extended[:, :img_local]
        + extended[:, 3 * img_local :]
    )
    return image_sums.reshape(views_local, img_local, tokens_per, model_width)


def solution(mesh):
    placed = (
        P("pair", None, None),
        P("pair", None),
        P("pair", None),
        P("branch", None, None),
        P("branch", None, None),
        P("branch", None, None),
        P("branch", None, None),
        P("branch", None, None),
    )
    return jax.shard_map(
        body, mesh=mesh, in_specs=placed, out_specs=P("branch", "pair", None, None), check_vma=False
    )
```

profile of v0, /device:TPU:1, one launch (start us, length us, event | category | flops | bytes accessed | tf_op | source)
XLA Modules:
  0.0 225.7 jit_solution(11989858726416793992)
XLA Ops:
  6.5 0.0 copy-start
  6.5 0.0 all-gather.2.cloned.1.call-start
  6.5 0.7 all-gather.2.cloned.1.call-update
  7.3 2.5 %collective-permute-start = (bf16[2,200704]{1,0:T(2,128)(2,1)}, bf16[2,200704]{1,0:T(2,128)(2,1)}, u32[]{:S(2)}, u32[]{:S(2)}) collective-permute-start(bf16[2,200704]{1,0:T(2,128)(2,1)} %bitcast.65), channel_id=1, source_target_pairs={{0,1},{1,2},{2,3},{3,4},{4,5},{5,6},{6,7},{7,8},{8,9},{9,10},{10,1... | collective-permute-start | bytes 2408456 | tf_op jit(solution)/shard_map/ppermute | solution.py:18
  9.8 8.7 %collective-permute-start.1 = (bf16[2,200704]{1,0:T(2,128)(2,1)}, bf16[2,200704]{1,0:T(2,128)(2,1)}, u32[]{:S(2)}, u32[]{:S(2)}) collective-permute-start(bf16[2,200704]{1,0:T(2,128)(2,1)} %bitcast.66), channel_id=1, source_target_pairs={{1,0},{2,1},{3,2},{4,3},{5,4},{6,5},{7,6},{8,7},{9,8},{10,9},{11,1... | collective-permute-start | bytes 2408456 | tf_op jit(solution)/shard_map/ppermute | solution.py:19
  18.5 0.8 and_select_fusion.1
  19.2 17.0 %collective-permute-done = bf16[2,200704]{1,0:T(2,128)(2,1)} collective-permute-done((bf16[2,200704]{1,0:T(2,128)(2,1)}, bf16[2,200704]{1,0:T(2,128)(2,1)}, u32[]{:S(2)}, u32[]{:S(2)}) %collective-permute-start) | collective-permute-done | bytes 802848 | tf_op jit(solution)/shard_map/ppermute | solution.py:18
  36.3 0.0 collective-permute-done.1
  36.3 5.6 %convolution_convert_fusion = bf16[4,200704]{1,0:T(4,128)(2,1)} fusion(bf16[2,200704]{1,0:T(2,128)(2,1)} %collective-permute-done.1, bf16[2,200704]{1,0:T(2,128)(2,1)} %bitcast.67, bf16[2,200704]{1,0:T(2,128)(2,1)} %collective-permute-done, s32[4]{0:T(128)S(1)} %fusion.31), kind=kOutput, calls=%fused_computation | convolution fusion | flops 17661976 | bytes 4014096 | tf_op jit(solution)/shard_map/dot_general | solution.py:78
  41.9 3.6 %reshape.134 = bf16[784,1024]{1,0:T(8,128)(2,1)} reshape(bf16[4,200704]{1,0:T(4,128)(2,1)} %convolution_convert_fusion) | data formatting | bytes 3211264 | tf_op jit(solution)/shard_map/reshape | solution.py:84
  45.5 68.6 %all-gather.2.cloned.1.call-done = bf16[1024,768]{1,0:T(8,128)(2,1)} async-done(((bf16[8,768]{1,0:T(8,128)(2,1)}), bf16[1024,768]{1,0:T(8,128)(2,1)}) %all-gather.2.cloned.1.call-update) | async-done | bytes 1572880 | tf_op jit(solution)/shard_map/all_gather | solution.py:113
  114.0 4.3 %convert_reduce_fusion.1 = (f32[784]{0:T(1024)S(1)}, bf16[784,768]{1,0:T(8,128)(2,1)}) fusion(bf16[784,1024]{1,0:T(8,128)(2,1)} %reshape.134, bf16[1024,768]{1,0:T(8,128)(2,1)} %all-gather.2.cloned.1.call-done), kind=kOutput, calls=%fused_computation.21 | convolution fusion | flops 1234930944 | bytes 4385856 | tf_op jit(solution)/shard_map/dot_general | solution.py:85
  118.4 2.2 reshape.135
  120.6 1.8 fusion.16
  122.4 2.7 %fusion.17 = bf16[784,768]{1,0:T(8,128)(2,1)} fusion(bf16[784,768]{1,0:T(8,128)(2,1)} %get-tuple-element.15, f32[784]{0:T(1024)S(1)} %add_rsqrt_fusion.2, f32[784]{0:T(1024)S(1)} %broadcast_multiply_fusion.2), kind=kLoop, calls=%fused_computation.33 | loop fusion | flops 2408448 | bytes 2414720 | tf_op jit(solution)/shard_map/convert_element_type | solution.py:35
  125.1 2.2 dot_general.40
  127.3 0.0 copy-done
  127.3 4.8 %convolution_convert_fusion.1 = bf16[4,196,2304]{2,1,0:T(8,128)(2,1)S(1)} fusion(bf16[4,196,768]{2,1,0:T(8,128)(2,1)} %dot_general.40, bf16[1,768,2304]{2,1,0:T(8,128)(2,1)S(1)} %copy-done), kind=kOutput, calls=%fused_computation.8 | convolution fusion | flops 2776338432 | bytes 8355840 | tf_op jit(solution)/shard_map/dot_general | solution.py:41
  132.1 1.9 fusion.39
  134.0 1.6 copy.78
  135.7 2.5 %copy.79 = bf16[4,196,768]{1,2,0:T(8,128)(2,1)} copy(bf16[4,196,768]{2,1,0:T(8,128)(2,1)} %get-tuple-element.9) | data formatting | bytes 2408448 | tf_op jit(solution)/shard_map/slice | solution.py:67
  138.2 2.5 %copy.77 = bf16[4,196,768]{1,2,0:T(8,128)(2,1)} copy(bf16[4,196,768]{2,1,0:T(8,128)(2,1)} %get-tuple-element.11) | data formatting | bytes 2408448 | tf_op jit(solution)/shard_map/slice | solution.py:68
  140.7 2.9 %copy.82 = bf16[4,196,768]{2,0,1:T(4,128)(2,1)} copy(bf16[4,196,768]{2,1,0:T(8,128)(2,1)} %reshape.135) | data formatting | bytes 2408448 | tf_op jit(solution)/shard_map/reshape | solution.py:88
  143.6 4.8 %collective-permute-start.2 = (bf16[4,196,768]{2,0,1:T(4,128)(2,1)}, bf16[4,196,768]{2,0,1:T(4,128)(2,1)S(1)}, u32[]{:S(2)}, u32[]{:S(2)}) collective-permute-start(bf16[4,196,768]{2,0,1:T(4,128)(2,1)} %copy.82), channel_id=1, source_target_pairs={{0,128},{128,0},{1,129},{129,1},{2,130},{130,2},{3,131},{131,3},{4... | collective-permute-start | bytes 3612680 | tf_op jit(solution)/shard_map/ppermute | solution.py:27
  148.4 0.0 copy-done.4
  148.4 2.1 fusion
  150.5 0.0 copy-done.6
  150.5 0.0 copy-start.5
  150.5 0.0 copy-start.10
  150.5 2.2 fusion.20
  152.7 0.0 copy-done.5
  152.7 0.0 copy-done.10
  152.7 1.3 fusion.41
  154.1 0.0 copy-start.11
  154.1 0.4 multiply_reduce_fusion
  154.5 1.0 copy-done.2
  155.5 0.7 copy-done.11
  156.2 2.3 %convolution_convert_fusion.3 = bf16[4,196,768]{2,1,0:T(8,128)(2,1)} fusion(f32[4,196,768]{2,1,0:T(8,128)S(1)} %get-tuple-element.19, f32[4,196]{1,0:T(4,128)S(1)} %add_rsqrt_fusion.1, f32[4,196]{1,0:T(4,128)S(1)} %broadcast_multiply_fusion.1, bf16[1,768,768]{2,1,0:T(8,128)(2,1)S(1)} %copy-done.11), kind=kOutput, calls=%fused_computation.37 | convolution fusion | flops 927252480 | bytes 4798592 | tf_op jit(solution)/shard_map/dot_general | solution.py:41
  158.5 1.6 copy.89
  160.1 0.0 collective-permute-done.2
  160.1 0.5 convert_reduce_fusion
  160.7 0.0 copy-start.9
  160.7 1.2 fusion.14
  161.9 0.9 fusion.15
  162.8 0.0 copy-done.9
  162.8 2.1 convolution_convert_fusion.2
  164.9 1.6 fusion.40
  166.5 2.5 %copy.90 = bf16[4,196,768]{1,2,0:T(8,128)(2,1)} copy(bf16[4,196,768]{2,1,0:T(8,128)(2,1)} %get-tuple-element.12) | data formatting | bytes 2408448 | tf_op jit(solution)/shard_map/slice | solution.py:73
  169.0 2.5 %copy.88 = bf16[4,196,768]{1,2,0:T(8,128)(2,1)} copy(bf16[4,196,768]{2,1,0:T(8,128)(2,1)} %get-tuple-element.13) | data formatting | bytes 2408448 | tf_op jit(solution)/shard_map/slice | solution.py:73
  171.6 3.7 %fusion.1 = (f32[4,12,196]{2,1,0:T(8,128)S(1)}, f32[4,12,196,196]{2,3,1,0:T(8,128)S(1)}) fusion(bf16[4,196,12,64]{1,3,2,0:T(8,128)(2,1)S(1)} %bitcast.58, bf16[4,196,12,64]{1,3,2,0:T(8,128)(2,1)} %bitcast.61), kind=kOutput, calls=%fused_computation.7 | convolution fusion | flops 239706432 | bytes 9821952 | tf_op jit(solution)/shard_map/bqhd,bkhd->bhqk/dot_general | solution.py:51
  175.2 0.0 copy-done.7
  175.3 0.0 copy-start.8
  175.3 2.4 %fusion.19 = bf16[4,12,64,196]{3,2,1,0:T(8,128)(2,1)S(1)} fusion(bf16[4,196,12,64]{1,3,2,0:T(8,128)(2,1)S(1)} %bitcast.63, f32[4,12,196,196]{2,3,1,0:T(8,128)S(1)} %get-tuple-element.21, f32[4,12,196]{2,1,0:T(8,128)S(1)} %get-tuple-element.20), kind=kOutput, calls=%fused_computation.35 | convolution fusion | flops 242161920 | bytes 9821952 | tf_op jit(solution)/shard_map/bhqk,bkhd->bqhd/dot_general | solution.py:56
  177.6 0.0 copy-done.3
  177.7 0.0 copy-done.8
  177.7 1.2 add_bitcast_fusion
  178.9 0.9 copy.98
  179.8 2.4 %convolution_bitcast_fusion = f32[1,6,150528]{2,1,0:T(8,128)S(1)} fusion(f32[4,150528]{1,0:T(4,128)S(1)} %bitcast.57, s32[4]{0:T(128)S(1)} %get-tuple-element.5), kind=kOutput, calls=%fused_computation.1 | convolution fusion | flops 43352088 | bytes 6021136 | tf_op jit(solution)/shard_map/dot_general | solution.py:135
  182.3 1.0 fusion.38
  183.3 1.2 collective-permute-start.3
  184.4 5.8 %collective-permute-start.4 = (f32[1,2,150528]{2,1,0:T(2,128)S(1)}, f32[1,2,150528]{2,1,0:T(2,128)S(1)}, u32[]{:S(2)}, u32[]{:S(2)}) collective-permute-start(f32[1,2,150528]{2,1,0:T(2,128)S(1)} %get-tuple-element.8), channel_id=1, source_target_pairs={{1,0},{2,1},{3,2},{4,3},{5,4},{6,5},{7,6},{8,7},{9,8},{10,9},{11,1... | collective-permute-start | bytes 3612680 | tf_op jit(solution)/shard_map/ppermute | solution.py:19
  190.2 26.6 %collective-permute-done.3 = f32[1,2,150528]{2,1,0:T(2,128)S(1)} collective-permute-done((f32[1,2,150528]{2,1,0:T(2,128)S(1)}, f32[1,2,150528]{2,1,0:T(2,128)S(1)}, u32[]{:S(2)}, u32[]{:S(2)}) %collective-permute-start.3) | collective-permute-done | bytes 1204256 | tf_op jit(solution)/shard_map/ppermute | solution.py:18
  216.8 0.0 collective-permute-done.4
  216.8 2.0 fusion.24
  (14 shorter events, 0.1 us)
Async XLA Ops:
  6.5 120.8 %copy-start = (bf16[1,768,2304]{2,1,0:T(8,128)(2,1)S(1)}, bf16[1,768,2304]{2,1,0:T(8,128)(2,1)}, u32[]{:S(2)}) copy-start(bf16[1,768,2304]{2,1,0:T(8,128)(2,1)} %param.11) | copy-start | bytes 10616836
  6.5 107.5 %all-gather.2.cloned.1.call-start = ((), (), s32[]{:S(2)}) async-start(), calls=%async_computation | async-start | bytes 1585152 | tf_op jit(solution)/shard_map/all_gather | solution.py:113
  7.3 29.0 %collective-permute-start = (bf16[2,200704]{1,0:T(2,128)(2,1)}, bf16[2,200704]{1,0:T(2,128)(2,1)}, u32[]{:S(2)}, u32[]{:S(2)}) collective-permute-start(bf16[2,200704]{1,0:T(2,128)(2,1)} %bitcast.65), channel_id=1, source_target_pairs={{0,1},{1,2},{2,3},{3,4},{4,5},{5,6},{6,7},{7,8},{8,9},{9,10},{10,1... | collective-permute-start | bytes 2408456 | tf_op jit(solution)/shard_map/ppermute | solution.py:18
  9.8 26.5 %collective-permute-start.1 = (bf16[2,200704]{1,0:T(2,128)(2,1)}, bf16[2,200704]{1,0:T(2,128)(2,1)}, u32[]{:S(2)}, u32[]{:S(2)}) collective-permute-start(bf16[2,200704]{1,0:T(2,128)(2,1)} %bitcast.66), channel_id=1, source_target_pairs={{1,0},{2,1},{3,2},{4,3},{5,4},{6,5},{7,6},{8,7},{9,8},{10,9},{11,1... | collective-permute-start | bytes 2408456 | tf_op jit(solution)/shard_map/ppermute | solution.py:19
  140.7 7.7 %copy-start.4 = (bf16[4,196,768]{1,2,0:T(8,128)(2,1)S(1)}, bf16[4,196,768]{1,2,0:T(8,128)(2,1)}, u32[]{:S(2)}) copy-start(bf16[4,196,768]{1,2,0:T(8,128)(2,1)} %copy.79) | copy-start | bytes 3612676
  143.6 16.5 %collective-permute-start.2 = (bf16[4,196,768]{2,0,1:T(4,128)(2,1)}, bf16[4,196,768]{2,0,1:T(4,128)(2,1)S(1)}, u32[]{:S(2)}, u32[]{:S(2)}) collective-permute-start(bf16[4,196,768]{2,0,1:T(4,128)(2,1)} %copy.82), channel_id=1, source_target_pairs={{0,128},{128,0},{1,129},{129,1},{2,130},{130,2},{3,131},{131,3},{4... | collective-permute-start | bytes 3612680 | tf_op jit(solution)/shard_map/ppermute | solution.py:27
  148.4 2.1 copy-start.6
  150.5 2.2 copy-start.5
  150.5 2.2 copy-start.10
  154.1 1.4 copy-start.2
  154.1 2.1 copy-start.11
  160.7 2.1 copy-start.9
  171.6 3.7 %copy-start.7 = (bf16[4,196,768]{1,2,0:T(8,128)(2,1)S(1)}, bf16[4,196,768]{1,2,0:T(8,128)(2,1)}, u32[]{:S(2)}) copy-start(bf16[4,196,768]{1,2,0:T(8,128)(2,1)} %copy.88) | copy-start | bytes 3612676
  175.2 2.4 %copy-start.3 = (f32[4,196,768]{2,1,0:T(8,128)S(1)}, f32[4,196,768]{2,1,0:T(8,128)}, u32[]{:S(2)}) copy-start(f32[4,196,768]{2,1,0:T(8,128)} %copy-done.2) | copy-start | bytes 7225348
  175.3 2.4 %copy-start.8 = (bf16[1,768,768]{2,1,0:T(8,128)(2,1)S(1)}, bf16[1,768,768]{2,1,0:T(8,128)(2,1)}, u32[]{:S(2)}) copy-start(bf16[1,768,768]{2,1,0:T(8,128)(2,1)} %param.15) | copy-start | bytes 3538948
  183.3 33.6 %collective-permute-start.3 = (f32[1,2,150528]{2,1,0:T(2,128)S(1)}, f32[1,2,150528]{2,1,0:T(2,128)S(1)}, u32[]{:S(2)}, u32[]{:S(2)}) collective-permute-start(f32[1,2,150528]{2,1,0:T(2,128)S(1)} %get-tuple-element.7), channel_id=1, source_target_pairs={{0,1},{1,2},{2,3},{3,4},{4,5},{5,6},{6,7},{7,8},{8,9},{9,10},{10,1... | collective-permute-start | bytes 3612680 | tf_op jit(solution)/shard_map/ppermute | solution.py:18
  184.4 34.4 %copy-start.1 = (bf16[1,768,2304]{2,1,0:T(8,128)(2,1)S(1)}, bf16[1,768,2304]{2,1,0:T(8,128)(2,1)}, u32[]{:S(2)}) copy-start(bf16[1,768,2304]{2,1,0:T(8,128)(2,1)} %param.11) | copy-start | bytes 10616836
  184.4 32.4 %collective-permute-start.4 = (f32[1,2,150528]{2,1,0:T(2,128)S(1)}, f32[1,2,150528]{2,1,0:T(2,128)S(1)}, u32[]{:S(2)}, u32[]{:S(2)}) collective-permute-start(f32[1,2,150528]{2,1,0:T(2,128)S(1)} %get-tuple-element.8), channel_id=1, source_target_pairs={{1,0},{2,1},{3,2},{4,3},{5,4},{6,5},{7,6},{8,7},{9,8},{10,9},{11,1... | collective-permute-start | bytes 3612680 | tf_op jit(solution)/shard_map/ppermute | solution.py:19
Sparse Core Ops, SparseCore 0:
  10.8 103.2 all-gather.1
where the time goes:
time: 226 us
  waiting for transfers between devices  113 us (50%)
  matrix products  34.4 us (15%)
  local copies, waits for them, and re-layouts  31.5 us (14%)
  starting transfers between devices  23 us (10%)
  between operations  13.7 us (6%)
  other arithmetic  10.3 us (5%)
    all_gather x1, waiting for transfers between devices, body(): full_embed = lax.all_gather(embed_weight, 'pair', axis=0, tiled=True)  68.6 us
    ppermute x2, waiting for transfers between devices, padded(): before = lax.ppermute(last, axis, up)  43.6 us
    ppermute x2, starting transfers between devices, padded(): after = lax.ppermute(initial, axis, down)  14.5 us
    dot_general x5, matrix products, project(): result = jnp.dot(flattened, matrix, preferred_element_type=jnp.float32)  11.8 us
    dot_general x2, matrix products, attend(): jnp.einsum('bqhd,bkhd->bhqk', query_heads, key_heads, preferred_element_t...  5.76 us
    dot_general x1, matrix products, select_rows(): jnp.dot(onehot.astype(jnp.bfloat16), window, preferred_element_type=jnp.f...  5.59 us
    reshape x2, local copies, waits for them, and re-layouts, embed_picked(): return embedded_rows.reshape(pair_count, tokens_per, model_width)  5.13 us
    ppermute x1, starting transfers between devices, swapped(): return lax.ppermute(value, axis, pairs)  4.77 us
  transfers between devices with their start and end apart: 6, of which 3 were waited for; matrix products, arithmetic and copies ran while one was open for 9% of the time, Pallas kernels for 0%

commit v1 on v0

--- a/solution.py
+++ b/solution.py
@@ -19,6 +19,29 @@
         after = lax.ppermute(initial, axis, down)
         x = jnp.concatenate([before, x, after], axis=dim)
     return x
+
+
+def branch_one_padded(x, dim, width):
+    peers, length = (lax.axis_size("pair"), x.shape[dim])
+    base = peers
+    up = [(base + i, base + (i + 1) % peers) for i in range(peers)]
+    down = [(j, i) for i, j in up]
+    last = lax.slice_in_dim(x, length - width, length, axis=dim)
+    initial = lax.slice_in_dim(x, 0, width, axis=dim)
+    before = lax.ppermute(last, ("branch", "pair"), up)
+    after = lax.ppermute(initial, ("branch", "pair"), down)
+    return jnp.concatenate([before, x, after], axis=dim)
+
+
+def gathered_weight(weight, branch_id, devices):
+    half = weight.shape[1] // 2
+    mine = lax.dynamic_slice_in_dim(weight, branch_id * half, half, 1)
+    spread = jnp.broadcast_to(mine[None], (devices,) + mine.shape)
+    got = lax.all_to_all(spread, "pair", 0, 0, tiled=True).reshape(-1, half)
+    other = lax.ppermute(got, "branch", [(0, 1), (1, 0)])
+    return jnp.where(
+        branch_id == 0, jnp.concatenate([got, other], 1), jnp.concatenate([other, got], 1)
+    )
 
 
 def swapped(value, axis, bit):
@@ -110,10 +133,10 @@
     own_places = [own_place]
     own_onehots = own_place[:, None] == slot_index[None, :]
     other_onehots.append(other_place[:, None] == slot_index[None, :])
-    full_embed = lax.all_gather(embed_weight, "pair", axis=0, tiled=True)
+    full_embed = gathered_weight(embed_weight, branch_id, devices)
     model_width = full_embed.shape[1]
     raw_local = encoder_rows.reshape(img_local, tokens_per * enc_width)
-    window = padded(raw_local, (("pair", 0),), img_local)
+    window = branch_one_padded(raw_local, 0, img_local)
     own_list = [
         embed_picked(
             own_onehots, window, full_embed, pair_count, tokens_per, enc_width, model_width
@@ -142,7 +165,7 @@
     rim_rows = jnp.concatenate(
         [contributions[:, :img_local], contributions[:, 2 * img_local :]], axis=1
     )
-    extended = padded(rim_rows, (("pair", 1),), img_local)
+    extended = branch_one_padded(rim_rows, 1, img_local)
     image_sums = (
         contributions[:, img_local : 2 * img_local]
         + extended[:, :img_local]

time: 226 us -> 152 us (0.67)
  waiting for transfers between devices: 113 us -> 31.1 us
  starting transfers between devices: 23 us -> 42.1 us
  between operations: 13.7 us -> 0.32 us
    all_gather x1 -> x0, waiting for transfers between devices: 68.6 us -> none  [body(): full_embed = lax.all_gather(embed_weight, 'pair', axis=0, tiled=True)]
    ppermute x4 -> x5, waiting for transfers between devices: 43.6 us -> 17.8 us  [the longest x2 16 us: branch_one_padded(): before = lax.ppermute(last, ('branch', 'pair'), up)]
    all_to_all x0 -> x1, starting transfers between devices: none -> 16.8 us  [gathered_weight(): got = lax.all_to_all(spread, 'pair', 0, 0, tiled=True).reshape(-1, half)]
    all_to_all x0 -> x1, waiting for transfers between devices: none -> 13.4 us  [gathered_weight(): got = lax.all_to_all(spread, 'pair', 0, 0, tiled=True).reshape(-1, half)]
    ppermute x4 -> x5, starting transfers between devices: 18.2 us -> 25.3 us  [the longest x2 17.4 us: branch_one_padded(): after = lax.ppermute(initial, ('branch', 'pair'), down)]
    ppermute x1, starting transfers between devices: 4.77 us -> 0.01 us  [swapped(): return lax.ppermute(value, axis, pairs)]
  transfers between devices with their start and end apart: 6 -> 7, of which waited for: 3 -> 4; matrix products, arithmetic and copies ran while one was open for 9% -> 13% of each run, Pallas kernels for 0% -> 0%
where the time goes in v1:
time: 152 us; the launch traced here: 151 us
  starting transfers between devices  42.1 us (28%)
  matrix products  35.1 us (23%)
  local copies, waits for them, and re-layouts  33.3 us (22%)
  waiting for transfers between devices  31.1 us (20%)
  other arithmetic  9.56 us (6%)
    ppermute x2, starting transfers between devices, branch_one_padded(): after = lax.ppermute(initial, ('branch', 'pair'), down)  17.4 us
    all_to_all x1, starting transfers between devices, gathered_weight(): got = lax.all_to_all(spread, 'pair', 0, 0, tiled=True).reshape(-1, half)  16.8 us
    ppermute x2, waiting for transfers between devices, branch_one_padded(): before = lax.ppermute(last, ('branch', 'pair'), up)  16 us
    all_to_all x1, waiting for transfers between devices, gathered_weight(): got = lax.all_to_all(spread, 'pair', 0, 0, tiled=True).reshape(-1, half)  13.4 us
    dot_general x5, matrix products, project(): result = jnp.dot(flattened, matrix, preferred_element_type=jnp.float32)  11.8 us
    dot_general x2, matrix products, attend(): jnp.einsum('bqhd,bkhd->bhqk', query_heads, key_heads, preferred_element_t...  5.75 us
    dot_general x1, matrix products, select_rows(): jnp.dot(onehot.astype(jnp.bfloat16), window, preferred_element_type=jnp.f...  5.58 us
    reshape x2, local copies, waits for them, and re-layouts, embed_picked(): return embedded_rows.reshape(pair_count, tokens_per, model_width)  5.15 us
  transfers between devices with their start and end apart: 7, of which 4 were waited for; matrix products, arithmetic and copies ran while one was open for 13% of the time, Pallas kernels for 0%

profile of v1, /device:TPU:1, one launch (start us, length us, event | category | flops | bytes accessed | tf_op | source)
XLA Modules:
  0.0 151.5 jit_solution(1716414209279159801)
XLA Ops:
  0.0 0.0 copy-start
  0.0 0.9 constant_dynamic-slice_fusion
  0.9 0.9 broadcast_in_dim.2
  1.8 16.8 %all-to-all-start = ((bf16[128,8,384]{2,1,0:T(8,128)(2,1)}), bf16[128,8,384]{2,1,0:T(8,128)(2,1)}, u32[]{:S(2)}, u32[]{:S(2)}) async-start(bf16[128,8,384]{2,1,0:T(8,128)(2,1)} %broadcast_in_dim.2), calls=%async_computation | async-start | bytes 1572864 | tf_op jit(solution)/shard_map/all_to_all | solution.py:40
  18.6 2.4 %collective-permute-start = (bf16[2,200704]{1,0:T(2,128)(2,1)}, bf16[2,200704]{1,0:T(2,128)(2,1)}, u32[]{:S(2)}, u32[]{:S(2)}) collective-permute-start(bf16[2,200704]{1,0:T(2,128)(2,1)} %bitcast.65), channel_id=1, source_target_pairs={{128,129},{129,130},{130,131},{131,132},{132,133},{133,134},{134,1... | collective-permute-start | bytes 2408456 | tf_op jit(solution)/shard_map/ppermute | solution.py:31
  21.0 8.3 %collective-permute-start.1 = (bf16[2,200704]{1,0:T(2,128)(2,1)}, bf16[2,200704]{1,0:T(2,128)(2,1)}, u32[]{:S(2)}, u32[]{:S(2)}) collective-permute-start(bf16[2,200704]{1,0:T(2,128)(2,1)} %bitcast.66), channel_id=1, source_target_pairs={{129,128},{130,129},{131,130},{132,131},{133,132},{134,133},{135,1... | collective-permute-start | bytes 2408456 | tf_op jit(solution)/shard_map/ppermute | solution.py:32
  29.3 13.4 %all-to-all-done = bf16[128,8,384]{2,1,0:T(8,128)(2,1)} async-done(((bf16[128,8,384]{2,1,0:T(8,128)(2,1)}), bf16[128,8,384]{2,1,0:T(8,128)(2,1)}, u32[]{:S(2)}, u32[]{:S(2)}) %all-to-all-start) | async-done | bytes 786464 | tf_op jit(solution)/shard_map/all_to_all | solution.py:40
  42.7 3.6 %collective-permute-start.2 = (bf16[1024,384]{1,0:T(8,128)(2,1)}, bf16[1024,384]{1,0:T(8,128)(2,1)}, u32[]{:S(2)}, u32[]{:S(2)}) collective-permute-start(bf16[1024,384]{1,0:T(8,128)(2,1)} %bitcast.3), channel_id=1, source_target_pairs={{0,128},{128,0},{1,129},{129,1},{2,130},{130,2},{3,131},{131,3},{4... | collective-permute-start | bytes 2359304 | tf_op jit(solution)/shard_map/ppermute | solution.py:41
  46.3 0.0 copy-done.9
  46.4 4.4 %collective-permute-done = bf16[2,200704]{1,0:T(2,128)(2,1)} collective-permute-done((bf16[2,200704]{1,0:T(2,128)(2,1)}, bf16[2,200704]{1,0:T(2,128)(2,1)}, u32[]{:S(2)}, u32[]{:S(2)}) %collective-permute-start) | collective-permute-done | bytes 802848 | tf_op jit(solution)/shard_map/ppermute | solution.py:31
  50.7 0.0 collective-permute-done.1
  50.7 5.6 %convolution_convert_fusion = bf16[4,200704]{1,0:T(4,128)(2,1)} fusion(bf16[2,200704]{1,0:T(2,128)(2,1)} %collective-permute-done.1, bf16[2,200704]{1,0:T(2,128)(2,1)} %bitcast.67, bf16[2,200704]{1,0:T(2,128)(2,1)} %collective-permute-done, s32[4]{0:T(128)S(1)} %fusion.39), kind=kOutput, calls=%fused_computation | convolution fusion | flops 17661976 | bytes 4014096 | tf_op jit(solution)/shard_map/dot_general | solution.py:101
  56.3 3.6 %reshape.138 = bf16[784,1024]{1,0:T(8,128)(2,1)} reshape(bf16[4,200704]{1,0:T(4,128)(2,1)} %convolution_convert_fusion) | data formatting | bytes 3211264 | tf_op jit(solution)/shard_map/reshape | solution.py:107
  59.9 0.0 collective-permute-done.2
  59.9 4.8 %convert_reduce_fusion.1 = (f32[784]{0:T(1024)S(1)}, bf16[784,768]{1,0:T(8,128)(2,1)}) fusion(bf16[784,1024]{1,0:T(8,128)(2,1)} %reshape.138, bf16[1024,384]{1,0:T(8,128)(2,1)} %collective-permute-done.2, bf16[1024,384]{1,0:T(8,128)(2,1)} %bitcast.3, pred[]{:T(512)S(6)} %eq.35), kind=kOutput, calls=%fused_computation.21 | convolution fusion | flops 1242008832 | bytes 4385857 | tf_op jit(solution)/shard_map/dot_general | solution.py:108
  64.7 2.3 %reshape.140 = bf16[4,196,768]{2,1,0:T(8,128)(2,1)} reshape(bf16[784,768]{1,0:T(8,128)(2,1)} %get-tuple-element.15) | data formatting | bytes 2408448 | tf_op jit(solution)/shard_map/reshape | solution.py:111
  67.0 1.8 %fusion.16 = f32[784]{0:T(1024)S(1)} fusion(bf16[784,768]{1,0:T(8,128)(2,1)} %get-tuple-element.15, f32[784]{0:T(1024)S(1)} %broadcast_multiply_fusion.2), kind=kLoop, calls=%fused_computation.32 | loop fusion | flops 2407664 | bytes 1210496 | tf_op jit(solution)/shard_map/reduce_sum | solution.py:57
  68.8 2.7 %fusion.17 = bf16[784,768]{1,0:T(8,128)(2,1)} fusion(bf16[784,768]{1,0:T(8,128)(2,1)} %get-tuple-element.15, f32[784]{0:T(1024)S(1)} %add_rsqrt_fusion.2, f32[784]{0:T(1024)S(1)} %broadcast_multiply_fusion.2), kind=kLoop, calls=%fused_computation.33 | loop fusion | flops 2408448 | bytes 2414720 | tf_op jit(solution)/shard_map/convert_element_type | solution.py:58
  71.4 2.2 %dot_general.40 = bf16[4,196,768]{2,1,0:T(8,128)(2,1)} reshape(bf16[784,768]{1,0:T(8,128)(2,1)} %fusion.17) | data formatting | bytes 2408448 | tf_op jit(solution)/shard_map/dot_general | solution.py:64
  73.7 0.0 copy-done
  73.7 4.8 %convolution_convert_fusion.1 = bf16[4,196,2304]{2,1,0:T(8,128)(2,1)S(1)} fusion(bf16[4,196,768]{2,1,0:T(8,128)(2,1)} %dot_general.40, bf16[1,768,2304]{2,1,0:T(8,128)(2,1)S(1)} %copy-done), kind=kOutput, calls=%fused_computation.8 | convolution fusion | flops 2776338432 | bytes 8355840 | tf_op jit(solution)/shard_map/dot_general | solution.py:64
  78.5 1.9 %fusion.48 = (bf16[4,196,768]{2,1,0:T(8,128)(2,1)}, bf16[4,196,768]{2,1,0:T(8,128)(2,1)}, bf16[4,196,768]{2,1,0:T(8,128)(2,1)}) fusion(bf16[4,196,2304]{2,1,0:T(8,128)(2,1)S(1)} %convolution_convert_fusion.1), kind=kLoop, calls=%fused_computation.82 | loop fusion | bytes 7225344 | tf_op jit(solution)/shard_map/slice | solution.py:90
  80.4 1.6 %copy.78 = bf16[4,196,768]{1,2,0:T(8,128)(2,1)S(1)} copy(bf16[4,196,768]{2,1,0:T(8,128)(2,1)} %get-tuple-element.10) | data formatting | bytes 2408448 | tf_op jit(solution)/shard_map/slice | solution.py:89
  82.0 2.5 %copy.79 = bf16[4,196,768]{1,2,0:T(8,128)(2,1)} copy(bf16[4,196,768]{2,1,0:T(8,128)(2,1)} %get-tuple-element.9) | data formatting | bytes 2408448 | tf_op jit(solution)/shard_map/slice | solution.py:90
  84.6 2.5 %copy.77 = bf16[4,196,768]{1,2,0:T(8,128)(2,1)} copy(bf16[4,196,768]{2,1,0:T(8,128)(2,1)} %get-tuple-element.11) | data formatting | bytes 2408448 | tf_op jit(solution)/shard_map/slice | solution.py:91
  87.1 2.9 %copy.82 = bf16[4,196,768]{2,0,1:T(4,128)(2,1)} copy(bf16[4,196,768]{2,1,0:T(8,128)(2,1)} %reshape.140) | data formatting | bytes 2408448 | tf_op jit(solution)/shard_map/reshape | solution.py:111
  90.0 0.0 collective-permute-start.3
  90.0 0.0 copy-done.4
  90.0 2.1 %fusion = (f32[4,12,196]{2,1,0:T(8,128)S(1)}, f32[4,12,196,196]{2,3,1,0:T(8,128)S(1)}) fusion(bf16[4,196,12,64]{1,3,2,0:T(8,128)(2,1)S(1)} %bitcast.59, bf16[4,196,12,64]{1,3,2,0:T(8,128)(2,1)S(1)} %bitcast.60), kind=kOutput, calls=%fused_computation.6 | convolution fusion | flops 239706432 | bytes 9821952 | tf_op jit(solution)/shard_map/bqhd,bkhd->bhqk/dot_general | solution.py:74
  92.1 0.0 copy-done.6
  92.1 0.0 copy-start.5
  92.1 0.0 copy-start.11
  92.1 2.4 %fusion.20 = bf16[4,12,64,196]{3,2,1,0:T(8,128)(2,1)S(1)} fusion(bf16[4,196,12,64]{1,3,2,0:T(8,128)(2,1)S(1)} %bitcast.62, f32[4,12,196,196]{2,3,1,0:T(8,128)S(1)} %get-tuple-element.17, f32[4,12,196]{2,1,0:T(8,128)S(1)} %get-tuple-element.16), kind=kOutput, calls=%fused_computation.36 | convolution fusion | flops 242161920 | bytes 9821952 | tf_op jit(solution)/shard_map/bhqk,bkhd->bqhd/dot_general | solution.py:79
  94.5 0.0 copy-done.5
  94.5 0.0 copy-done.11
  94.5 1.3 fusion.50
  95.9 0.0 copy-start.12
  95.9 0.4 multiply_reduce_fusion
  96.4 1.0 copy-done.2
  97.3 0.7 copy-done.12
  98.0 2.3 %convolution_convert_fusion.3 = bf16[4,196,768]{2,1,0:T(8,128)(2,1)} fusion(f32[4,196,768]{2,1,0:T(8,128)S(1)} %get-tuple-element.19, f32[4,196]{1,0:T(4,128)S(1)} %add_rsqrt_fusion.1, f32[4,196]{1,0:T(4,128)S(1)} %broadcast_multiply_fusion.1, bf16[1,768,768]{2,1,0:T(8,128)(2,1)S(1)} %copy-done.12), kind=kOutput, calls=%fused_computation.45 | convolution fusion | flops 927252480 | bytes 4798592 | tf_op jit(solution)/shard_map/dot_general | solution.py:64
  100.3 1.6 %copy.89 = bf16[4,196,768]{1,2,0:T(8,128)(2,1)S(1)} copy(bf16[4,196,768]{2,1,0:T(8,128)(2,1)} %convolution_convert_fusion.3) | data formatting | bytes 2408448 | tf_op jit(solution)/shard_map/convert_element_type | solution.py:94
  101.9 0.0 collective-permute-done.3
  101.9 0.5 convert_reduce_fusion
  102.5 1.2 fusion.14
  103.7 0.9 fusion.15
  104.6 0.0 copy-done.10
  104.6 2.1 %convolution_convert_fusion.2 = bf16[4,196,1536]{2,1,0:T(8,128)(2,1)S(1)} fusion(bf16[1,768,1536]{2,1,0:T(8,128)(2,1)S(1)} %copy-done.10, bf16[4,196,768]{2,0,1:T(4,128)(2,1)S(1)} %fusion.15), kind=kOutput, calls=%fused_computation.12 | convolution fusion | flops 1850892288 | bytes 5971968 | tf_op jit(solution)/shard_map/dot_general | solution.py:64
  106.7 1.6 %fusion.49 = (bf16[4,196,768]{2,1,0:T(8,128)(2,1)}, bf16[4,196,768]{2,1,0:T(8,128)(2,1)}) fusion(bf16[4,196,1536]{2,1,0:T(8,128)(2,1)S(1)} %convolution_convert_fusion.2), kind=kLoop, calls=%fused_computation.83 | loop fusion | bytes 4816896 | tf_op jit(solution)/shard_map/slice | solution.py:96
  108.3 2.5 %copy.90 = bf16[4,196,768]{1,2,0:T(8,128)(2,1)} copy(bf16[4,196,768]{2,1,0:T(8,128)(2,1)} %get-tuple-element.12) | data formatting | bytes 2408448 | tf_op jit(solution)/shard_map/slice | solution.py:96
  110.8 2.5 %copy.88 = bf16[4,196,768]{1,2,0:T(8,128)(2,1)} copy(bf16[4,196,768]{2,1,0:T(8,128)(2,1)} %get-tuple-element.13) | data formatting | bytes 2408448 | tf_op jit(solution)/shard_map/slice | solution.py:96
  113.4 3.6 %fusion.1 = (f32[4,12,196]{2,1,0:T(8,128)S(1)}, f32[4,12,196,196]{2,3,1,0:T(8,128)S(1)}) fusion(bf16[4,196,12,64]{1,3,2,0:T(8,128)(2,1)S(1)} %bitcast.58, bf16[4,196,12,64]{1,3,2,0:T(8,128)(2,1)} %bitcast.61), kind=kOutput, calls=%fused_computation.7 | convolution fusion | flops 239706432 | bytes 9821952 | tf_op jit(solution)/shard_map/bqhd,bkhd->bhqk/dot_general | solution.py:74
  117.1 0.0 copy-start.8
  117.1 2.4 %fusion.19 = bf16[4,12,64,196]{3,2,1,0:T(8,128)(2,1)S(1)} fusion(bf16[4,196,12,64]{1,3,2,0:T(8,128)(2,1)S(1)} %bitcast.63, f32[4,12,196,196]{2,3,1,0:T(8,128)S(1)} %get-tuple-element.21, f32[4,12,196]{2,1,0:T(8,128)S(1)} %get-tuple-element.20), kind=kOutput, calls=%fused_computation.35 | convolution fusion | flops 242161920 | bytes 9821952 | tf_op jit(solution)/shard_map/bhqk,bkhd->bqhd/dot_general | solution.py:79
  119.5 1.2 add_bitcast_fusion
  120.7 0.9 copy.98
  121.7 2.4 %convolution_bitcast_fusion = f32[1,6,150528]{2,1,0:T(8,128)S(1)} fusion(f32[4,150528]{1,0:T(4,128)S(1)} %bitcast.57, s32[4]{0:T(128)S(1)} %get-tuple-element.5), kind=kOutput, calls=%fused_computation.1 | convolution fusion | flops 43352088 | bytes 6021136 | tf_op jit(solution)/shard_map/dot_general | solution.py:158
  124.1 1.0 fusion.47
  125.1 1.9 %collective-permute-start.4 = (f32[1,2,150528]{2,1,0:T(2,128)S(1)}, f32[1,2,150528]{2,1,0:T(2,128)S(1)}, u32[]{:S(2)}, u32[]{:S(2)}) collective-permute-start(f32[1,2,150528]{2,1,0:T(2,128)S(1)} %get-tuple-element.7), channel_id=1, source_target_pairs={{128,129},{129,130},{130,131},{131,132},{132,133},{133,134},{134,1... | collective-permute-start | bytes 3612680 | tf_op jit(solution)/shard_map/ppermute | solution.py:31
  127.0 0.0 copy-start.1
  127.0 9.1 %collective-permute-start.5 = (f32[1,2,150528]{2,1,0:T(2,128)S(1)}, f32[1,2,150528]{2,1,0:T(2,128)S(1)}, u32[]{:S(2)}, u32[]{:S(2)}) collective-permute-start(f32[1,2,150528]{2,1,0:T(2,128)S(1)} %get-tuple-element.8), channel_id=1, source_target_pairs={{129,128},{130,129},{131,130},{132,131},{133,132},{134,133},{135,1... | collective-permute-start | bytes 3612680 | tf_op jit(solution)/shard_map/ppermute | solution.py:32
  136.1 11.6 %collective-permute-done.4 = f32[1,2,150528]{2,1,0:T(2,128)S(1)} collective-permute-done((f32[1,2,150528]{2,1,0:T(2,128)S(1)}, f32[1,2,150528]{2,1,0:T(2,128)S(1)}, u32[]{:S(2)}, u32[]{:S(2)}) %collective-permute-start.4) | collective-permute-done | bytes 1204256 | tf_op jit(solution)/shard_map/ppermute | solution.py:31
  147.7 1.8 %collective-permute-done.5 = f32[1,2,150528]{2,1,0:T(2,128)S(1)} collective-permute-done((f32[1,2,150528]{2,1,0:T(2,128)S(1)}, f32[1,2,150528]{2,1,0:T(2,128)S(1)}, u32[]{:S(2)}, u32[]{:S(2)}) %collective-permute-start.5) | collective-permute-done | bytes 1204256 | tf_op jit(solution)/shard_map/ppermute | solution.py:32
  149.5 2.0 %fusion.32 = f32[1,2,150528]{2,1,0:T(2,128)} fusion(f32[1,2,150528]{2,1,0:T(2,128)S(1)} %collective-permute-done.5, f32[1,2,150528]{2,1,0:T(2,128)S(1)} %collective-permute-done.4, f32[1,6,150528]{2,1,0:T(8,128)S(1)} %convolution_bitcast_fusion), kind=kLoop, calls=%fused_computation.51 | loop fusion | flops 602112 | bytes 4816896 | tf_op jit(solution)/shard_map/add | solution.py:170
  (19 shorter events, 0.1 us)
Async XLA Ops:
  0.0 73.7 %copy-start = (bf16[1,768,2304]{2,1,0:T(8,128)(2,1)S(1)}, bf16[1,768,2304]{2,1,0:T(8,128)(2,1)}, u32[]{:S(2)}) copy-start(bf16[1,768,2304]{2,1,0:T(8,128)(2,1)} %param.11) | copy-start | bytes 10616836
  0.0 46.3 %copy-start.9 = (s32[4,2]{0,1:T(2,128)S(1)}, s32[4,2]{0,1:T(2,128)}, u32[]{:S(2)}) copy-start(s32[4,2]{0,1:T(2,128)} %param.9) | copy-start | bytes 100
  1.8 40.9 %all-to-all-start = ((bf16[128,8,384]{2,1,0:T(8,128)(2,1)}), bf16[128,8,384]{2,1,0:T(8,128)(2,1)}, u32[]{:S(2)}, u32[]{:S(2)}) async-start(bf16[128,8,384]{2,1,0:T(8,128)(2,1)} %broadcast_in_dim.2), calls=%async_computation | async-start | bytes 1572864 | tf_op jit(solution)/shard_map/all_to_all | solution.py:40
  18.6 32.1 %collective-permute-start = (bf16[2,200704]{1,0:T(2,128)(2,1)}, bf16[2,200704]{1,0:T(2,128)(2,1)}, u32[]{:S(2)}, u32[]{:S(2)}) collective-permute-start(bf16[2,200704]{1,0:T(2,128)(2,1)} %bitcast.65), channel_id=1, source_target_pairs={{128,129},{129,130},{130,131},{131,132},{132,133},{133,134},{134,1... | collective-permute-start | bytes 2408456 | tf_op jit(solution)/shard_map/ppermute | solution.py:31
  21.0 29.7 %collective-permute-start.1 = (bf16[2,200704]{1,0:T(2,128)(2,1)}, bf16[2,200704]{1,0:T(2,128)(2,1)}, u32[]{:S(2)}, u32[]{:S(2)}) collective-permute-start(bf16[2,200704]{1,0:T(2,128)(2,1)} %bitcast.66), channel_id=1, source_target_pairs={{129,128},{130,129},{131,130},{132,131},{133,132},{134,133},{135,1... | collective-permute-start | bytes 2408456 | tf_op jit(solution)/shard_map/ppermute | solution.py:32
  42.7 17.2 %collective-permute-start.2 = (bf16[1024,384]{1,0:T(8,128)(2,1)}, bf16[1024,384]{1,0:T(8,128)(2,1)}, u32[]{:S(2)}, u32[]{:S(2)}) collective-permute-start(bf16[1024,384]{1,0:T(8,128)(2,1)} %bitcast.3), channel_id=1, source_target_pairs={{0,128},{128,0},{1,129},{129,1},{2,130},{130,2},{3,131},{131,3},{4... | collective-permute-start | bytes 2359304 | tf_op jit(solution)/shard_map/ppermute | solution.py:41
  87.1 2.9 %copy-start.4 = (bf16[4,196,768]{1,2,0:T(8,128)(2,1)S(1)}, bf16[4,196,768]{1,2,0:T(8,128)(2,1)}, u32[]{:S(2)}) copy-start(bf16[4,196,768]{1,2,0:T(8,128)(2,1)} %copy.79) | copy-start | bytes 3612676
  90.0 12.0 %collective-permute-start.3 = (bf16[4,196,768]{2,0,1:T(4,128)(2,1)}, bf16[4,196,768]{2,0,1:T(4,128)(2,1)S(1)}, u32[]{:S(2)}, u32[]{:S(2)}) collective-permute-start(bf16[4,196,768]{2,0,1:T(4,128)(2,1)} %copy.82), channel_id=1, source_target_pairs={{0,128},{128,0},{1,129},{129,1},{2,130},{130,2},{3,131},{131,3},{4... | collective-permute-start | bytes 3612680 | tf_op jit(solution)/shard_map/ppermute | solution.py:50
  90.0 2.1 %copy-start.6 = (bf16[4,196,768]{1,2,0:T(8,128)(2,1)S(1)}, bf16[4,196,768]{1,2,0:T(8,128)(2,1)}, u32[]{:S(2)}) copy-start(bf16[4,196,768]{1,2,0:T(8,128)(2,1)} %copy.77) | copy-start | bytes 3612676
  92.1 2.4 %copy-start.5 = (bf16[4,196,768]{2,1,0:T(8,128)(2,1)S(1)}, bf16[4,196,768]{2,1,0:T(8,128)(2,1)}, u32[]{:S(2)}) copy-start(bf16[4,196,768]{2,1,0:T(8,128)(2,1)} %reshape.140) | copy-start | bytes 3612676
  92.1 2.4 %copy-start.11 = (bf16[1,768,768]{2,1,0:T(8,128)(2,1)S(1)}, bf16[1,768,768]{2,1,0:T(8,128)(2,1)}, u32[]{:S(2)}) copy-start(bf16[1,768,768]{2,1,0:T(8,128)(2,1)} %param.12) | copy-start | bytes 3538948
  95.9 1.4 copy-start.2
  95.9 2.1 %copy-start.12 = (bf16[1,768,768]{2,1,0:T(8,128)(2,1)S(1)}, bf16[1,768,768]{2,1,0:T(8,128)(2,1)}, u32[]{:S(2)}) copy-start(bf16[1,768,768]{2,1,0:T(8,128)(2,1)} %param.13) | copy-start | bytes 3538948
  102.5 2.1 %copy-start.10 = (bf16[1,768,1536]{2,1,0:T(8,128)(2,1)S(1)}, bf16[1,768,1536]{2,1,0:T(8,128)(2,1)}, u32[]{:S(2)}) copy-start(bf16[1,768,1536]{2,1,0:T(8,128)(2,1)} %param.14) | copy-start | bytes 7077892
  113.4 3.7 %copy-start.7 = (bf16[4,196,768]{1,2,0:T(8,128)(2,1)S(1)}, bf16[4,196,768]{1,2,0:T(8,128)(2,1)}, u32[]{:S(2)}) copy-start(bf16[4,196,768]{1,2,0:T(8,128)(2,1)} %copy.88) | copy-start | bytes 3612676
  117.0 2.4 %copy-start.3 = (f32[4,196,768]{2,1,0:T(8,128)S(1)}, f32[4,196,768]{2,1,0:T(8,128)}, u32[]{:S(2)}) copy-start(f32[4,196,768]{2,1,0:T(8,128)} %copy-done.2) | copy-start | bytes 7225348
  117.1 2.4 %copy-start.8 = (bf16[1,768,768]{2,1,0:T(8,128)(2,1)S(1)}, bf16[1,768,768]{2,1,0:T(8,128)(2,1)}, u32[]{:S(2)}) copy-start(bf16[1,768,768]{2,1,0:T(8,128)(2,1)} %param.15) | copy-start | bytes 3538948
  125.1 22.6 %collective-permute-start.4 = (f32[1,2,150528]{2,1,0:T(2,128)S(1)}, f32[1,2,150528]{2,1,0:T(2,128)S(1)}, u32[]{:S(2)}, u32[]{:S(2)}) collective-permute-start(f32[1,2,150528]{2,1,0:T(2,128)S(1)} %get-tuple-element.7), channel_id=1, source_target_pairs={{128,129},{129,130},{130,131},{131,132},{132,133},{133,134},{134,1... | collective-permute-start | bytes 3612680 | tf_op jit(solution)/shard_map/ppermute | solution.py:31
  127.0 24.5 %copy-start.1 = (bf16[1,768,2304]{2,1,0:T(8,128)(2,1)S(1)}, bf16[1,768,2304]{2,1,0:T(8,128)(2,1)}, u32[]{:S(2)}) copy-start(bf16[1,768,2304]{2,1,0:T(8,128)(2,1)} %param.11) | copy-start | bytes 10616836
  127.0 22.5 %collective-permute-start.5 = (f32[1,2,150528]{2,1,0:T(2,128)S(1)}, f32[1,2,150528]{2,1,0:T(2,128)S(1)}, u32[]{:S(2)}, u32[]{:S(2)}) collective-permute-start(f32[1,2,150528]{2,1,0:T(2,128)S(1)} %get-tuple-element.8), channel_id=1, source_target_pairs={{129,128},{130,129},{131,130},{132,131},{133,132},{134,133},{135,1... | collective-permute-start | bytes 3612680 | tf_op jit(solution)/shard_map/ppermute | solution.py:32

commit v2 on v1

--- a/solution.py
+++ b/solution.py
@@ -103,8 +103,9 @@
     )
 
 
-def embed_picked(onehot, window, full_embed, pair_count, tokens_per, enc_width, model_width):
-    picked = select_rows(onehot, window).reshape(pair_count * tokens_per, enc_width)
+def embed_picked(places, window, full_embed, pair_count, tokens_per, enc_width, model_width):
+    rows = window.reshape(window.shape[0], tokens_per, enc_width)
+    picked = jnp.take(rows, places, axis=0, mode="clip").reshape(pair_count * tokens_per, enc_width)
     embedded_rows = jnp.dot(picked, full_embed, preferred_element_type=jnp.float32).astype(
         jnp.bfloat16
     )
@@ -139,7 +140,7 @@
     window = branch_one_padded(raw_local, 0, img_local)
     own_list = [
         embed_picked(
-            own_onehots, window, full_embed, pair_count, tokens_per, enc_width, model_width
+            own_place, window, full_embed, pair_count, tokens_per, enc_width, model_width
         )
     ]
     partner_list = [swapped(own_list[0], "branch", 0)]
@@ -165,7 +166,7 @@
     rim_rows = jnp.concatenate(
         [contributions[:, :img_local], contributions[:, 2 * img_local :]], axis=1
     )
-    extended = branch_one_padded(rim_rows, 1, img_local)
+    extended = branch_one_padded(rim_rows.astype(jnp.bfloat16), 1, img_local).astype(jnp.float32)
     image_sums = (
         contributions[:, img_local : 2 * img_local]
         + extended[:, :img_local]

time: 152 us -> 153 us (level)
  local copies, waits for them, and re-layouts: 33.3 us -> 43.6 us
  waiting for transfers between devices: 31.1 us -> 21.1 us
  other arithmetic: 9.56 us -> 15.6 us
  matrix products: 35.1 us -> 29.4 us
    ppermute x2, waiting for transfers between devices: 16 us -> 6.26 us  [branch_one_padded(): before = lax.ppermute(last, ('branch', 'pair'), up)]
    dot_general x1 -> x0, matrix products: 5.58 us -> none  [select_rows(): jnp.dot(onehot.astype(jnp.bfloat16), window, preferred_element_type=jnp.f...]
    concatenate x0 -> x2, local copies, waits for them, and re-layouts: none -> 5.05 us  [branch_one_padded(): return jnp.concatenate([before, x, after], axis=dim)]
    concatenate x0 -> x2, other arithmetic: none -> 4.66 us  [branch_one_padded(): return jnp.concatenate([before, x, after], axis=dim)]
    gather x0 -> x1, local copies, waits for them, and re-layouts: none -> 3.5 us  [embed_picked(): jnp.take(rows, places, axis=0, mode='clip')]
    unnamed x27 -> x30, local copies, waits for them, and re-layouts: 2.64 us -> 5.6 us
    add x1, other arithmetic: 2.01 us -> 4.61 us  [body(): contributions[:, img_local:2 * img_local] + extended[:, :img_local]]
  transfers between devices with their start and end apart: 7 -> 7, of which waited for: 4 -> 4; matrix products, arithmetic and copies ran while one was open for 13% -> 18% of each run, Pallas kernels for 0% -> 0%
where the time goes in v2:
time: 153 us; the launch traced here: 152 us
  local copies, waits for them, and re-layouts  43.6 us (28%)
  starting transfers between devices  42 us (27%)
  matrix products  29.4 us (19%)
  waiting for transfers between devices  21.1 us (14%)
  other arithmetic  15.6 us (10%)
    ppermute x2, starting transfers between devices, branch_one_padded(): after = lax.ppermute(initial, ('branch', 'pair'), down)  17.1 us
    all_to_all x1, starting transfers between devices, gathered_weight(): got = lax.all_to_all(spread, 'pair', 0, 0, tiled=True).reshape(-1, half)  16.9 us
    all_to_all x1, waiting for transfers between devices, gathered_weight(): got = lax.all_to_all(spread, 'pair', 0, 0, tiled=True).reshape(-1, half)  13.4 us
    dot_general x5, matrix products, project(): result = jnp.dot(flattened, matrix, preferred_element_type=jnp.float32)  11.8 us
    ppermute x2, waiting for transfers between devices, branch_one_padded(): before = lax.ppermute(last, ('branch', 'pair'), up)  6.26 us
    dot_general x2, matrix products, attend(): jnp.einsum('bqhd,bkhd->bhqk', query_heads, key_heads, preferred_element_t...  5.74 us
    unnamed x30, local copies, waits for them, and re-layouts  5.6 us
    reshape x2, local copies, waits for them, and re-layouts, embed_picked(): return embedded_rows.reshape(pair_count, tokens_per, model_width)  5.14 us
  transfers between devices with their start and end apart: 7, of which 4 were waited for; matrix products, arithmetic and copies ran while one was open for 18% of the time, Pallas kernels for 0%

profile of v2, /device:TPU:1, one launch (start us, length us, event | category | flops | bytes accessed | tf_op | source)
XLA Modules:
  0.0 152.1 jit_solution(1704021512454261113)
XLA Ops:
  0.0 0.0 copy-start
  0.0 0.8 constant_dynamic-slice_fusion
  0.8 0.9 broadcast_in_dim.3
  1.8 16.9 %all-to-all-start = ((bf16[128,8,384]{2,1,0:T(8,128)(2,1)}), bf16[128,8,384]{2,1,0:T(8,128)(2,1)}, u32[]{:S(2)}, u32[]{:S(2)}) async-start(bf16[128,8,384]{2,1,0:T(8,128)(2,1)} %broadcast_in_dim.3), calls=%async_computation | async-start | bytes 1572864 | tf_op jit(solution)/shard_map/all_to_all | solution.py:40
  18.7 2.4 %collective-permute-start = (bf16[2,200704]{1,0:T(2,128)(2,1)}, bf16[2,200704]{1,0:T(2,128)(2,1)}, u32[]{:S(2)}, u32[]{:S(2)}) collective-permute-start(bf16[2,200704]{1,0:T(2,128)(2,1)} %bitcast.71), channel_id=1, source_target_pairs={{128,129},{129,130},{130,131},{131,132},{132,133},{133,134},{134,1... | collective-permute-start | bytes 2408456 | tf_op jit(solution)/shard_map/ppermute | solution.py:31
  21.2 8.3 %collective-permute-start.1 = (bf16[2,200704]{1,0:T(2,128)(2,1)}, bf16[2,200704]{1,0:T(2,128)(2,1)}, u32[]{:S(2)}, u32[]{:S(2)}) collective-permute-start(bf16[2,200704]{1,0:T(2,128)(2,1)} %bitcast.72), channel_id=1, source_target_pairs={{129,128},{130,129},{131,130},{132,131},{133,132},{134,133},{135,1... | collective-permute-start | bytes 2408456 | tf_op jit(solution)/shard_map/ppermute | solution.py:32
  29.5 13.4 %all-to-all-done = bf16[128,8,384]{2,1,0:T(8,128)(2,1)} async-done(((bf16[128,8,384]{2,1,0:T(8,128)(2,1)}), bf16[128,8,384]{2,1,0:T(8,128)(2,1)}, u32[]{:S(2)}, u32[]{:S(2)}) %all-to-all-start) | async-done | bytes 786464 | tf_op jit(solution)/shard_map/all_to_all | solution.py:40
  42.8 3.6 %collective-permute-start.2 = (bf16[1024,384]{1,0:T(8,128)(2,1)}, bf16[1024,384]{1,0:T(8,128)(2,1)}, u32[]{:S(2)}, u32[]{:S(2)}) collective-permute-start(bf16[1024,384]{1,0:T(8,128)(2,1)} %bitcast.3), channel_id=1, source_target_pairs={{0,128},{128,0},{1,129},{129,1},{2,130},{130,2},{3,131},{131,3},{4... | collective-permute-start | bytes 2359304 | tf_op jit(solution)/shard_map/ppermute | solution.py:41
  46.5 2.2 %copy.93 = bf16[2,196,1024]{2,1,0:T(8,128)(2,1)} copy(bf16[2,196,1024]{2,0,1:T(2,128)(2,1)} %param.8) | data formatting | bytes 1605632 | tf_op args[0]
  48.7 2.1 %collective-permute-done = bf16[2,200704]{1,0:T(2,128)(2,1)} collective-permute-done((bf16[2,200704]{1,0:T(2,128)(2,1)}, bf16[2,200704]{1,0:T(2,128)(2,1)}, u32[]{:S(2)}, u32[]{:S(2)}) %collective-permute-start) | collective-permute-done | bytes 802848 | tf_op jit(solution)/shard_map/ppermute | solution.py:31
  50.9 2.5 %concatenate.51 = bf16[2,196,1024]{2,1,0:T(8,128)(2,1)} reshape(bf16[2,200704]{1,0:T(2,128)(2,1)} %collective-permute-done) | data formatting | bytes 1605632 | tf_op jit(solution)/shard_map/concatenate | solution.py:33
  53.4 0.0 collective-permute-done.1
  53.4 2.5 %concatenate.52 = bf16[2,196,1024]{2,1,0:T(8,128)(2,1)} reshape(bf16[2,200704]{1,0:T(2,128)(2,1)} %collective-permute-done.1) | data formatting | bytes 1605632 | tf_op jit(solution)/shard_map/concatenate | solution.py:33
  55.9 3.4 %pad_maximum_fusion = bf16[6,196,1024]{2,1,0:T(8,128)(2,1)} fusion(bf16[2,196,1024]{2,1,0:T(8,128)(2,1)} %concatenate.52, bf16[2,196,1024]{2,1,0:T(8,128)(2,1)} %copy.93, bf16[2,196,1024]{2,1,0:T(8,128)(2,1)} %concatenate.51), kind=kLoop, calls=%fused_computation.21 | loop fusion | flops 2408448 | bytes 4816896 | tf_op jit(solution)/shard_map/concatenate | solution.py:33
  59.3 3.5 %gather_fusion = bf16[4,196,1024]{2,1,0:T(8,128)(2,1)} fusion(bf16[6,196,1024]{2,1,0:T(8,128)(2,1)} %pad_maximum_fusion, s32[1024]{0:T(1024)S(1)} %pad_clamp_fusion), kind=kCustom, calls=%fused_computation | custom fusion | bytes 3211280 | tf_op jit(solution)/shard_map/jit(_take)/gather | solution.py:108
  62.8 2.5 %reshape.235 = bf16[784,1024]{1,0:T(8,128)(2,1)} reshape(bf16[4,196,1024]{2,1,0:T(8,128)(2,1)} %gather_fusion) | data formatting | bytes 3211264 | tf_op jit(solution)/shard_map/reshape | solution.py:108
  65.2 0.0 collective-permute-done.2
  65.3 4.8 %convert_reduce_fusion.1 = (f32[784]{0:T(1024)S(1)}, bf16[784,768]{1,0:T(8,128)(2,1)}) fusion(bf16[784,1024]{1,0:T(8,128)(2,1)} %reshape.235, bf16[1024,384]{1,0:T(8,128)(2,1)} %collective-permute-done.2, bf16[1024,384]{1,0:T(8,128)(2,1)} %bitcast.3, pred[]{:T(512)S(6)} %eq.20), kind=kOutput, calls=%fused_computation.16 | convolution fusion | flops 1242008832 | bytes 4385857 | tf_op jit(solution)/shard_map/dot_general | solution.py:109
  70.1 2.3 %reshape.237 = bf16[4,196,768]{2,1,0:T(8,128)(2,1)} reshape(bf16[784,768]{1,0:T(8,128)(2,1)} %get-tuple-element.15) | data formatting | bytes 2408448 | tf_op jit(solution)/shard_map/reshape | solution.py:112
  72.3 1.9 %fusion.11 = f32[784]{0:T(1024)S(1)} fusion(bf16[784,768]{1,0:T(8,128)(2,1)} %get-tuple-element.15, f32[784]{0:T(1024)S(1)} %broadcast_multiply_fusion.2), kind=kLoop, calls=%fused_computation.28 | loop fusion | flops 2407664 | bytes 1210496 | tf_op jit(solution)/shard_map/reduce_sum | solution.py:57
  74.2 1.4 fusion.12
  75.6 2.2 %dot_general.36 = bf16[4,196,768]{2,1,0:T(8,128)(2,1)} reshape(bf16[784,768]{1,0:T(8,128)(2,1)} %fusion.12) | data formatting | bytes 2408448 | tf_op jit(solution)/shard_map/dot_general | solution.py:64
  77.8 4.8 %convolution_convert_fusion = bf16[4,196,2304]{2,1,0:T(8,128)(2,1)S(1)} fusion(bf16[4,196,768]{2,1,0:T(8,128)(2,1)} %dot_general.36, bf16[1,768,2304]{2,1,0:T(8,128)(2,1)S(1)} %copy-done), kind=kOutput, calls=%fused_computation.8 | convolution fusion | flops 2776338432 | bytes 8355840 | tf_op jit(solution)/shard_map/dot_general | solution.py:64
  82.7 1.9 %fusion.41 = (bf16[4,196,768]{2,1,0:T(8,128)(2,1)}, bf16[4,196,768]{2,1,0:T(8,128)(2,1)}, bf16[4,196,768]{2,1,0:T(8,128)(2,1)}) fusion(bf16[4,196,2304]{2,1,0:T(8,128)(2,1)S(1)} %convolution_convert_fusion), kind=kLoop, calls=%fused_computation.81 | loop fusion | bytes 7225344 | tf_op jit(solution)/shard_map/slice | solution.py:90
  84.6 1.6 %copy.95 = bf16[4,196,768]{1,2,0:T(8,128)(2,1)S(1)} copy(bf16[4,196,768]{2,1,0:T(8,128)(2,1)} %get-tuple-element.10) | data formatting | bytes 2408448 | tf_op jit(solution)/shard_map/slice | solution.py:89
  86.2 2.5 %copy.96 = bf16[4,196,768]{1,2,0:T(8,128)(2,1)} copy(bf16[4,196,768]{2,1,0:T(8,128)(2,1)} %get-tuple-element.9) | data formatting | bytes 2408448 | tf_op jit(solution)/shard_map/slice | solution.py:90
  88.7 2.5 %copy.94 = bf16[4,196,768]{1,2,0:T(8,128)(2,1)} copy(bf16[4,196,768]{2,1,0:T(8,128)(2,1)} %get-tuple-element.11) | data formatting | bytes 2408448 | tf_op jit(solution)/shard_map/slice | solution.py:91
  91.3 2.9 %copy.99 = bf16[4,196,768]{2,0,1:T(4,128)(2,1)} copy(bf16[4,196,768]{2,1,0:T(8,128)(2,1)} %reshape.237) | data formatting | bytes 2408448 | tf_op jit(solution)/shard_map/reshape | solution.py:112
  94.1 0.0 collective-permute-start.3
  94.2 2.1 %fusion = (f32[4,12,196]{2,1,0:T(8,128)S(1)}, f32[4,12,196,196]{2,3,1,0:T(8,128)S(1)}) fusion(bf16[4,196,12,64]{1,3,2,0:T(8,128)(2,1)S(1)} %bitcast.63, bf16[4,196,12,64]{1,3,2,0:T(8,128)(2,1)S(1)} %bitcast.64), kind=kOutput, calls=%fused_computation.6 | convolution fusion | flops 239706432 | bytes 9821952 | tf_op jit(solution)/shard_map/bqhd,bkhd->bhqk/dot_general | solution.py:74
  96.3 0.0 copy-done.7
  96.3 0.0 copy-start.6
  96.3 0.0 copy-start.12
  96.3 2.3 %fusion.15 = bf16[4,12,64,196]{3,2,1,0:T(8,128)(2,1)S(1)} fusion(bf16[4,196,12,64]{1,3,2,0:T(8,128)(2,1)S(1)} %bitcast.68, f32[4,12,196,196]{2,3,1,0:T(8,128)S(1)} %get-tuple-element.17, f32[4,12,196]{2,1,0:T(8,128)S(1)} %get-tuple-element.16), kind=kOutput, calls=%fused_computation.32 | convolution fusion | flops 242161920 | bytes 9821952 | tf_op jit(solution)/shard_map/bhqk,bkhd->bqhd/dot_general | solution.py:79
  98.7 1.3 fusion.43
  100.0 0.0 copy-start.13
  100.0 0.4 multiply_reduce_fusion
  100.5 1.0 copy-done.3
  101.5 0.7 copy-done.13
  102.1 2.3 %convolution_convert_fusion.2 = bf16[4,196,768]{2,1,0:T(8,128)(2,1)} fusion(f32[4,196,768]{2,1,0:T(8,128)S(1)} %get-tuple-element.19, f32[4,196]{1,0:T(4,128)S(1)} %add_rsqrt_fusion.1, f32[4,196]{1,0:T(4,128)S(1)} %broadcast_multiply_fusion.1, bf16[1,768,768]{2,1,0:T(8,128)(2,1)S(1)} %copy-done.13), kind=kOutput, calls=%fused_computation.41 | convolution fusion | flops 927252480 | bytes 4798592 | tf_op jit(solution)/shard_map/dot_general | solution.py:64
  104.4 1.6 %copy.106 = bf16[4,196,768]{1,2,0:T(8,128)(2,1)S(1)} copy(bf16[4,196,768]{2,1,0:T(8,128)(2,1)} %convolution_convert_fusion.2) | data formatting | bytes 2408448 | tf_op jit(solution)/shard_map/convert_element_type | solution.py:94
  106.0 0.0 collective-permute-done.3
  106.1 0.5 convert_reduce_fusion
  106.6 1.2 fusion.9
  107.8 0.9 fusion.10
  108.7 0.7 copy-done.11
  109.4 2.1 %convolution_convert_fusion.1 = bf16[4,196,1536]{2,1,0:T(8,128)(2,1)S(1)} fusion(bf16[1,768,1536]{2,1,0:T(8,128)(2,1)S(1)} %copy-done.11, bf16[4,196,768]{2,0,1:T(4,128)(2,1)S(1)} %fusion.10), kind=kOutput, calls=%fused_computation.12 | convolution fusion | flops 1850892288 | bytes 5971968 | tf_op jit(solution)/shard_map/dot_general | solution.py:64
  111.5 1.6 %fusion.42 = (bf16[4,196,768]{2,1,0:T(8,128)(2,1)}, bf16[4,196,768]{2,1,0:T(8,128)(2,1)}) fusion(bf16[4,196,1536]{2,1,0:T(8,128)(2,1)S(1)} %convolution_convert_fusion.1), kind=kLoop, calls=%fused_computation.82 | loop fusion | bytes 4816896 | tf_op jit(solution)/shard_map/slice | solution.py:96
  113.1 2.5 %copy.107 = bf16[4,196,768]{1,2,0:T(8,128)(2,1)} copy(bf16[4,196,768]{2,1,0:T(8,128)(2,1)} %get-tuple-element.12) | data formatting | bytes 2408448 | tf_op jit(solution)/shard_map/slice | solution.py:96
  115.7 2.6 %copy.105 = bf16[4,196,768]{1,2,0:T(8,128)(2,1)} copy(bf16[4,196,768]{2,1,0:T(8,128)(2,1)} %get-tuple-element.13) | data formatting | bytes 2408448 | tf_op jit(solution)/shard_map/slice | solution.py:96
  118.2 3.6 %fusion.1 = (f32[4,12,196]{2,1,0:T(8,128)S(1)}, f32[4,12,196,196]{2,3,1,0:T(8,128)S(1)}) fusion(bf16[4,196,12,64]{1,3,2,0:T(8,128)(2,1)S(1)} %bitcast.62, bf16[4,196,12,64]{1,3,2,0:T(8,128)(2,1)} %bitcast.65), kind=kOutput, calls=%fused_computation.7 | convolution fusion | flops 239706432 | bytes 9821952 | tf_op jit(solution)/shard_map/bqhd,bkhd->bhqk/dot_general | solution.py:74
  121.9 0.0 copy-start.9
  121.9 2.4 %fusion.14 = bf16[4,12,64,196]{3,2,1,0:T(8,128)(2,1)S(1)} fusion(bf16[4,196,12,64]{1,3,2,0:T(8,128)(2,1)S(1)} %bitcast.69, f32[4,12,196,196]{2,3,1,0:T(8,128)S(1)} %get-tuple-element.21, f32[4,12,196]{2,1,0:T(8,128)S(1)} %get-tuple-element.20), kind=kOutput, calls=%fused_computation.31 | convolution fusion | flops 242161920 | bytes 9821952 | tf_op jit(solution)/shard_map/bhqk,bkhd->bqhd/dot_general | solution.py:79
  124.3 1.2 add_bitcast_fusion
  125.5 0.9 copy.115
  126.5 2.4 %convolution_bitcast_fusion = f32[1,6,150528]{2,1,0:T(8,128)S(1)} fusion(f32[4,150528]{1,0:T(4,128)S(1)} %bitcast.61, s32[4]{0:T(128)S(1)} %get-tuple-element.5), kind=kOutput, calls=%fused_computation.1 | convolution fusion | flops 43352088 | bytes 6021136 | tf_op jit(solution)/shard_map/dot_general | solution.py:159
  128.9 0.9 fusion.40
  129.8 1.9 %collective-permute-start.4 = (bf16[1,2,150528]{2,1,0:T(2,128)(2,1)S(1)}, bf16[1,2,150528]{2,1,0:T(2,128)(2,1)S(1)}, u32[]{:S(2)}, u32[]{:S(2)}) collective-permute-start(bf16[1,2,150528]{2,1,0:T(2,128)(2,1)S(1)} %get-tuple-element.7), channel_id=1, source_target_pairs={{128,129},{129,130},{130,131},{131,132},{132,133},{133,134},{134,1... | collective-permute-start | bytes 1806344 | tf_op jit(solution)/shard_map/ppermute | solution.py:31
  131.7 8.8 %collective-permute-start.5 = (bf16[1,2,150528]{2,1,0:T(2,128)(2,1)S(1)}, bf16[1,2,150528]{2,1,0:T(2,128)(2,1)S(1)}, u32[]{:S(2)}, u32[]{:S(2)}) collective-permute-start(bf16[1,2,150528]{2,1,0:T(2,128)(2,1)S(1)} %get-tuple-element.8), channel_id=1, source_target_pairs={{129,128},{130,129},{131,130},{132,131},{133,132},{134,133},{135,1... | collective-permute-start | bytes 1806344 | tf_op jit(solution)/shard_map/ppermute | solution.py:32
  140.5 0.0 copy-start.1
  140.5 1.3 maximum_bitcast_fusion
  141.8 4.1 %collective-permute-done.4 = bf16[1,2,150528]{2,1,0:T(2,128)(2,1)S(1)} collective-permute-done((bf16[1,2,150528]{2,1,0:T(2,128)(2,1)S(1)}, bf16[1,2,150528]{2,1,0:T(2,128)(2,1)S(1)}, u32[]{:S(2)}, u32[]{:S(2)}) %collective-permute-start.4) | collective-permute-done | bytes 602144 | tf_op jit(solution)/shard_map/ppermute | solution.py:31
  146.0 1.5 collective-permute-done.5
  147.5 4.6 %fusion.27 = f32[1,2,150528]{2,1,0:T(2,128)} fusion(f32[1,6,150528]{2,1,0:T(8,128)S(1)} %convolution_bitcast_fusion, bf16[1,2,150528]{2,1,0:T(2,128)(2,1)S(1)} %collective-permute-done.5, bf16[1,4,150528]{2,1,0:T(4,128)(2,1)S(1)} %maximum_bitcast_fusion, bf16[1,2,150528]{2,1,0:T(2,128)(2,1)S(1)} %collective-permute-done.4), kind=kLoop, calls=%fused_computation.47 | loop fusion | flops 4214784 | bytes 4816896 | tf_op jit(solution)/shard_map/add | solution.py:171
  (27 shorter events, 0.1 us)
Async XLA Ops:
  0.0 77.8 %copy-start = (bf16[1,768,2304]{2,1,0:T(8,128)(2,1)S(1)}, bf16[1,768,2304]{2,1,0:T(8,128)(2,1)}, u32[]{:S(2)}) copy-start(bf16[1,768,2304]{2,1,0:T(8,128)(2,1)} %param.11) | copy-start | bytes 10616836
  1.8 46.9 %copy-start.10 = (s32[4,2]{0,1:T(2,128)S(1)}, s32[4,2]{0,1:T(2,128)}, u32[]{:S(2)}) copy-start(s32[4,2]{0,1:T(2,128)} %param.9) | copy-start | bytes 100
  1.8 41.0 %all-to-all-start = ((bf16[128,8,384]{2,1,0:T(8,128)(2,1)}), bf16[128,8,384]{2,1,0:T(8,128)(2,1)}, u32[]{:S(2)}, u32[]{:S(2)}) async-start(bf16[128,8,384]{2,1,0:T(8,128)(2,1)} %broadcast_in_dim.3), calls=%async_computation | async-start | bytes 1572864 | tf_op jit(solution)/shard_map/all_to_all | solution.py:40
  18.7 32.1 %collective-permute-start = (bf16[2,200704]{1,0:T(2,128)(2,1)}, bf16[2,200704]{1,0:T(2,128)(2,1)}, u32[]{:S(2)}, u32[]{:S(2)}) collective-permute-start(bf16[2,200704]{1,0:T(2,128)(2,1)} %bitcast.71), channel_id=1, source_target_pairs={{128,129},{129,130},{130,131},{131,132},{132,133},{133,134},{134,1... | collective-permute-start | bytes 2408456 | tf_op jit(solution)/shard_map/ppermute | solution.py:31
  21.2 32.2 %collective-permute-start.1 = (bf16[2,200704]{1,0:T(2,128)(2,1)}, bf16[2,200704]{1,0:T(2,128)(2,1)}, u32[]{:S(2)}, u32[]{:S(2)}) collective-permute-start(bf16[2,200704]{1,0:T(2,128)(2,1)} %bitcast.72), channel_id=1, source_target_pairs={{129,128},{130,129},{131,130},{132,131},{133,132},{134,133},{135,1... | collective-permute-start | bytes 2408456 | tf_op jit(solution)/shard_map/ppermute | solution.py:32
  42.8 22.4 %collective-permute-start.2 = (bf16[1024,384]{1,0:T(8,128)(2,1)}, bf16[1024,384]{1,0:T(8,128)(2,1)}, u32[]{:S(2)}, u32[]{:S(2)}) collective-permute-start(bf16[1024,384]{1,0:T(8,128)(2,1)} %bitcast.3), channel_id=1, source_target_pairs={{0,128},{128,0},{1,129},{129,1},{2,130},{130,2},{3,131},{131,3},{4... | collective-permute-start | bytes 2359304 | tf_op jit(solution)/shard_map/ppermute | solution.py:41
  72.3 1.9 %copy-start.2 = (bf16[784,768]{1,0:T(8,128)(2,1)S(1)}, bf16[784,768]{1,0:T(8,128)(2,1)}, u32[]{:S(2)}) copy-start(bf16[784,768]{1,0:T(8,128)(2,1)} %get-tuple-element.15) | copy-start | bytes 3612676
  91.3 2.9 %copy-start.5 = (bf16[4,196,768]{1,2,0:T(8,128)(2,1)S(1)}, bf16[4,196,768]{1,2,0:T(8,128)(2,1)}, u32[]{:S(2)}) copy-start(bf16[4,196,768]{1,2,0:T(8,128)(2,1)} %copy.96) | copy-start | bytes 3612676
  94.1 11.9 %collective-permute-start.3 = (bf16[4,196,768]{2,0,1:T(4,128)(2,1)}, bf16[4,196,768]{2,0,1:T(4,128)(2,1)S(1)}, u32[]{:S(2)}, u32[]{:S(2)}) collective-permute-start(bf16[4,196,768]{2,0,1:T(4,128)(2,1)} %copy.99), channel_id=1, source_target_pairs={{0,128},{128,0},{1,129},{129,1},{2,130},{130,2},{3,131},{131,3},{4... | collective-permute-start | bytes 3612680 | tf_op jit(solution)/shard_map/ppermute | solution.py:50
  94.2 2.1 %copy-start.7 = (bf16[4,196,768]{1,2,0:T(8,128)(2,1)S(1)}, bf16[4,196,768]{1,2,0:T(8,128)(2,1)}, u32[]{:S(2)}) copy-start(bf16[4,196,768]{1,2,0:T(8,128)(2,1)} %copy.94) | copy-start | bytes 3612676
  96.3 2.4 %copy-start.6 = (bf16[4,196,768]{2,1,0:T(8,128)(2,1)S(1)}, bf16[4,196,768]{2,1,0:T(8,128)(2,1)}, u32[]{:S(2)}) copy-start(bf16[4,196,768]{2,1,0:T(8,128)(2,1)} %reshape.237) | copy-start | bytes 3612676
  96.3 2.4 %copy-start.12 = (bf16[1,768,768]{2,1,0:T(8,128)(2,1)S(1)}, bf16[1,768,768]{2,1,0:T(8,128)(2,1)}, u32[]{:S(2)}) copy-start(bf16[1,768,768]{2,1,0:T(8,128)(2,1)} %param.12) | copy-start | bytes 3538948
  100.0 1.5 copy-start.3
  100.0 2.1 %copy-start.13 = (bf16[1,768,768]{2,1,0:T(8,128)(2,1)S(1)}, bf16[1,768,768]{2,1,0:T(8,128)(2,1)}, u32[]{:S(2)}) copy-start(bf16[1,768,768]{2,1,0:T(8,128)(2,1)} %param.13) | copy-start | bytes 3538948
  107.8 1.7 %copy-start.11 = (bf16[1,768,1536]{2,1,0:T(8,128)(2,1)S(1)}, bf16[1,768,1536]{2,1,0:T(8,128)(2,1)}, u32[]{:S(2)}) copy-start(bf16[1,768,1536]{2,1,0:T(8,128)(2,1)} %param.14) | copy-start | bytes 7077892
  118.2 3.7 %copy-start.8 = (bf16[4,196,768]{1,2,0:T(8,128)(2,1)S(1)}, bf16[4,196,768]{1,2,0:T(8,128)(2,1)}, u32[]{:S(2)}) copy-start(bf16[4,196,768]{1,2,0:T(8,128)(2,1)} %copy.105) | copy-start | bytes 3612676
  121.9 2.4 %copy-start.4 = (f32[4,196,768]{2,1,0:T(8,128)S(1)}, f32[4,196,768]{2,1,0:T(8,128)}, u32[]{:S(2)}) copy-start(f32[4,196,768]{2,1,0:T(8,128)} %copy-done.3) | copy-start | bytes 7225348
  121.9 2.4 %copy-start.9 = (bf16[1,768,768]{2,1,0:T(8,128)(2,1)S(1)}, bf16[1,768,768]{2,1,0:T(8,128)(2,1)}, u32[]{:S(2)}) copy-start(bf16[1,768,768]{2,1,0:T(8,128)(2,1)} %param.15) | copy-start | bytes 3538948
  129.8 16.2 %collective-permute-start.4 = (bf16[1,2,150528]{2,1,0:T(2,128)(2,1)S(1)}, bf16[1,2,150528]{2,1,0:T(2,128)(2,1)S(1)}, u32[]{:S(2)}, u32[]{:S(2)}) collective-permute-start(bf16[1,2,150528]{2,1,0:T(2,128)(2,1)S(1)} %get-tuple-element.7), channel_id=1, source_target_pairs={{128,129},{129,130},{130,131},{131,132},{132,133},{133,134},{134,1... | collective-permute-start | bytes 1806344 | tf_op jit(solution)/shard_map/ppermute | solution.py:31
  131.7 15.7 %collective-permute-start.5 = (bf16[1,2,150528]{2,1,0:T(2,128)(2,1)S(1)}, bf16[1,2,150528]{2,1,0:T(2,128)(2,1)S(1)}, u32[]{:S(2)}, u32[]{:S(2)}) collective-permute-start(bf16[1,2,150528]{2,1,0:T(2,128)(2,1)S(1)} %get-tuple-element.8), channel_id=1, source_target_pairs={{129,128},{130,129},{131,130},{132,131},{133,132},{134,133},{135,1... | collective-permute-start | bytes 1806344 | tf_op jit(solution)/shard_map/ppermute | solution.py:32
  140.5 11.5 %copy-start.1 = (bf16[1,768,2304]{2,1,0:T(8,128)(2,1)S(1)}, bf16[1,768,2304]{2,1,0:T(8,128)(2,1)}, u32[]{:S(2)}) copy-start(bf16[1,768,2304]{2,1,0:T(8,128)(2,1)} %param.11) | copy-start | bytes 10616836

commit v3 on v1

--- a/solution.py
+++ b/solution.py
@@ -2,6 +2,8 @@
 
 import jax
 import jax.numpy as jnp
+from jax.experimental import pallas as pl
+from jax.experimental.pallas import tpu as pltpu
 from jax import lax
 from jax.sharding import PartitionSpec as P
 
@@ -82,18 +84,65 @@
     return mixed_rows.reshape(pair_count, length, model_width).astype(jnp.bfloat16)
 
 
+def attention_kernel(q_ref, k_ref, v_ref, o_ref):
+    length = q_ref.shape[1]
+    lane_block = 2 * (q_ref.shape[2] // HEADS)
+    head_dim = lane_block // 2
+    lanes = lax.broadcasted_iota(jnp.int32, (length, lane_block), 1)
+
+    def one_block(h, carry):
+        columns = pl.ds(pl.multiple_of(h * lane_block, lane_block), lane_block)
+        q = q_ref[0, :, columns]
+        k = k_ref[0, :, columns]
+        v = v_ref[0, :, columns]
+        total = None
+        for i in range(2):
+            keep = (lanes >= i * head_dim) & (lanes < (i + 1) * head_dim)
+            q_i = jnp.where(keep, q, jnp.zeros_like(q))
+            scores = lax.dot_general(
+                q_i, k, (((1,), (1,)), ((), ())), preferred_element_type=jnp.float32
+            ) * (1.0 / math.sqrt(head_dim))
+            raised = jnp.exp(scores)
+            probs = (raised / jnp.sum(raised, axis=-1, keepdims=True)).astype(jnp.bfloat16)
+            v_i = jnp.where(keep, v, jnp.zeros_like(v))
+            mixed = jnp.dot(probs, v_i, preferred_element_type=jnp.float32)
+            total = mixed if total is None else total + mixed
+        o_ref[0, :, columns] = total.astype(o_ref.dtype)
+        return carry
+
+    lax.fori_loop(0, q_ref.shape[2] // lane_block, one_block, 0)
+
+
+def attend_blocks(q_arr, k_arr, v_arr, q_off, k_off, v_off, width):
+    pair_count, length = q_arr.shape[0], q_arr.shape[1]
+    block = (1, length, width)
+    flops = pair_count * HEADS * length * length * (width // HEADS) * 4 * 2
+    return pl.pallas_call(
+        attention_kernel,
+        out_shape=jax.ShapeDtypeStruct((pair_count, length, width), jnp.bfloat16),
+        grid=(pair_count,),
+        in_specs=[
+            pl.BlockSpec(block, lambda b: (b, 0, q_off)),
+            pl.BlockSpec(block, lambda b: (b, 0, k_off)),
+            pl.BlockSpec(block, lambda b: (b, 0, v_off)),
+        ],
+        out_specs=pl.BlockSpec(block, lambda b: (b, 0, 0)),
+        cost_estimate=pl.CostEstimate(
+            flops=flops,
+            transcendentals=pair_count * HEADS * length * length,
+            bytes_accessed=4 * pair_count * length * width * 2,
+        ),
+    )(q_arr, k_arr, v_arr)
+
+
 def attention_part(own_rows, partner_rows, w_qkv, w_self, w_query, w_pair, w_cross):
     model_width = own_rows.shape[-1]
     triple = project(layer_norm(own_rows), w_qkv).astype(jnp.bfloat16)
-    attended = attend(
-        triple[..., :model_width],
-        triple[..., model_width : 2 * model_width],
-        triple[..., 2 * model_width :],
-    )
+    attended = attend_blocks(triple, triple, triple, 0, 1, 2, model_width)
     stream = own_rows.astype(jnp.float32) + project(attended, w_self)
     query_rows = project(layer_norm(stream), w_query).astype(jnp.bfloat16)
     pair_kv = project(layer_norm(partner_rows), w_pair).astype(jnp.bfloat16)
-    crossed = attend(query_rows, pair_kv[..., :model_width], pair_kv[..., model_width:])
+    crossed = attend_blocks(query_rows, pair_kv, pair_kv, 0, 0, 1, model_width)
     return stream + project(crossed, w_cross)
 
 
@@ -165,7 +214,7 @@
     rim_rows = jnp.concatenate(
         [contributions[:, :img_local], contributions[:, 2 * img_local :]], axis=1
     )
-    extended = branch_one_padded(rim_rows, 1, img_local)
+    extended = branch_one_padded(rim_rows.astype(jnp.bfloat16), 1, img_local).astype(jnp.float32)
     image_sums = (
         contributions[:, img_local : 2 * img_local]
         + extended[:, :img_local]

time: 152 us -> 158 us (1.039)
  Pallas kernels: 0 us -> 30.2 us
  local copies, waits for them, and re-layouts: 33.3 us -> 15.3 us
  starting transfers between devices: 42.1 us -> 36.7 us
  matrix products: 35.1 us -> 30.8 us
  other arithmetic: 9.56 us -> 13.5 us
    pallas_call x0 -> x2, Pallas kernels: none -> 30.2 us  [attend_blocks(): pl.pallas_call(attention_kernel, out_shape=jax.ShapeDtypeStruct((pair_cou...]
    slice x7 -> x0, local copies, waits for them, and re-layouts: 15.2 us -> none  [the longest x2 4.4 us: attention_part(): triple[..., model_width:2 * model_width]]
    dot_general x4 -> x0, matrix products: 10.5 us -> none  [the longest x2 5.75 us: attend(): jnp.einsum('bqhd,bkhd->bhqk', query_heads, key_heads, preferred_element_t...]
    dot_general x5, matrix products: 11.8 us -> 18 us  [project(): result = jnp.dot(flattened, matrix, preferred_element_type=jnp.float32)]
    ppermute x2, starting transfers between devices: 17.4 us -> 11.7 us  [branch_one_padded(): after = lax.ppermute(initial, ('branch', 'pair'), down)]
    ppermute x2, waiting for transfers between devices: 16 us -> 12.9 us  [branch_one_padded(): before = lax.ppermute(last, ('branch', 'pair'), up)]
    add x1, other arithmetic: 2.01 us -> 4.59 us  [body(): contributions[:, img_local:2 * img_local] + extended[:, :img_local]]
    ppermute x2, waiting for transfers between devices: 1.75 us -> 3.93 us  [branch_one_padded(): after = lax.ppermute(initial, ('branch', 'pair'), down)]
  transfers between devices with their start and end apart: 7 -> 7, of which waited for: 4 -> 4; matrix products, arithmetic and copies ran while one was open for 13% -> 10% of each run, Pallas kernels for 0% -> 0%
where the time goes in v3:
time: 158 us; the launch traced here: 157 us
  starting transfers between devices  36.7 us (23%)
  matrix products  30.8 us (19%)
  waiting for transfers between devices  30.4 us (19%)
  Pallas kernels  30.2 us (19%)
  local copies, waits for them, and re-layouts  15.3 us (10%)
  other arithmetic  13.5 us (9%)
    pallas_call x2, Pallas kernels, attend_blocks(): pl.pallas_call(attention_kernel, out_shape=jax.ShapeDtypeStruct((pair_cou...  30.2 us
    dot_general x5, matrix products, project(): result = jnp.dot(flattened, matrix, preferred_element_type=jnp.float32)  18 us
    all_to_all x1, starting transfers between devices, gathered_weight(): got = lax.all_to_all(spread, 'pair', 0, 0, tiled=True).reshape(-1, half)  16.8 us
    all_to_all x1, waiting for transfers between devices, gathered_weight(): got = lax.all_to_all(spread, 'pair', 0, 0, tiled=True).reshape(-1, half)  13.6 us
    ppermute x2, waiting for transfers between devices, branch_one_padded(): before = lax.ppermute(last, ('branch', 'pair'), up)  12.9 us
    ppermute x2, starting transfers between devices, branch_one_padded(): after = lax.ppermute(initial, ('branch', 'pair'), down)  11.7 us
    dot_general x1, matrix products, select_rows(): jnp.dot(onehot.astype(jnp.bfloat16), window, preferred_element_type=jnp.f...  5.6 us
    dot_general x1, matrix products, embed_picked(): jnp.dot(picked, full_embed, preferred_element_type=jnp.float32)  4.8 us
  transfers between devices with their start and end apart: 7, of which 4 were waited for; matrix products, arithmetic and copies ran while one was open for 10% of the time, Pallas kernels for 0%

profile of v3, /device:TPU:1, one launch (start us, length us, event | category | flops | bytes accessed | tf_op | source)
XLA Modules:
  0.0 157.1 jit_solution(6656598429148871865)
XLA Ops:
  0.0 0.0 copy-start
  0.0 0.0 copy-start.3
  0.0 0.9 constant_dynamic-slice_fusion
  0.9 0.9 broadcast_in_dim.2
  1.8 16.8 %all-to-all-start = ((bf16[128,8,384]{2,1,0:T(8,128)(2,1)}), bf16[128,8,384]{2,1,0:T(8,128)(2,1)}, u32[]{:S(2)}, u32[]{:S(2)}) async-start(bf16[128,8,384]{2,1,0:T(8,128)(2,1)} %broadcast_in_dim.2), calls=%async_computation | async-start | bytes 1572864 | tf_op jit(solution)/shard_map/all_to_all | solution.py:42
  18.6 8.6 %collective-permute-start.1 = (bf16[2,200704]{1,0:T(2,128)(2,1)}, bf16[2,200704]{1,0:T(2,128)(2,1)}, u32[]{:S(2)}, u32[]{:S(2)}) collective-permute-start(bf16[2,200704]{1,0:T(2,128)(2,1)} %bitcast.46), channel_id=1, source_target_pairs={{129,128},{130,129},{131,130},{132,131},{133,132},{134,133},{135,1... | collective-permute-start | bytes 2408456 | tf_op jit(solution)/shard_map/ppermute | solution.py:34
  27.2 1.9 %collective-permute-start = (bf16[2,200704]{1,0:T(2,128)(2,1)}, bf16[2,200704]{1,0:T(2,128)(2,1)}, u32[]{:S(2)}, u32[]{:S(2)}) collective-permute-start(bf16[2,200704]{1,0:T(2,128)(2,1)} %bitcast.47), channel_id=1, source_target_pairs={{128,129},{129,130},{130,131},{131,132},{132,133},{133,134},{134,1... | collective-permute-start | bytes 2408456 | tf_op jit(solution)/shard_map/ppermute | solution.py:33
  29.1 13.6 %all-to-all-done = bf16[128,8,384]{2,1,0:T(8,128)(2,1)} async-done(((bf16[128,8,384]{2,1,0:T(8,128)(2,1)}), bf16[128,8,384]{2,1,0:T(8,128)(2,1)}, u32[]{:S(2)}, u32[]{:S(2)}) %all-to-all-start) | async-done | bytes 786464 | tf_op jit(solution)/shard_map/all_to_all | solution.py:42
  42.7 3.6 %collective-permute-start.2 = (bf16[1024,384]{1,0:T(8,128)(2,1)}, bf16[1024,384]{1,0:T(8,128)(2,1)}, u32[]{:S(2)}, u32[]{:S(2)}) collective-permute-start(bf16[1024,384]{1,0:T(8,128)(2,1)} %bitcast.3), channel_id=1, source_target_pairs={{0,128},{128,0},{1,129},{129,1},{2,130},{130,2},{3,131},{131,3},{4... | collective-permute-start | bytes 2359304 | tf_op jit(solution)/shard_map/ppermute | solution.py:43
  46.3 0.0 copy-done.3
  46.4 0.0 collective-permute-done.1
  46.4 4.4 %collective-permute-done = bf16[2,200704]{1,0:T(2,128)(2,1)} collective-permute-done((bf16[2,200704]{1,0:T(2,128)(2,1)}, bf16[2,200704]{1,0:T(2,128)(2,1)}, u32[]{:S(2)}, u32[]{:S(2)}) %collective-permute-start) | collective-permute-done | bytes 802848 | tf_op jit(solution)/shard_map/ppermute | solution.py:33
  50.7 5.6 %convolution_convert_fusion = bf16[4,200704]{1,0:T(4,128)(2,1)} fusion(bf16[2,200704]{1,0:T(2,128)(2,1)} %collective-permute-done.1, bf16[2,200704]{1,0:T(2,128)(2,1)} %bitcast.48, bf16[2,200704]{1,0:T(2,128)(2,1)} %collective-permute-done, s32[4]{0:T(128)S(1)} %fusion.33), kind=kOutput, calls=%fused_computation | convolution fusion | flops 17661976 | bytes 4014096 | tf_op jit(solution)/shard_map/dot_general | solution.py:150
  56.3 3.6 %reshape.204 = bf16[784,1024]{1,0:T(8,128)(2,1)} reshape(bf16[4,200704]{1,0:T(4,128)(2,1)} %convolution_convert_fusion) | data formatting | bytes 3211264 | tf_op jit(solution)/shard_map/reshape | solution.py:156
  59.9 0.0 collective-permute-done.2
  59.9 4.8 %convert_reduce_fusion.1 = (f32[784]{0:T(1024)S(1)}, bf16[784,768]{1,0:T(8,128)(2,1)}) fusion(bf16[784,1024]{1,0:T(8,128)(2,1)} %reshape.204, bf16[1024,384]{1,0:T(8,128)(2,1)} %collective-permute-done.2, bf16[1024,384]{1,0:T(8,128)(2,1)} %bitcast.3, pred[]{:T(512)S(6)} %eq.35), kind=kOutput, calls=%fused_computation.13 | convolution fusion | flops 1242008832 | bytes 4385857 | tf_op jit(solution)/shard_map/dot_general | solution.py:157
  64.7 2.2 %reshape.206 = bf16[4,196,768]{2,1,0:T(8,128)(2,1)} reshape(bf16[784,768]{1,0:T(8,128)(2,1)} %get-tuple-element.10) | data formatting | bytes 2408448 | tf_op jit(solution)/shard_map/reshape | solution.py:160
  67.0 1.8 %fusion.12 = f32[784]{0:T(1024)S(1)} fusion(bf16[784,768]{1,0:T(8,128)(2,1)} %get-tuple-element.10, f32[784]{0:T(1024)S(1)} %broadcast_multiply_fusion.2), kind=kLoop, calls=%fused_computation.24 | loop fusion | flops 2407664 | bytes 1210496 | tf_op jit(solution)/shard_map/reduce_sum | solution.py:59
  68.8 2.7 %fusion.13 = bf16[784,768]{1,0:T(8,128)(2,1)} fusion(bf16[784,768]{1,0:T(8,128)(2,1)} %get-tuple-element.10, f32[784]{0:T(1024)S(1)} %add_rsqrt_fusion.2, f32[784]{0:T(1024)S(1)} %broadcast_multiply_fusion.2), kind=kLoop, calls=%fused_computation.25 | loop fusion | flops 2408448 | bytes 2414720 | tf_op jit(solution)/shard_map/convert_element_type | solution.py:60
  71.4 2.2 %dot_general.28 = bf16[4,196,768]{2,1,0:T(8,128)(2,1)} reshape(bf16[784,768]{1,0:T(8,128)(2,1)} %fusion.13) | data formatting | bytes 2408448 | tf_op jit(solution)/shard_map/dot_general | solution.py:66
  73.7 0.0 copy-done
  73.7 6.1 %convolution_convert_fusion.1.q_ref.k_ref.v_ref = bf16[4,196,2304]{2,1,0:T(8,128)(2,1)} fusion(bf16[4,196,768]{2,1,0:T(8,128)(2,1)} %dot_general.28, bf16[1,768,2304]{2,1,0:T(8,128)(2,1)S(1)} %copy-done), kind=kOutput, calls=%fused_computation.2 | convolution fusion | flops 2776338432 | bytes 8355840 | tf_op jit(solution)/shard_map/dot_general | solution.py:66
  79.8 15.1 %shard_map.82 = bf16[4,196,768]{2,1,0:T(8,128)(2,1)} custom-call(bf16[4,196,2304]{2,1,0:T(8,128)(2,1)} %convolution_convert_fusion.1.q_ref.k_ref.v_ref, bf16[4,196,2304]{2,1,0:T(8,128)(2,1)} %convolution_convert_fusion.1.q_ref.k_ref.v_ref, bf16[4,196,2304]{2,1,0:T(8,128)(2,1)} %convolution_convert_fusion.1.q_ref.k_ref.v_ref), custom_call_target="tpu_custom_call" | custom-call | flops 944111616 | bytes 4816896 | tf_op jit(solution)/shard_map/pallas_call | solution.py:120
  94.9 0.0 copy-start.2
  94.9 0.0 copy-start.5
  94.9 1.9 %copy.21 = bf16[4,196,768]{2,0,1:T(4,128)(2,1)S(1)} copy(bf16[4,196,768]{2,1,0:T(8,128)(2,1)} %reshape.206) | data formatting | bytes 2408448 | tf_op jit(solution)/shard_map/reshape | solution.py:160
  96.8 0.3 collective-permute-start.3
  97.1 0.0 copy-done.2
  97.1 0.0 copy-done.5
  97.1 2.5 %fusion.40 = (f32[4,196]{1,0:T(4,128)S(1)}, f32[4,196,768]{2,1,0:T(8,128)S(1)}) fusion(bf16[4,196,768]{2,1,0:T(8,128)(2,1)} %shard_map.82, bf16[1,768,768]{2,1,0:T(8,128)(2,1)S(1)} %copy-done.5, bf16[4,196,768]{2,1,0:T(8,128)(2,1)S(1)} %copy-done.2), kind=kOutput, calls=%fused_computation.75 | convolution fusion | flops 926649600 | bytes 5999680 | tf_op jit(solution)/shard_map/dot_general | solution.py:66
  99.6 0.0 copy-start.1
  99.6 0.0 copy-start.6
  99.7 0.4 multiply_reduce_fusion
  100.1 1.7 %copy-done.6 = bf16[1,768,768]{2,1,0:T(8,128)(2,1)S(1)} copy-done((bf16[1,768,768]{2,1,0:T(8,128)(2,1)S(1)}, bf16[1,768,768]{2,1,0:T(8,128)(2,1)}, u32[]{:S(2)}) %copy-start.6) | copy-done | bytes 1179672
  101.8 2.3 %convolution_convert_fusion.3.q_ref = bf16[4,196,768]{2,1,0:T(8,128)(2,1)} fusion(f32[4,196,768]{2,1,0:T(8,128)S(1)} %get-tuple-element.12, f32[4,196]{1,0:T(4,128)S(1)} %add_rsqrt_fusion.1, f32[4,196]{1,0:T(4,128)S(1)} %broadcast_multiply_fusion.1, bf16[1,768,768]{2,1,0:T(8,128)(2,1)S(1)} %copy-done.6), kind=kOutput, calls=%fused_computation.35 | convolution fusion | flops 927252480 | bytes 4798592 | tf_op jit(solution)/shard_map/dot_general | solution.py:66
  104.0 0.0 copy-done.1
  104.1 0.0 collective-permute-done.3
  104.1 0.5 convert_reduce_fusion
  104.6 0.0 copy-start.4
  104.6 1.2 fusion.10
  105.9 0.9 fusion.11
  106.8 0.0 copy-done.4
  106.8 3.5 %convolution_convert_fusion.2.k_ref.v_ref = bf16[4,196,1536]{2,1,0:T(8,128)(2,1)} fusion(bf16[1,768,1536]{2,1,0:T(8,128)(2,1)S(1)} %copy-done.4, bf16[4,196,768]{2,0,1:T(4,128)(2,1)S(1)} %fusion.11), kind=kOutput, calls=%fused_computation.4 | convolution fusion | flops 1850892288 | bytes 5971968 | tf_op jit(solution)/shard_map/dot_general | solution.py:66
  110.3 15.1 %shard_map.83 = bf16[4,196,768]{2,1,0:T(8,128)(2,1)} custom-call(bf16[4,196,768]{2,1,0:T(8,128)(2,1)} %convolution_convert_fusion.3.q_ref, bf16[4,196,1536]{2,1,0:T(8,128)(2,1)} %convolution_convert_fusion.2.k_ref.v_ref, bf16[4,196,1536]{2,1,0:T(8,128)(2,1)} %convolution_convert_fusion.2.k_ref.v_ref), custom_call_target="tpu_custom_call" | custom-call | flops 944111616 | bytes 4816896 | tf_op jit(solution)/shard_map/pallas_call | solution.py:120
  125.4 3.6 %add_bitcast_fusion = f32[1,4,196,768]{3,2,1,0:T(8,128)S(1)} fusion(f32[4,196,768]{2,1,0:T(8,128)} %copy-done.1, bf16[4,196,768]{2,1,0:T(8,128)(2,1)} %shard_map.83, bf16[1,768,768]{2,1,0:T(8,128)(2,1)} %param.15), kind=kOutput, calls=%fused_computation.18 | convolution fusion | flops 925446144 | bytes 7200768 | tf_op jit(solution)/shard_map/dot_general | solution.py:66
  129.0 0.9 copy.28
  129.9 2.4 %convolution_bitcast_fusion = f32[1,6,150528]{2,1,0:T(8,128)S(1)} fusion(f32[4,150528]{1,0:T(4,128)S(1)} %bitcast.43, s32[4]{0:T(128)S(1)} %get-tuple-element.5), kind=kOutput, calls=%fused_computation.1 | convolution fusion | flops 43352088 | bytes 6021136 | tf_op jit(solution)/shard_map/dot_general | solution.py:207
  132.4 0.9 fusion.39
  133.2 3.1 %collective-permute-start.5 = (bf16[1,2,150528]{2,1,0:T(2,128)(2,1)S(1)}, bf16[1,2,150528]{2,1,0:T(2,128)(2,1)S(1)}, u32[]{:S(2)}, u32[]{:S(2)}) collective-permute-start(bf16[1,2,150528]{2,1,0:T(2,128)(2,1)S(1)} %get-tuple-element.8), channel_id=1, source_target_pairs={{129,128},{130,129},{131,130},{132,131},{133,132},{134,133},{135,1... | collective-permute-start | bytes 1806344 | tf_op jit(solution)/shard_map/ppermute | solution.py:34
  136.3 2.4 %collective-permute-start.4 = (bf16[1,2,150528]{2,1,0:T(2,128)(2,1)S(1)}, bf16[1,2,150528]{2,1,0:T(2,128)(2,1)S(1)}, u32[]{:S(2)}, u32[]{:S(2)}) collective-permute-start(bf16[1,2,150528]{2,1,0:T(2,128)(2,1)S(1)} %get-tuple-element.7), channel_id=1, source_target_pairs={{128,129},{129,130},{130,131},{131,132},{132,133},{133,134},{134,1... | collective-permute-start | bytes 1806344 | tf_op jit(solution)/shard_map/ppermute | solution.py:33
  138.8 1.3 maximum_bitcast_fusion
  140.1 3.9 %collective-permute-done.5 = bf16[1,2,150528]{2,1,0:T(2,128)(2,1)S(1)} collective-permute-done((bf16[1,2,150528]{2,1,0:T(2,128)(2,1)S(1)}, bf16[1,2,150528]{2,1,0:T(2,128)(2,1)S(1)}, u32[]{:S(2)}, u32[]{:S(2)}) %collective-permute-start.5) | collective-permute-done | bytes 602144 | tf_op jit(solution)/shard_map/ppermute | solution.py:34
  144.0 8.5 %collective-permute-done.4 = bf16[1,2,150528]{2,1,0:T(2,128)(2,1)S(1)} collective-permute-done((bf16[1,2,150528]{2,1,0:T(2,128)(2,1)S(1)}, bf16[1,2,150528]{2,1,0:T(2,128)(2,1)S(1)}, u32[]{:S(2)}, u32[]{:S(2)}) %collective-permute-start.4) | collective-permute-done | bytes 602144 | tf_op jit(solution)/shard_map/ppermute | solution.py:33
  152.5 4.6 %fusion.26 = f32[1,2,150528]{2,1,0:T(2,128)} fusion(f32[1,6,150528]{2,1,0:T(8,128)S(1)} %convolution_bitcast_fusion, bf16[1,2,150528]{2,1,0:T(2,128)(2,1)S(1)} %collective-permute-done.5, bf16[1,4,150528]{2,1,0:T(4,128)(2,1)S(1)} %maximum_bitcast_fusion, bf16[1,2,150528]{2,1,0:T(2,128)(2,1)S(1)} %collective-permute-done.4), kind=kLoop, calls=%fused_computation.41 | loop fusion | flops 4214784 | bytes 4816896 | tf_op jit(solution)/shard_map/add | solution.py:219
  (8 shorter events, 0.1 us)
Async XLA Ops:
  0.0 73.7 %copy-start = (bf16[1,768,2304]{2,1,0:T(8,128)(2,1)S(1)}, bf16[1,768,2304]{2,1,0:T(8,128)(2,1)}, u32[]{:S(2)}) copy-start(bf16[1,768,2304]{2,1,0:T(8,128)(2,1)} %param.11) | copy-start | bytes 10616836
  0.0 46.3 %copy-start.3 = (s32[4,2]{0,1:T(2,128)S(1)}, s32[4,2]{0,1:T(2,128)}, u32[]{:S(2)}) copy-start(s32[4,2]{0,1:T(2,128)} %param.9) | copy-start | bytes 100
  1.8 40.9 %all-to-all-start = ((bf16[128,8,384]{2,1,0:T(8,128)(2,1)}), bf16[128,8,384]{2,1,0:T(8,128)(2,1)}, u32[]{:S(2)}, u32[]{:S(2)}) async-start(bf16[128,8,384]{2,1,0:T(8,128)(2,1)} %broadcast_in_dim.2), calls=%async_computation | async-start | bytes 1572864 | tf_op jit(solution)/shard_map/all_to_all | solution.py:42
  18.6 27.8 %collective-permute-start.1 = (bf16[2,200704]{1,0:T(2,128)(2,1)}, bf16[2,200704]{1,0:T(2,128)(2,1)}, u32[]{:S(2)}, u32[]{:S(2)}) collective-permute-start(bf16[2,200704]{1,0:T(2,128)(2,1)} %bitcast.46), channel_id=1, source_target_pairs={{129,128},{130,129},{131,130},{132,131},{133,132},{134,133},{135,1... | collective-permute-start | bytes 2408456 | tf_op jit(solution)/shard_map/ppermute | solution.py:34
  27.2 23.5 %collective-permute-start = (bf16[2,200704]{1,0:T(2,128)(2,1)}, bf16[2,200704]{1,0:T(2,128)(2,1)}, u32[]{:S(2)}, u32[]{:S(2)}) collective-permute-start(bf16[2,200704]{1,0:T(2,128)(2,1)} %bitcast.47), channel_id=1, source_target_pairs={{128,129},{129,130},{130,131},{131,132},{132,133},{133,134},{134,1... | collective-permute-start | bytes 2408456 | tf_op jit(solution)/shard_map/ppermute | solution.py:33
  42.7 17.2 %collective-permute-start.2 = (bf16[1024,384]{1,0:T(8,128)(2,1)}, bf16[1024,384]{1,0:T(8,128)(2,1)}, u32[]{:S(2)}, u32[]{:S(2)}) collective-permute-start(bf16[1024,384]{1,0:T(8,128)(2,1)} %bitcast.3), channel_id=1, source_target_pairs={{0,128},{128,0},{1,129},{129,1},{2,130},{130,2},{3,131},{131,3},{4... | collective-permute-start | bytes 2359304 | tf_op jit(solution)/shard_map/ppermute | solution.py:43
  94.9 2.2 %copy-start.2 = (bf16[4,196,768]{2,1,0:T(8,128)(2,1)S(1)}, bf16[4,196,768]{2,1,0:T(8,128)(2,1)}, u32[]{:S(2)}) copy-start(bf16[4,196,768]{2,1,0:T(8,128)(2,1)} %reshape.206) | copy-start | bytes 3612676
  94.9 2.2 %copy-start.5 = (bf16[1,768,768]{2,1,0:T(8,128)(2,1)S(1)}, bf16[1,768,768]{2,1,0:T(8,128)(2,1)}, u32[]{:S(2)}) copy-start(bf16[1,768,768]{2,1,0:T(8,128)(2,1)} %param.12) | copy-start | bytes 3538948
  96.8 7.3 %collective-permute-start.3 = (bf16[4,196,768]{2,0,1:T(4,128)(2,1)S(1)}, bf16[4,196,768]{2,0,1:T(4,128)(2,1)S(1)}, u32[]{:S(2)}, u32[]{:S(2)}) collective-permute-start(bf16[4,196,768]{2,0,1:T(4,128)(2,1)S(1)} %copy.21), channel_id=1, source_target_pairs={{0,128},{128,0},{1,129},{129,1},{2,130},{130,2},{3,131},{131,3},{4... | collective-permute-start | bytes 3612680 | tf_op jit(solution)/shard_map/ppermute | solution.py:52
  99.6 4.4 %copy-start.1 = (f32[4,196,768]{2,1,0:T(8,128)}, f32[4,196,768]{2,1,0:T(8,128)S(1)}, u32[]{:S(2)}) copy-start(f32[4,196,768]{2,1,0:T(8,128)S(1)} %get-tuple-element.12) | copy-start | bytes 7225348
  99.6 2.1 %copy-start.6 = (bf16[1,768,768]{2,1,0:T(8,128)(2,1)S(1)}, bf16[1,768,768]{2,1,0:T(8,128)(2,1)}, u32[]{:S(2)}) copy-start(bf16[1,768,768]{2,1,0:T(8,128)(2,1)} %param.13) | copy-start | bytes 3538948
  104.6 2.2 %copy-start.4 = (bf16[1,768,1536]{2,1,0:T(8,128)(2,1)S(1)}, bf16[1,768,1536]{2,1,0:T(8,128)(2,1)}, u32[]{:S(2)}) copy-start(bf16[1,768,1536]{2,1,0:T(8,128)(2,1)} %param.14) | copy-start | bytes 7077892
  133.2 10.8 %collective-permute-start.5 = (bf16[1,2,150528]{2,1,0:T(2,128)(2,1)S(1)}, bf16[1,2,150528]{2,1,0:T(2,128)(2,1)S(1)}, u32[]{:S(2)}, u32[]{:S(2)}) collective-permute-start(bf16[1,2,150528]{2,1,0:T(2,128)(2,1)S(1)} %get-tuple-element.8), channel_id=1, source_target_pairs={{129,128},{130,129},{131,130},{132,131},{133,132},{134,133},{135,1... | collective-permute-start | bytes 1806344 | tf_op jit(solution)/shard_map/ppermute | solution.py:34
  136.3 16.2 %collective-permute-start.4 = (bf16[1,2,150528]{2,1,0:T(2,128)(2,1)S(1)}, bf16[1,2,150528]{2,1,0:T(2,128)(2,1)S(1)}, u32[]{:S(2)}, u32[]{:S(2)}) collective-permute-start(bf16[1,2,150528]{2,1,0:T(2,128)(2,1)S(1)} %get-tuple-element.7), channel_id=1, source_target_pairs={{128,129},{129,130},{130,131},{131,132},{132,133},{133,134},{134,1... | collective-permute-start | bytes 1806344 | tf_op jit(solution)/shard_map/ppermute | solution.py:33

commit v4 on v2

--- a/solution.py
+++ b/solution.py
@@ -82,19 +82,39 @@
     return mixed_rows.reshape(pair_count, length, model_width).astype(jnp.bfloat16)
 
 
+def heads_of(values, matrix, parts):
+    width = values.shape[-1]
+    shaped = matrix.reshape(width, parts, HEADS, matrix.shape[-1] // (parts * HEADS))
+    return jnp.einsum(
+        "btd,dshe->sbhte", values, shaped, preferred_element_type=jnp.float32
+    ).astype(jnp.bfloat16)
+
+
+def attend_heads(query_heads, key_heads, value_heads):
+    head_dim = query_heads.shape[-1]
+    scores = jnp.einsum(
+        "bhqe,bhke->bhqk", query_heads, key_heads, preferred_element_type=jnp.float32
+    ) * (1.0 / math.sqrt(head_dim))
+    raised = jnp.exp(scores)
+    attn_probs = (raised / jnp.sum(raised, axis=-1, keepdims=True)).astype(jnp.bfloat16)
+    return jnp.einsum(
+        "bhqk,bhke->bhqe", attn_probs, value_heads, preferred_element_type=jnp.float32
+    ).astype(jnp.bfloat16)
+
+
+def merged(mixed, matrix):
+    shaped = matrix.reshape(HEADS, mixed.shape[-1], matrix.shape[-1])
+    return jnp.einsum("bhte,hed->btd", mixed, shaped, preferred_element_type=jnp.float32)
+
+
 def attention_part(own_rows, partner_rows, w_qkv, w_self, w_query, w_pair, w_cross):
-    model_width = own_rows.shape[-1]
-    triple = project(layer_norm(own_rows), w_qkv).astype(jnp.bfloat16)
-    attended = attend(
-        triple[..., :model_width],
-        triple[..., model_width : 2 * model_width],
-        triple[..., 2 * model_width :],
-    )
-    stream = own_rows.astype(jnp.float32) + project(attended, w_self)
-    query_rows = project(layer_norm(stream), w_query).astype(jnp.bfloat16)
-    pair_kv = project(layer_norm(partner_rows), w_pair).astype(jnp.bfloat16)
-    crossed = attend(query_rows, pair_kv[..., :model_width], pair_kv[..., model_width:])
-    return stream + project(crossed, w_cross)
+    triple = heads_of(layer_norm(own_rows), w_qkv, 3)
+    attended = attend_heads(triple[0], triple[1], triple[2])
+    stream = own_rows.astype(jnp.float32) + merged(attended, w_self)
+    query_rows = heads_of(layer_norm(stream), w_query, 1)[0]
+    pair_kv = heads_of(layer_norm(partner_rows), w_pair, 2)
+    crossed = attend_heads(query_rows, pair_kv[0], pair_kv[1])
+    return stream + merged(crossed, w_cross)
 
 
 def select_rows(onehot, window):

time: 153 us -> 156 us (1.020)
  matrix products: 29.4 us -> 49.1 us
  local copies, waits for them, and re-layouts: 43.6 us -> 29 us
  waiting for transfers between devices: 21.1 us -> 18.7 us
    dot_general x9 -> x6, matrix products: 22.2 us -> 42.8 us  [the longest x2 18.1 us: merged(): jnp.einsum('bhte,hed->btd', mixed, shaped, preferred_element_type=jnp.flo...]
    slice x7 -> x0, local copies, waits for them, and re-layouts: 15.3 us -> none  [the longest x2 4.41 us: attention_part(): triple[..., model_width:2 * model_width]]
    unnamed x30 -> x23, local copies, waits for them, and re-layouts: 5.6 us -> 14.4 us
    reshape x2, local copies, waits for them, and re-layouts: 5.14 us -> 2.68 us  [embed_picked(): return embedded_rows.reshape(pair_count, tokens_per, model_width)]
    ppermute x2, waiting for transfers between devices: 6.26 us -> 3.88 us  [branch_one_padded(): before = lax.ppermute(last, ('branch', 'pair'), up)]
    dot_general x1 -> x0, local copies, waits for them, and re-layouts: 2.23 us -> none  [project(): result = jnp.dot(flattened, matrix, preferred_element_type=jnp.float32)]
  transfers between devices with their start and end apart: 7 -> 7, of which waited for: 4 -> 3; matrix products, arithmetic and copies ran while one was open for 18% -> 22% of each run, Pallas kernels for 0% -> 0%
where the time goes in v4:
time: 156 us; the launch traced here: 155 us
  matrix products  49.1 us (31%)
  starting transfers between devices  41.9 us (27%)
  local copies, waits for them, and re-layouts  29 us (19%)
  waiting for transfers between devices  18.7 us (12%)
  other arithmetic  15.9 us (10%)
    dot_general x2, matrix products, merged(): jnp.einsum('bhte,hed->btd', mixed, shaped, preferred_element_type=jnp.flo...  18.1 us
    ppermute x2, starting transfers between devices, branch_one_padded(): after = lax.ppermute(initial, ('branch', 'pair'), down)  16.9 us
    all_to_all x1, starting transfers between devices, gathered_weight(): got = lax.all_to_all(spread, 'pair', 0, 0, tiled=True).reshape(-1, half)  16.8 us
    dot_general x2, matrix products, attend_heads(): jnp.einsum('bhqe,bhke->bhqk', query_heads, key_heads, preferred_element_t...  14.6 us
    unnamed x23, local copies, waits for them, and re-layouts  14.4 us
    all_to_all x1, waiting for transfers between devices, gathered_weight(): got = lax.all_to_all(spread, 'pair', 0, 0, tiled=True).reshape(-1, half)  13.4 us
    dot_general x2, matrix products, heads_of(): jnp.einsum('btd,dshe->sbhte', values, shaped, preferred_element_type=jnp....  10.2 us
    add x1, other arithmetic, body(): contributions[:, img_local:2 * img_local] + extended[:, :img_local]  4.61 us
  transfers between devices with their start and end apart: 7, of which 3 were waited for; matrix products, arithmetic and copies ran while one was open for 22% of the time, Pallas kernels for 0%

profile of v4, /device:TPU:1, one launch (start us, length us, event | category | flops | bytes accessed | tf_op | source)
XLA Modules:
  0.0 154.8 jit_solution(16373539398238885176)
XLA Ops:
  0.0 0.0 copy-start
  0.0 0.0 copy-start.7
  0.0 0.8 constant_dynamic-slice_fusion
  0.8 0.9 broadcast_in_dim.3
  1.8 16.8 %all-to-all-start = ((bf16[128,8,384]{2,1,0:T(8,128)(2,1)}), bf16[128,8,384]{2,1,0:T(8,128)(2,1)}, u32[]{:S(2)}, u32[]{:S(2)}) async-start(bf16[128,8,384]{2,1,0:T(8,128)(2,1)} %broadcast_in_dim.3), calls=%async_computation | async-start | bytes 1572864 | tf_op jit(solution)/shard_map/all_to_all | solution.py:40
  18.6 2.4 %collective-permute-start = (bf16[2,200704]{1,0:T(2,128)(2,1)}, bf16[2,200704]{1,0:T(2,128)(2,1)}, u32[]{:S(2)}, u32[]{:S(2)}) collective-permute-start(bf16[2,200704]{1,0:T(2,128)(2,1)} %bitcast.106), channel_id=1, source_target_pairs={{128,129},{129,130},{130,131},{131,132},{132,133},{133,134},{134,1... | collective-permute-start | bytes 2408456 | tf_op jit(solution)/shard_map/ppermute | solution.py:31
  21.0 8.3 %collective-permute-start.1 = (bf16[2,200704]{1,0:T(2,128)(2,1)}, bf16[2,200704]{1,0:T(2,128)(2,1)}, u32[]{:S(2)}, u32[]{:S(2)}) collective-permute-start(bf16[2,200704]{1,0:T(2,128)(2,1)} %bitcast.107), channel_id=1, source_target_pairs={{129,128},{130,129},{131,130},{132,131},{133,132},{134,133},{135,1... | collective-permute-start | bytes 2408456 | tf_op jit(solution)/shard_map/ppermute | solution.py:32
  29.3 13.4 %all-to-all-done = bf16[128,8,384]{2,1,0:T(8,128)(2,1)} async-done(((bf16[128,8,384]{2,1,0:T(8,128)(2,1)}), bf16[128,8,384]{2,1,0:T(8,128)(2,1)}, u32[]{:S(2)}, u32[]{:S(2)}) %all-to-all-start) | async-done | bytes 786464 | tf_op jit(solution)/shard_map/all_to_all | solution.py:40
  42.7 3.6 %collective-permute-start.2 = (bf16[1024,384]{1,0:T(8,128)(2,1)}, bf16[1024,384]{1,0:T(8,128)(2,1)}, u32[]{:S(2)}, u32[]{:S(2)}) collective-permute-start(bf16[1024,384]{1,0:T(8,128)(2,1)} %bitcast.3), channel_id=1, source_target_pairs={{0,128},{128,0},{1,129},{129,1},{2,130},{130,2},{3,131},{131,3},{4... | collective-permute-start | bytes 2359304 | tf_op jit(solution)/shard_map/ppermute | solution.py:41
  46.3 0.0 copy-done.7
  46.3 0.2 copy.47
  46.5 5.8 %copy.48 = bf16[1,768,2304]{1,2,0:T(8,128)(2,1)} copy(bf16[1,768,2304]{2,1,0:T(8,128)(2,1)} %param.11) | data formatting | bytes 7077888 | tf_op args[3]
  52.3 0.0 copy-start.6
  52.3 0.0 copy-start.8
  52.3 4.4 %copy.56 = bf16[1,768,1536]{1,2,0:T(8,128)(2,1)} copy(bf16[1,768,1536]{2,1,0:T(8,128)(2,1)} %param.14) | data formatting | bytes 4718592 | tf_op args[6]
  56.6 0.0 copy-done.6
  56.6 1.5 copy.50
  58.1 0.0 copy-done.8
  58.1 0.0 collective-permute-done
  58.1 1.6 %concatenate.51 = bf16[2,196,1024]{2,1,0:T(8,128)(2,1)S(1)} reshape(bf16[2,200704]{1,0:T(2,128)(2,1)} %collective-permute-done) | data formatting | bytes 1605632 | tf_op jit(solution)/shard_map/concatenate | solution.py:33
  59.8 0.0 collective-permute-done.1
  59.8 2.5 %concatenate.52 = bf16[2,196,1024]{2,1,0:T(8,128)(2,1)} reshape(bf16[2,200704]{1,0:T(2,128)(2,1)} %collective-permute-done.1) | data formatting | bytes 1605632 | tf_op jit(solution)/shard_map/concatenate | solution.py:33
  62.3 2.9 %pad_maximum_fusion = bf16[6,196,1024]{2,1,0:T(8,128)(2,1)} fusion(bf16[2,196,1024]{2,1,0:T(8,128)(2,1)} %concatenate.52, bf16[2,196,1024]{2,1,0:T(8,128)(2,1)S(1)} %copy.47, bf16[2,196,1024]{2,1,0:T(8,128)(2,1)S(1)} %concatenate.51), kind=kLoop, calls=%fused_computation.20 | loop fusion | flops 2408448 | bytes 4816896 | tf_op jit(solution)/shard_map/concatenate | solution.py:33
  65.2 2.3 %gather_fusion = bf16[4,196,1024]{2,1,0:T(8,128)(2,1)S(1)} fusion(bf16[6,196,1024]{2,1,0:T(8,128)(2,1)} %pad_maximum_fusion, s32[1024]{0:T(1024)S(1)} %pad_clamp_fusion), kind=kCustom, calls=%fused_computation | custom fusion | bytes 3211280 | tf_op jit(solution)/shard_map/jit(_take)/gather | solution.py:128
  67.5 1.4 reshape.199
  68.9 0.0 collective-permute-done.2
  68.9 3.9 %convert_reduce_fusion.1 = (f32[784]{0:T(1024)S(1)}, bf16[784,768]{1,0:T(8,128)(2,1)S(1)}) fusion(bf16[784,1024]{1,0:T(8,128)(2,1)} %reshape.199, bf16[1024,384]{1,0:T(8,128)(2,1)} %collective-permute-done.2, bf16[1024,384]{1,0:T(8,128)(2,1)} %bitcast.3, pred[]{:T(512)S(6)} %eq.20), kind=kOutput, calls=%fused_computation.15 | convolution fusion | flops 1242008832 | bytes 4385857 | tf_op jit(solution)/shard_map/dot_general | solution.py:129
  72.8 1.2 reshape.201
  74.0 0.5 fusion.11
  74.5 1.4 fusion.12
  75.9 1.4 reshape.213
  77.2 6.1 %convert_bitcast_fusion = bf16[3,4,12,196,64]{3,4,2,0,1:T(8,128)(2,1)S(1)} fusion(bf16[768,3,12,64,1]{0,3,2,1,4:T(8,128)(2,1)} %bitcast.102, bf16[4,196,768,1,1]{2,1,0,3,4:T(8,128)(2,1)S(1)} %reshape.213), kind=kOutput, calls=%fused_computation.10 | convolution fusion | flops 2776338432 | bytes 8355840 | tf_op jit(solution)/shard_map/btd,dshe->sbhte/dot_general | solution.py:88
  83.4 0.0 copy-start.5
  83.4 0.0 copy-start.2
  83.4 5.2 %fusion = (f32[4,12,196]{2,1,0:T(8,128)S(1)}, f32[4,12,196,196]{2,3,1,0:T(8,128)}) fusion(bf16[3,4,12,196,64]{3,4,2,0,1:T(8,128)(2,1)S(1)} %convert_bitcast_fusion), kind=kOutput, calls=%fused_computation.6 | convolution fusion | flops 239706432 | bytes 10559232 | tf_op jit(solution)/shard_map/bhqe,bhke->bhqk/dot_general | solution.py:95
  88.6 0.0 copy-done.5
  88.6 0.0 copy-done.2
  88.6 1.5 copy.51
  90.1 0.0 collective-permute-start.3
  90.1 0.0 copy-done
  90.1 8.7 %fusion.49 = (f32[4,196]{1,0:T(4,128)S(1)}, f32[4,196,768]{2,1,0:T(8,128)}) fusion(bf16[12,64,768,1]{2,1,0,3:T(8,128)(2,1)S(1)} %bitcast.99, f32[4,12,196,196]{2,3,1,0:T(8,128)} %get-tuple-element.12, f32[4,12,196]{2,1,0:T(8,128)S(1)} %get-tuple-element.11, bf16[3,4,12,196,64]{3,4,2,0,1:T(8,128)(2,1)} %copy-done.5, bf16[4,196,768]{2,1,0:T(8,128)(2,1)} %reshape.201), kind=kOutput, calls=%fused_computation.88 | convolution fusion | flops 1168811520 | bytes 16260928 | tf_op jit(solution)/shard_map/bhte,hed->btd/dot_general | solution.py:107
  98.8 2.1 %multiply_reduce_fusion = f32[4,196]{1,0:T(4,128)S(1)} fusion(f32[4,196,768]{2,1,0:T(8,128)} %get-tuple-element.14, f32[4,196]{1,0:T(4,128)S(1)} %broadcast_multiply_fusion.1), kind=kLoop, calls=%fused_computation.25 | loop fusion | flops 1805552 | bytes 2414720 | tf_op jit(solution)/shard_map/reduce_sum | solution.py:57
  100.9 0.0 collective-permute-done.3
  100.9 0.5 convert_reduce_fusion
  101.4 0.0 copy-start.4
  101.5 1.1 fusion.9
  102.6 1.1 fusion.35
  103.8 0.0 copy-done.4
  103.8 0.0 copy-start.3
  103.8 4.1 %convert_bitcast_fusion.1 = bf16[2,4,12,196,64]{3,4,2,0,1:T(8,128)(2,1)} fusion(bf16[768,2,12,64,1]{0,3,2,1,4:T(8,128)(2,1)S(1)} %bitcast.105, bf16[4,196,768,1,1]{2,0,1,4,3:T(4,128)(2,1)S(1)} %fusion.35), kind=kOutput, calls=%fused_computation.11 | convolution fusion | flops 1850892288 | bytes 5971968 | tf_op jit(solution)/shard_map/btd,dshe->sbhte/dot_general | solution.py:88
  107.9 0.0 copy-done.3
  107.9 9.3 %fusion.1 = (f32[4,12,196]{2,1,0:T(8,128)S(1)}, f32[4,12,196,196]{2,3,1,0:T(8,128)}) fusion(bf16[2,4,12,196,64]{3,4,2,0,1:T(8,128)(2,1)} %convert_bitcast_fusion.1, bf16[768,12,64,1]{0,2,1,3:T(8,128)(2,1)S(1)} %bitcast.101, f32[4,196,768]{2,1,0:T(8,128)} %get-tuple-element.14, f32[4,196]{1,0:T(4,128)S(1)} %add_rsqrt_fusion.1, ...), kind=kOutput, calls=%fused_computation.7 | convolution fusion | flops 1166958848 | bytes 12629888 | tf_op jit(solution)/shard_map/bhqe,bhke->bhqk/dot_general | solution.py:95
  117.2 9.4 %fusion.8 = f32[1,4,196,768]{3,2,1,0:T(8,128)} fusion(f32[4,196,768]{2,1,0:T(8,128)} %get-tuple-element.14, bf16[12,64,768,1]{2,1,0,3:T(8,128)(2,1)} %bitcast.108, f32[4,12,196,196]{2,3,1,0:T(8,128)} %get-tuple-element.16, f32[4,12,196]{2,1,0:T(8,128)S(1)} %get-tuple-element.15, bf16[2,4,12,196,64]{3,4,2,0,1:T(8,128)(2,1)} %convert_bitcast_fusion.1), kind=kOutput, calls=%fused_computation.22 | convolution fusion | flops 1167608064 | bytes 17486592 | tf_op jit(solution)/shard_map/bhte,hed->btd/dot_general | solution.py:107
  126.6 2.6 %copy.69 = f32[1,4,196,768]{3,1,2,0:T(4,128)S(1)} copy(f32[1,4,196,768]{3,2,1,0:T(8,128)} %fusion.8) | data formatting | bytes 4816896
  129.2 2.4 %convolution_bitcast_fusion = f32[1,6,150528]{2,1,0:T(8,128)S(1)} fusion(f32[4,150528]{1,0:T(4,128)S(1)} %bitcast.100, s32[4]{0:T(128)S(1)} %get-tuple-element.5), kind=kOutput, calls=%fused_computation.1 | convolution fusion | flops 43352088 | bytes 6021136 | tf_op jit(solution)/shard_map/dot_general | solution.py:179
  131.6 0.9 fusion.48
  132.5 2.1 %collective-permute-start.4 = (bf16[1,2,150528]{2,1,0:T(2,128)(2,1)S(1)}, bf16[1,2,150528]{2,1,0:T(2,128)(2,1)S(1)}, u32[]{:S(2)}, u32[]{:S(2)}) collective-permute-start(bf16[1,2,150528]{2,1,0:T(2,128)(2,1)S(1)} %get-tuple-element.7), channel_id=1, source_target_pairs={{128,129},{129,130},{130,131},{131,132},{132,133},{133,134},{134,1... | collective-permute-start | bytes 1806344 | tf_op jit(solution)/shard_map/ppermute | solution.py:31
  134.7 8.6 %collective-permute-start.5 = (bf16[1,2,150528]{2,1,0:T(2,128)(2,1)S(1)}, bf16[1,2,150528]{2,1,0:T(2,128)(2,1)S(1)}, u32[]{:S(2)}, u32[]{:S(2)}) collective-permute-start(bf16[1,2,150528]{2,1,0:T(2,128)(2,1)S(1)} %get-tuple-element.8), channel_id=1, source_target_pairs={{129,128},{130,129},{131,130},{132,131},{133,132},{134,133},{135,1... | collective-permute-start | bytes 1806344 | tf_op jit(solution)/shard_map/ppermute | solution.py:32
  143.3 0.0 copy-start.1
  143.3 1.6 %maximum_bitcast_fusion = bf16[1,4,150528]{2,1,0:T(4,128)(2,1)S(1)} fusion(bf16[2,150528]{1,0:T(2,128)(2,1)S(1)} %bitcast.104, bf16[2,150528]{1,0:T(2,128)(2,1)S(1)} %bitcast.103), kind=kLoop, calls=%fused_computation.60 | loop fusion | flops 2408448 | bytes 2408448 | tf_op jit(solution)/shard_map/concatenate | solution.py:33
  144.8 3.9 %collective-permute-done.4 = bf16[1,2,150528]{2,1,0:T(2,128)(2,1)S(1)} collective-permute-done((bf16[1,2,150528]{2,1,0:T(2,128)(2,1)S(1)}, bf16[1,2,150528]{2,1,0:T(2,128)(2,1)S(1)}, u32[]{:S(2)}, u32[]{:S(2)}) %collective-permute-start.4) | collective-permute-done | bytes 602144 | tf_op jit(solution)/shard_map/ppermute | solution.py:31
  148.7 1.5 collective-permute-done.5
  150.2 4.6 %fusion.36 = f32[1,2,150528]{2,1,0:T(2,128)} fusion(f32[1,6,150528]{2,1,0:T(8,128)S(1)} %convolution_bitcast_fusion, bf16[1,2,150528]{2,1,0:T(2,128)(2,1)S(1)} %collective-permute-done.5, bf16[1,4,150528]{2,1,0:T(4,128)(2,1)S(1)} %maximum_bitcast_fusion, bf16[1,2,150528]{2,1,0:T(2,128)(2,1)S(1)} %collective-permute-done.4), kind=kLoop, calls=%fused_computation.57 | loop fusion | flops 4214784 | bytes 4816896 | tf_op jit(solution)/shard_map/add | solution.py:191
  154.8 0.0 copy-done.1
  (9 shorter events, 0.1 us)
Async XLA Ops:
  0.0 90.1 %copy-start = (bf16[1,768,768]{2,1,0:T(8,128)(2,1)S(1)}, bf16[1,768,768]{2,1,0:T(8,128)(2,1)}, u32[]{:S(2)}) copy-start(bf16[1,768,768]{2,1,0:T(8,128)(2,1)} %param.12) | copy-start | bytes 3538948
  0.0 46.3 %copy-start.7 = (bf16[2,196,1024]{2,0,1:T(2,128)(2,1)S(1)}, bf16[2,196,1024]{2,0,1:T(2,128)(2,1)}, u32[]{:S(2)}) copy-start(bf16[2,196,1024]{2,0,1:T(2,128)(2,1)} %param.8) | copy-start | bytes 2408452
  1.8 40.9 %all-to-all-start = ((bf16[128,8,384]{2,1,0:T(8,128)(2,1)}), bf16[128,8,384]{2,1,0:T(8,128)(2,1)}, u32[]{:S(2)}, u32[]{:S(2)}) async-start(bf16[128,8,384]{2,1,0:T(8,128)(2,1)} %broadcast_in_dim.3), calls=%async_computation | async-start | bytes 1572864 | tf_op jit(solution)/shard_map/all_to_all | solution.py:40
  18.6 39.5 %collective-permute-start = (bf16[2,200704]{1,0:T(2,128)(2,1)}, bf16[2,200704]{1,0:T(2,128)(2,1)}, u32[]{:S(2)}, u32[]{:S(2)}) collective-permute-start(bf16[2,200704]{1,0:T(2,128)(2,1)} %bitcast.106), channel_id=1, source_target_pairs={{128,129},{129,130},{130,131},{131,132},{132,133},{133,134},{134,1... | collective-permute-start | bytes 2408456 | tf_op jit(solution)/shard_map/ppermute | solution.py:31
  21.0 38.8 %collective-permute-start.1 = (bf16[2,200704]{1,0:T(2,128)(2,1)}, bf16[2,200704]{1,0:T(2,128)(2,1)}, u32[]{:S(2)}, u32[]{:S(2)}) collective-permute-start(bf16[2,200704]{1,0:T(2,128)(2,1)} %bitcast.107), channel_id=1, source_target_pairs={{129,128},{130,129},{131,130},{132,131},{133,132},{134,133},{135,1... | collective-permute-start | bytes 2408456 | tf_op jit(solution)/shard_map/ppermute | solution.py:32
  42.7 26.2 %collective-permute-start.2 = (bf16[1024,384]{1,0:T(8,128)(2,1)}, bf16[1024,384]{1,0:T(8,128)(2,1)}, u32[]{:S(2)}, u32[]{:S(2)}) collective-permute-start(bf16[1024,384]{1,0:T(8,128)(2,1)} %bitcast.3), channel_id=1, source_target_pairs={{0,128},{128,0},{1,129},{129,1},{2,130},{130,2},{3,131},{131,3},{4... | collective-permute-start | bytes 2359304 | tf_op jit(solution)/shard_map/ppermute | solution.py:41
  52.3 4.4 %copy-start.6 = (bf16[1,768,768]{2,1,0:T(8,128)(2,1)S(1)}, bf16[1,768,768]{2,1,0:T(8,128)(2,1)}, u32[]{:S(2)}) copy-start(bf16[1,768,768]{2,1,0:T(8,128)(2,1)} %param.13) | copy-start | bytes 3538948
  52.3 5.8 %copy-start.8 = (s32[4,2]{0,1:T(2,128)S(1)}, s32[4,2]{0,1:T(2,128)}, u32[]{:S(2)}) copy-start(s32[4,2]{0,1:T(2,128)} %param.9) | copy-start | bytes 100
  83.4 5.3 %copy-start.5 = (bf16[3,4,12,196,64]{3,4,2,0,1:T(8,128)(2,1)}, bf16[3,4,12,196,64]{3,4,2,0,1:T(8,128)(2,1)S(1)}, u32[]{:S(2)}) copy-start(bf16[3,4,12,196,64]{3,4,2,0,1:T(8,128)(2,1)S(1)} %convert_bitcast_fusion) | copy-start | bytes 10838020
  83.4 5.3 %copy-start.2 = (bf16[4,196,768]{2,1,0:T(8,128)(2,1)S(1)}, bf16[4,196,768]{2,1,0:T(8,128)(2,1)}, u32[]{:S(2)}) copy-start(bf16[4,196,768]{2,1,0:T(8,128)(2,1)} %reshape.201) | copy-start | bytes 3612676
  90.1 10.8 %collective-permute-start.3 = (bf16[4,196,768]{2,0,1:T(4,128)(2,1)}, bf16[4,196,768]{2,0,1:T(4,128)(2,1)S(1)}, u32[]{:S(2)}, u32[]{:S(2)}) collective-permute-start(bf16[4,196,768]{2,0,1:T(4,128)(2,1)} %copy.51), channel_id=1, source_target_pairs={{0,128},{128,0},{1,129},{129,1},{2,130},{130,2},{3,131},{131,3},{4... | collective-permute-start | bytes 3612680 | tf_op jit(solution)/shard_map/ppermute | solution.py:50
  101.4 2.3 %copy-start.4 = (bf16[1,768,1536]{1,2,0:T(8,128)(2,1)S(1)}, bf16[1,768,1536]{1,2,0:T(8,128)(2,1)}, u32[]{:S(2)}) copy-start(bf16[1,768,1536]{1,2,0:T(8,128)(2,1)} %copy.56) | copy-start | bytes 7077892
  103.8 4.1 %copy-start.3 = (bf16[1,768,768]{1,2,0:T(8,128)(2,1)S(1)}, bf16[1,768,768]{1,2,0:T(8,128)(2,1)}, u32[]{:S(2)}) copy-start(bf16[1,768,768]{1,2,0:T(8,128)(2,1)} %copy.50) | copy-start | bytes 3538948
  132.5 16.2 %collective-permute-start.4 = (bf16[1,2,150528]{2,1,0:T(2,128)(2,1)S(1)}, bf16[1,2,150528]{2,1,0:T(2,128)(2,1)S(1)}, u32[]{:S(2)}, u32[]{:S(2)}) collective-permute-start(bf16[1,2,150528]{2,1,0:T(2,128)(2,1)S(1)} %get-tuple-element.7), channel_id=1, source_target_pairs={{128,129},{129,130},{130,131},{131,132},{132,133},{133,134},{134,1... | collective-permute-start | bytes 1806344 | tf_op jit(solution)/shard_map/ppermute | solution.py:31
  134.7 15.5 %collective-permute-start.5 = (bf16[1,2,150528]{2,1,0:T(2,128)(2,1)S(1)}, bf16[1,2,150528]{2,1,0:T(2,128)(2,1)S(1)}, u32[]{:S(2)}, u32[]{:S(2)}) collective-permute-start(bf16[1,2,150528]{2,1,0:T(2,128)(2,1)S(1)} %get-tuple-element.8), channel_id=1, source_target_pairs={{129,128},{130,129},{131,130},{132,131},{133,132},{134,133},{135,1... | collective-permute-start | bytes 1806344 | tf_op jit(solution)/shard_map/ppermute | solution.py:32
  143.3 11.5 %copy-start.1 = (bf16[1,768,768]{2,1,0:T(8,128)(2,1)S(1)}, bf16[1,768,768]{2,1,0:T(8,128)(2,1)}, u32[]{:S(2)}) copy-start(bf16[1,768,768]{2,1,0:T(8,128)(2,1)} %param.12) | copy-start | bytes 3538948

commit v5 on v1

--- a/solution.py
+++ b/solution.py
@@ -165,7 +165,7 @@
     rim_rows = jnp.concatenate(
         [contributions[:, :img_local], contributions[:, 2 * img_local :]], axis=1
     )
-    extended = branch_one_padded(rim_rows, 1, img_local)
+    extended = branch_one_padded(rim_rows.astype(jnp.bfloat16), 1, img_local).astype(jnp.float32)
     image_sums = (
         contributions[:, img_local : 2 * img_local]
         + extended[:, :img_local]

time: 152 us -> 147 us (0.967)
  waiting for transfers between devices: 31.1 us -> 23.4 us
  other arithmetic: 9.56 us -> 12.3 us
    ppermute x2, waiting for transfers between devices: 16 us -> 8.52 us  [branch_one_padded(): before = lax.ppermute(last, ('branch', 'pair'), up)]
    add x1, other arithmetic: 2.01 us -> 4.61 us  [body(): contributions[:, img_local:2 * img_local] + extended[:, :img_local]]
    unnamed x27 -> x29, local copies, waits for them, and re-layouts: 2.64 us -> 3.36 us
  transfers between devices with their start and end apart: 7 -> 7, of which waited for: 4 -> 4; matrix products, arithmetic and copies ran while one was open for 13% -> 14% of each run, Pallas kernels for 0% -> 0%
where the time goes in v5:
time: 147 us
  starting transfers between devices  41.9 us (29%)
  matrix products  35.1 us (24%)
  local copies, waits for them, and re-layouts  33.9 us (23%)
  waiting for transfers between devices  23.4 us (16%)
  other arithmetic  12.3 us (8%)
    ppermute x2, starting transfers between devices, branch_one_padded(): after = lax.ppermute(initial, ('branch', 'pair'), down)  17.1 us
    all_to_all x1, starting transfers between devices, gathered_weight(): got = lax.all_to_all(spread, 'pair', 0, 0, tiled=True).reshape(-1, half)  16.8 us
    all_to_all x1, waiting for transfers between devices, gathered_weight(): got = lax.all_to_all(spread, 'pair', 0, 0, tiled=True).reshape(-1, half)  13.4 us
    dot_general x5, matrix products, project(): result = jnp.dot(flattened, matrix, preferred_element_type=jnp.float32)  11.7 us
    ppermute x2, waiting for transfers between devices, branch_one_padded(): before = lax.ppermute(last, ('branch', 'pair'), up)  8.52 us
    dot_general x2, matrix products, attend(): jnp.einsum('bqhd,bkhd->bhqk', query_heads, key_heads, preferred_element_t...  5.75 us
    dot_general x1, matrix products, select_rows(): jnp.dot(onehot.astype(jnp.bfloat16), window, preferred_element_type=jnp.f...  5.59 us
    reshape x2, local copies, waits for them, and re-layouts, embed_picked(): return embedded_rows.reshape(pair_count, tokens_per, model_width)  5.14 us
  transfers between devices with their start and end apart: 7, of which 4 were waited for; matrix products, arithmetic and copies ran while one was open for 14% of the time, Pallas kernels for 0%

profile of v5, /device:TPU:1, one launch (start us, length us, event | category | flops | bytes accessed | tf_op | source)
XLA Modules:
  0.0 146.8 jit_solution(4174409460705207238)
XLA Ops:
  0.0 0.0 copy-start
  0.0 0.9 constant_dynamic-slice_fusion
  0.9 0.9 broadcast_in_dim.2
  1.8 16.8 %all-to-all-start = ((bf16[128,8,384]{2,1,0:T(8,128)(2,1)}), bf16[128,8,384]{2,1,0:T(8,128)(2,1)}, u32[]{:S(2)}, u32[]{:S(2)}) async-start(bf16[128,8,384]{2,1,0:T(8,128)(2,1)} %broadcast_in_dim.2), calls=%async_computation | async-start | bytes 1572864 | tf_op jit(solution)/shard_map/all_to_all | solution.py:40
  18.6 2.4 %collective-permute-start = (bf16[2,200704]{1,0:T(2,128)(2,1)}, bf16[2,200704]{1,0:T(2,128)(2,1)}, u32[]{:S(2)}, u32[]{:S(2)}) collective-permute-start(bf16[2,200704]{1,0:T(2,128)(2,1)} %bitcast.71), channel_id=1, source_target_pairs={{128,129},{129,130},{130,131},{131,132},{132,133},{133,134},{134,1... | collective-permute-start | bytes 2408456 | tf_op jit(solution)/shard_map/ppermute | solution.py:31
  21.0 8.3 %collective-permute-start.1 = (bf16[2,200704]{1,0:T(2,128)(2,1)}, bf16[2,200704]{1,0:T(2,128)(2,1)}, u32[]{:S(2)}, u32[]{:S(2)}) collective-permute-start(bf16[2,200704]{1,0:T(2,128)(2,1)} %bitcast.72), channel_id=1, source_target_pairs={{129,128},{130,129},{131,130},{132,131},{133,132},{134,133},{135,1... | collective-permute-start | bytes 2408456 | tf_op jit(solution)/shard_map/ppermute | solution.py:32
  29.3 13.4 %all-to-all-done = bf16[128,8,384]{2,1,0:T(8,128)(2,1)} async-done(((bf16[128,8,384]{2,1,0:T(8,128)(2,1)}), bf16[128,8,384]{2,1,0:T(8,128)(2,1)}, u32[]{:S(2)}, u32[]{:S(2)}) %all-to-all-start) | async-done | bytes 786464 | tf_op jit(solution)/shard_map/all_to_all | solution.py:40
  42.7 3.6 %collective-permute-start.2 = (bf16[1024,384]{1,0:T(8,128)(2,1)}, bf16[1024,384]{1,0:T(8,128)(2,1)}, u32[]{:S(2)}, u32[]{:S(2)}) collective-permute-start(bf16[1024,384]{1,0:T(8,128)(2,1)} %bitcast.3), channel_id=1, source_target_pairs={{0,128},{128,0},{1,129},{129,1},{2,130},{130,2},{3,131},{131,3},{4... | collective-permute-start | bytes 2359304 | tf_op jit(solution)/shard_map/ppermute | solution.py:41
  46.3 0.0 copy-done.10
  46.4 4.4 %collective-permute-done = bf16[2,200704]{1,0:T(2,128)(2,1)} collective-permute-done((bf16[2,200704]{1,0:T(2,128)(2,1)}, bf16[2,200704]{1,0:T(2,128)(2,1)}, u32[]{:S(2)}, u32[]{:S(2)}) %collective-permute-start) | collective-permute-done | bytes 802848 | tf_op jit(solution)/shard_map/ppermute | solution.py:31
  50.7 0.0 collective-permute-done.1
  50.7 5.6 %convolution_convert_fusion = bf16[4,200704]{1,0:T(4,128)(2,1)} fusion(bf16[2,200704]{1,0:T(2,128)(2,1)} %collective-permute-done.1, bf16[2,200704]{1,0:T(2,128)(2,1)} %bitcast.73, bf16[2,200704]{1,0:T(2,128)(2,1)} %collective-permute-done, s32[4]{0:T(128)S(1)} %fusion.39), kind=kOutput, calls=%fused_computation | convolution fusion | flops 17661976 | bytes 4014096 | tf_op jit(solution)/shard_map/dot_general | solution.py:101
  56.3 3.6 %reshape.230 = bf16[784,1024]{1,0:T(8,128)(2,1)} reshape(bf16[4,200704]{1,0:T(4,128)(2,1)} %convolution_convert_fusion) | data formatting | bytes 3211264 | tf_op jit(solution)/shard_map/reshape | solution.py:107
  59.9 0.0 collective-permute-done.2
  59.9 4.8 %convert_reduce_fusion.1 = (f32[784]{0:T(1024)S(1)}, bf16[784,768]{1,0:T(8,128)(2,1)}) fusion(bf16[784,1024]{1,0:T(8,128)(2,1)} %reshape.230, bf16[1024,384]{1,0:T(8,128)(2,1)} %collective-permute-done.2, bf16[1024,384]{1,0:T(8,128)(2,1)} %bitcast.3, pred[]{:T(512)S(6)} %eq.35), kind=kOutput, calls=%fused_computation.21 | convolution fusion | flops 1242008832 | bytes 4385857 | tf_op jit(solution)/shard_map/dot_general | solution.py:108
  64.7 2.3 %reshape.232 = bf16[4,196,768]{2,1,0:T(8,128)(2,1)} reshape(bf16[784,768]{1,0:T(8,128)(2,1)} %get-tuple-element.15) | data formatting | bytes 2408448 | tf_op jit(solution)/shard_map/reshape | solution.py:111
  67.0 1.9 %fusion.16 = f32[784]{0:T(1024)S(1)} fusion(bf16[784,768]{1,0:T(8,128)(2,1)} %get-tuple-element.15, f32[784]{0:T(1024)S(1)} %broadcast_multiply_fusion.2), kind=kLoop, calls=%fused_computation.32 | loop fusion | flops 2407664 | bytes 1210496 | tf_op jit(solution)/shard_map/reduce_sum | solution.py:57
  68.9 0.0 copy-done.2
  68.9 1.4 fusion.17
  70.3 2.2 %dot_general.40 = bf16[4,196,768]{2,1,0:T(8,128)(2,1)} reshape(bf16[784,768]{1,0:T(8,128)(2,1)} %fusion.17) | data formatting | bytes 2408448 | tf_op jit(solution)/shard_map/dot_general | solution.py:64
  72.5 4.8 %convolution_convert_fusion.1 = bf16[4,196,2304]{2,1,0:T(8,128)(2,1)S(1)} fusion(bf16[4,196,768]{2,1,0:T(8,128)(2,1)} %dot_general.40, bf16[1,768,2304]{2,1,0:T(8,128)(2,1)S(1)} %copy-done), kind=kOutput, calls=%fused_computation.8 | convolution fusion | flops 2776338432 | bytes 8355840 | tf_op jit(solution)/shard_map/dot_general | solution.py:64
  77.4 1.9 %fusion.48 = (bf16[4,196,768]{2,1,0:T(8,128)(2,1)}, bf16[4,196,768]{2,1,0:T(8,128)(2,1)}, bf16[4,196,768]{2,1,0:T(8,128)(2,1)}) fusion(bf16[4,196,2304]{2,1,0:T(8,128)(2,1)S(1)} %convolution_convert_fusion.1), kind=kLoop, calls=%fused_computation.87 | loop fusion | bytes 7225344 | tf_op jit(solution)/shard_map/slice | solution.py:90
  79.2 1.6 %copy.78 = bf16[4,196,768]{1,2,0:T(8,128)(2,1)S(1)} copy(bf16[4,196,768]{2,1,0:T(8,128)(2,1)} %get-tuple-element.10) | data formatting | bytes 2408448 | tf_op jit(solution)/shard_map/slice | solution.py:89
  80.9 2.5 %copy.79 = bf16[4,196,768]{1,2,0:T(8,128)(2,1)} copy(bf16[4,196,768]{2,1,0:T(8,128)(2,1)} %get-tuple-element.9) | data formatting | bytes 2408448 | tf_op jit(solution)/shard_map/slice | solution.py:90
  83.4 2.5 %copy.77 = bf16[4,196,768]{1,2,0:T(8,128)(2,1)} copy(bf16[4,196,768]{2,1,0:T(8,128)(2,1)} %get-tuple-element.11) | data formatting | bytes 2408448 | tf_op jit(solution)/shard_map/slice | solution.py:91
  85.9 2.9 %copy.82 = bf16[4,196,768]{2,0,1:T(4,128)(2,1)} copy(bf16[4,196,768]{2,1,0:T(8,128)(2,1)} %reshape.232) | data formatting | bytes 2408448 | tf_op jit(solution)/shard_map/reshape | solution.py:111
  88.8 0.0 collective-permute-start.3
  88.8 2.1 %fusion = (f32[4,12,196]{2,1,0:T(8,128)S(1)}, f32[4,12,196,196]{2,3,1,0:T(8,128)S(1)}) fusion(bf16[4,196,12,64]{1,3,2,0:T(8,128)(2,1)S(1)} %bitcast.63, bf16[4,196,12,64]{1,3,2,0:T(8,128)(2,1)S(1)} %bitcast.64), kind=kOutput, calls=%fused_computation.6 | convolution fusion | flops 239706432 | bytes 9821952 | tf_op jit(solution)/shard_map/bqhd,bkhd->bhqk/dot_general | solution.py:74
  91.0 0.0 copy-start.12
  91.0 2.4 %fusion.20 = bf16[4,12,64,196]{3,2,1,0:T(8,128)(2,1)S(1)} fusion(bf16[4,196,12,64]{1,3,2,0:T(8,128)(2,1)S(1)} %bitcast.68, f32[4,12,196,196]{2,3,1,0:T(8,128)S(1)} %get-tuple-element.17, f32[4,12,196]{2,1,0:T(8,128)S(1)} %get-tuple-element.16), kind=kOutput, calls=%fused_computation.36 | convolution fusion | flops 242161920 | bytes 9821952 | tf_op jit(solution)/shard_map/bhqk,bkhd->bqhd/dot_general | solution.py:79
  93.4 0.0 copy-done.6
  93.4 0.0 copy-done.12
  93.4 1.3 fusion.50
  94.7 0.0 copy-start.13
  94.8 0.4 multiply_reduce_fusion
  95.2 1.0 copy-done.3
  96.2 0.7 copy-done.13
  96.9 2.3 %convolution_convert_fusion.3 = bf16[4,196,768]{2,1,0:T(8,128)(2,1)} fusion(f32[4,196,768]{2,1,0:T(8,128)S(1)} %get-tuple-element.19, f32[4,196]{1,0:T(4,128)S(1)} %add_rsqrt_fusion.1, f32[4,196]{1,0:T(4,128)S(1)} %broadcast_multiply_fusion.1, bf16[1,768,768]{2,1,0:T(8,128)(2,1)S(1)} %copy-done.13), kind=kOutput, calls=%fused_computation.45 | convolution fusion | flops 927252480 | bytes 4798592 | tf_op jit(solution)/shard_map/dot_general | solution.py:64
  99.1 1.6 %copy.89 = bf16[4,196,768]{1,2,0:T(8,128)(2,1)S(1)} copy(bf16[4,196,768]{2,1,0:T(8,128)(2,1)} %convolution_convert_fusion.3) | data formatting | bytes 2408448 | tf_op jit(solution)/shard_map/convert_element_type | solution.py:94
  100.8 0.0 collective-permute-done.3
  100.8 0.5 convert_reduce_fusion
  101.3 1.2 fusion.14
  102.5 0.9 fusion.15
  103.4 0.7 copy-done.11
  104.2 2.1 %convolution_convert_fusion.2 = bf16[4,196,1536]{2,1,0:T(8,128)(2,1)S(1)} fusion(bf16[1,768,1536]{2,1,0:T(8,128)(2,1)S(1)} %copy-done.11, bf16[4,196,768]{2,0,1:T(4,128)(2,1)S(1)} %fusion.15), kind=kOutput, calls=%fused_computation.12 | convolution fusion | flops 1850892288 | bytes 5971968 | tf_op jit(solution)/shard_map/dot_general | solution.py:64
  106.2 1.6 %fusion.49 = (bf16[4,196,768]{2,1,0:T(8,128)(2,1)}, bf16[4,196,768]{2,1,0:T(8,128)(2,1)}) fusion(bf16[4,196,1536]{2,1,0:T(8,128)(2,1)S(1)} %convolution_convert_fusion.2), kind=kLoop, calls=%fused_computation.88 | loop fusion | bytes 4816896 | tf_op jit(solution)/shard_map/slice | solution.py:96
  107.9 2.5 %copy.90 = bf16[4,196,768]{1,2,0:T(8,128)(2,1)} copy(bf16[4,196,768]{2,1,0:T(8,128)(2,1)} %get-tuple-element.12) | data formatting | bytes 2408448 | tf_op jit(solution)/shard_map/slice | solution.py:96
  110.4 2.6 %copy.88 = bf16[4,196,768]{1,2,0:T(8,128)(2,1)} copy(bf16[4,196,768]{2,1,0:T(8,128)(2,1)} %get-tuple-element.13) | data formatting | bytes 2408448 | tf_op jit(solution)/shard_map/slice | solution.py:96
  113.0 3.7 %fusion.1 = (f32[4,12,196]{2,1,0:T(8,128)S(1)}, f32[4,12,196,196]{2,3,1,0:T(8,128)S(1)}) fusion(bf16[4,196,12,64]{1,3,2,0:T(8,128)(2,1)S(1)} %bitcast.62, bf16[4,196,12,64]{1,3,2,0:T(8,128)(2,1)} %bitcast.65), kind=kOutput, calls=%fused_computation.7 | convolution fusion | flops 239706432 | bytes 9821952 | tf_op jit(solution)/shard_map/bqhd,bkhd->bhqk/dot_general | solution.py:74
  116.6 0.0 copy-start.9
  116.6 2.4 %fusion.19 = bf16[4,12,64,196]{3,2,1,0:T(8,128)(2,1)S(1)} fusion(bf16[4,196,12,64]{1,3,2,0:T(8,128)(2,1)S(1)} %bitcast.69, f32[4,12,196,196]{2,3,1,0:T(8,128)S(1)} %get-tuple-element.21, f32[4,12,196]{2,1,0:T(8,128)S(1)} %get-tuple-element.20), kind=kOutput, calls=%fused_computation.35 | convolution fusion | flops 242161920 | bytes 9821952 | tf_op jit(solution)/shard_map/bhqk,bkhd->bqhd/dot_general | solution.py:79
  119.1 0.0 copy-done.4
  119.1 0.0 copy-done.9
  119.1 1.2 add_bitcast_fusion
  120.3 0.9 copy.98
  121.3 2.4 %convolution_bitcast_fusion = f32[1,6,150528]{2,1,0:T(8,128)S(1)} fusion(f32[4,150528]{1,0:T(4,128)S(1)} %bitcast.61, s32[4]{0:T(128)S(1)} %get-tuple-element.5), kind=kOutput, calls=%fused_computation.1 | convolution fusion | flops 43352088 | bytes 6021136 | tf_op jit(solution)/shard_map/dot_general | solution.py:158
  123.7 0.9 fusion.47
  124.6 1.9 %collective-permute-start.4 = (bf16[1,2,150528]{2,1,0:T(2,128)(2,1)S(1)}, bf16[1,2,150528]{2,1,0:T(2,128)(2,1)S(1)}, u32[]{:S(2)}, u32[]{:S(2)}) collective-permute-start(bf16[1,2,150528]{2,1,0:T(2,128)(2,1)S(1)} %get-tuple-element.7), channel_id=1, source_target_pairs={{128,129},{129,130},{130,131},{131,132},{132,133},{133,134},{134,1... | collective-permute-start | bytes 1806344 | tf_op jit(solution)/shard_map/ppermute | solution.py:31
  126.5 8.8 %collective-permute-start.5 = (bf16[1,2,150528]{2,1,0:T(2,128)(2,1)S(1)}, bf16[1,2,150528]{2,1,0:T(2,128)(2,1)S(1)}, u32[]{:S(2)}, u32[]{:S(2)}) collective-permute-start(bf16[1,2,150528]{2,1,0:T(2,128)(2,1)S(1)} %get-tuple-element.8), channel_id=1, source_target_pairs={{129,128},{130,129},{131,130},{132,131},{133,132},{134,133},{135,1... | collective-permute-start | bytes 1806344 | tf_op jit(solution)/shard_map/ppermute | solution.py:32
  135.3 0.0 copy-start.1
  135.3 1.3 maximum_bitcast_fusion
  136.6 4.1 %collective-permute-done.4 = bf16[1,2,150528]{2,1,0:T(2,128)(2,1)S(1)} collective-permute-done((bf16[1,2,150528]{2,1,0:T(2,128)(2,1)S(1)}, bf16[1,2,150528]{2,1,0:T(2,128)(2,1)S(1)}, u32[]{:S(2)}, u32[]{:S(2)}) %collective-permute-start.4) | collective-permute-done | bytes 602144 | tf_op jit(solution)/shard_map/ppermute | solution.py:31
  140.8 1.5 %collective-permute-done.5 = bf16[1,2,150528]{2,1,0:T(2,128)(2,1)S(1)} collective-permute-done((bf16[1,2,150528]{2,1,0:T(2,128)(2,1)S(1)}, bf16[1,2,150528]{2,1,0:T(2,128)(2,1)S(1)}, u32[]{:S(2)}, u32[]{:S(2)}) %collective-permute-start.5) | collective-permute-done | bytes 602144 | tf_op jit(solution)/shard_map/ppermute | solution.py:32
  142.2 4.6 %fusion.32 = f32[1,2,150528]{2,1,0:T(2,128)} fusion(f32[1,6,150528]{2,1,0:T(8,128)S(1)} %convolution_bitcast_fusion, bf16[1,2,150528]{2,1,0:T(2,128)(2,1)S(1)} %collective-permute-done.5, bf16[1,4,150528]{2,1,0:T(4,128)(2,1)S(1)} %maximum_bitcast_fusion, bf16[1,2,150528]{2,1,0:T(2,128)(2,1)S(1)} %collective-permute-done.4), kind=kLoop, calls=%fused_computation.51 | loop fusion | flops 4214784 | bytes 4816896 | tf_op jit(solution)/shard_map/add | solution.py:170
  (22 shorter events, 0.1 us)
Async XLA Ops:
  0.0 72.5 %copy-start = (bf16[1,768,2304]{2,1,0:T(8,128)(2,1)S(1)}, bf16[1,768,2304]{2,1,0:T(8,128)(2,1)}, u32[]{:S(2)}) copy-start(bf16[1,768,2304]{2,1,0:T(8,128)(2,1)} %param.11) | copy-start | bytes 10616836
  0.0 46.3 %copy-start.10 = (s32[4,2]{0,1:T(2,128)S(1)}, s32[4,2]{0,1:T(2,128)}, u32[]{:S(2)}) copy-start(s32[4,2]{0,1:T(2,128)} %param.9) | copy-start | bytes 100
  1.8 40.9 %all-to-all-start = ((bf16[128,8,384]{2,1,0:T(8,128)(2,1)}), bf16[128,8,384]{2,1,0:T(8,128)(2,1)}, u32[]{:S(2)}, u32[]{:S(2)}) async-start(bf16[128,8,384]{2,1,0:T(8,128)(2,1)} %broadcast_in_dim.2), calls=%async_computation | async-start | bytes 1572864 | tf_op jit(solution)/shard_map/all_to_all | solution.py:40
  18.6 32.1 %collective-permute-start = (bf16[2,200704]{1,0:T(2,128)(2,1)}, bf16[2,200704]{1,0:T(2,128)(2,1)}, u32[]{:S(2)}, u32[]{:S(2)}) collective-permute-start(bf16[2,200704]{1,0:T(2,128)(2,1)} %bitcast.71), channel_id=1, source_target_pairs={{128,129},{129,130},{130,131},{131,132},{132,133},{133,134},{134,1... | collective-permute-start | bytes 2408456 | tf_op jit(solution)/shard_map/ppermute | solution.py:31
  21.0 29.7 %collective-permute-start.1 = (bf16[2,200704]{1,0:T(2,128)(2,1)}, bf16[2,200704]{1,0:T(2,128)(2,1)}, u32[]{:S(2)}, u32[]{:S(2)}) collective-permute-start(bf16[2,200704]{1,0:T(2,128)(2,1)} %bitcast.72), channel_id=1, source_target_pairs={{129,128},{130,129},{131,130},{132,131},{133,132},{134,133},{135,1... | collective-permute-start | bytes 2408456 | tf_op jit(solution)/shard_map/ppermute | solution.py:32
  42.7 17.2 %collective-permute-start.2 = (bf16[1024,384]{1,0:T(8,128)(2,1)}, bf16[1024,384]{1,0:T(8,128)(2,1)}, u32[]{:S(2)}, u32[]{:S(2)}) collective-permute-start(bf16[1024,384]{1,0:T(8,128)(2,1)} %bitcast.3), channel_id=1, source_target_pairs={{0,128},{128,0},{1,129},{129,1},{2,130},{130,2},{3,131},{131,3},{4... | collective-permute-start | bytes 2359304 | tf_op jit(solution)/shard_map/ppermute | solution.py:41
  67.0 1.9 %copy-start.2 = (bf16[784,768]{1,0:T(8,128)(2,1)S(1)}, bf16[784,768]{1,0:T(8,128)(2,1)}, u32[]{:S(2)}) copy-start(bf16[784,768]{1,0:T(8,128)(2,1)} %get-tuple-element.15) | copy-start | bytes 3612676
  85.9 2.9 %copy-start.5 = (bf16[4,196,768]{1,2,0:T(8,128)(2,1)S(1)}, bf16[4,196,768]{1,2,0:T(8,128)(2,1)}, u32[]{:S(2)}) copy-start(bf16[4,196,768]{1,2,0:T(8,128)(2,1)} %copy.79) | copy-start | bytes 3612676
  88.8 11.9 %collective-permute-start.3 = (bf16[4,196,768]{2,0,1:T(4,128)(2,1)}, bf16[4,196,768]{2,0,1:T(4,128)(2,1)S(1)}, u32[]{:S(2)}, u32[]{:S(2)}) collective-permute-start(bf16[4,196,768]{2,0,1:T(4,128)(2,1)} %copy.82), channel_id=1, source_target_pairs={{0,128},{128,0},{1,129},{129,1},{2,130},{130,2},{3,131},{131,3},{4... | collective-permute-start | bytes 3612680 | tf_op jit(solution)/shard_map/ppermute | solution.py:50
  88.8 2.1 %copy-start.7 = (bf16[4,196,768]{1,2,0:T(8,128)(2,1)S(1)}, bf16[4,196,768]{1,2,0:T(8,128)(2,1)}, u32[]{:S(2)}) copy-start(bf16[4,196,768]{1,2,0:T(8,128)(2,1)} %copy.77) | copy-start | bytes 3612676
  91.0 2.4 %copy-start.6 = (bf16[4,196,768]{2,1,0:T(8,128)(2,1)S(1)}, bf16[4,196,768]{2,1,0:T(8,128)(2,1)}, u32[]{:S(2)}) copy-start(bf16[4,196,768]{2,1,0:T(8,128)(2,1)} %reshape.232) | copy-start | bytes 3612676
  91.0 2.4 %copy-start.12 = (bf16[1,768,768]{2,1,0:T(8,128)(2,1)S(1)}, bf16[1,768,768]{2,1,0:T(8,128)(2,1)}, u32[]{:S(2)}) copy-start(bf16[1,768,768]{2,1,0:T(8,128)(2,1)} %param.12) | copy-start | bytes 3538948
  94.7 1.5 copy-start.3
  94.7 2.1 %copy-start.13 = (bf16[1,768,768]{2,1,0:T(8,128)(2,1)S(1)}, bf16[1,768,768]{2,1,0:T(8,128)(2,1)}, u32[]{:S(2)}) copy-start(bf16[1,768,768]{2,1,0:T(8,128)(2,1)} %param.13) | copy-start | bytes 3538948
  102.5 1.7 %copy-start.11 = (bf16[1,768,1536]{2,1,0:T(8,128)(2,1)S(1)}, bf16[1,768,1536]{2,1,0:T(8,128)(2,1)}, u32[]{:S(2)}) copy-start(bf16[1,768,1536]{2,1,0:T(8,128)(2,1)} %param.14) | copy-start | bytes 7077892
  112.9 3.7 %copy-start.8 = (bf16[4,196,768]{1,2,0:T(8,128)(2,1)S(1)}, bf16[4,196,768]{1,2,0:T(8,128)(2,1)}, u32[]{:S(2)}) copy-start(bf16[4,196,768]{1,2,0:T(8,128)(2,1)} %copy.88) | copy-start | bytes 3612676
  116.6 2.4 %copy-start.4 = (f32[4,196,768]{2,1,0:T(8,128)S(1)}, f32[4,196,768]{2,1,0:T(8,128)}, u32[]{:S(2)}) copy-start(f32[4,196,768]{2,1,0:T(8,128)} %copy-done.3) | copy-start | bytes 7225348
  116.6 2.4 %copy-start.9 = (bf16[1,768,768]{2,1,0:T(8,128)(2,1)S(1)}, bf16[1,768,768]{2,1,0:T(8,128)(2,1)}, u32[]{:S(2)}) copy-start(bf16[1,768,768]{2,1,0:T(8,128)(2,1)} %param.15) | copy-start | bytes 3538948
  124.6 16.2 %collective-permute-start.4 = (bf16[1,2,150528]{2,1,0:T(2,128)(2,1)S(1)}, bf16[1,2,150528]{2,1,0:T(2,128)(2,1)S(1)}, u32[]{:S(2)}, u32[]{:S(2)}) collective-permute-start(bf16[1,2,150528]{2,1,0:T(2,128)(2,1)S(1)} %get-tuple-element.7), channel_id=1, source_target_pairs={{128,129},{129,130},{130,131},{131,132},{132,133},{133,134},{134,1... | collective-permute-start | bytes 1806344 | tf_op jit(solution)/shard_map/ppermute | solution.py:31
  126.5 15.7 %collective-permute-start.5 = (bf16[1,2,150528]{2,1,0:T(2,128)(2,1)S(1)}, bf16[1,2,150528]{2,1,0:T(2,128)(2,1)S(1)}, u32[]{:S(2)}, u32[]{:S(2)}) collective-permute-start(bf16[1,2,150528]{2,1,0:T(2,128)(2,1)S(1)} %get-tuple-element.8), channel_id=1, source_target_pairs={{129,128},{130,129},{131,130},{132,131},{133,132},{134,133},{135,1... | collective-permute-start | bytes 1806344 | tf_op jit(solution)/shard_map/ppermute | solution.py:32
  135.3 11.5 %copy-start.1 = (bf16[1,768,2304]{2,1,0:T(8,128)(2,1)S(1)}, bf16[1,768,2304]{2,1,0:T(8,128)(2,1)}, u32[]{:S(2)}) copy-start(bf16[1,768,2304]{2,1,0:T(8,128)(2,1)} %param.11) | copy-start | bytes 10616836

commit v6 on v5

--- a/solution.py
+++ b/solution.py
@@ -59,10 +59,7 @@
 
 
 def project(values, matrix):
-    leading = values.shape[:-1]
-    flattened = values.reshape(-1, values.shape[-1])
-    result = jnp.dot(flattened, matrix, preferred_element_type=jnp.float32)
-    return result.reshape(leading + (matrix.shape[-1],))
+    return jnp.einsum("btd,de->bte", values, matrix, preferred_element_type=jnp.float32)
 
 
 def attend(queries, keys_in, values_in):
@@ -98,17 +95,14 @@
 
 
 def select_rows(onehot, window):
-    return jnp.dot(onehot.astype(jnp.bfloat16), window, preferred_element_type=jnp.float32).astype(
-        jnp.bfloat16
-    )
+    return jnp.einsum(
+        "js,std->jtd", onehot.astype(jnp.bfloat16), window, preferred_element_type=jnp.float32
+    ).astype(jnp.bfloat16)
 
 
 def embed_picked(onehot, window, full_embed, pair_count, tokens_per, enc_width, model_width):
-    picked = select_rows(onehot, window).reshape(pair_count * tokens_per, enc_width)
-    embedded_rows = jnp.dot(picked, full_embed, preferred_element_type=jnp.float32).astype(
-        jnp.bfloat16
-    )
-    return embedded_rows.reshape(pair_count, tokens_per, model_width)
+    picked = select_rows(onehot, window)
+    return project(picked, full_embed).astype(jnp.bfloat16)
 
 
 def body(encoder_rows, pair_list, embed_weight, self_qkv, self_out, cross_q, cross_kv, cross_out):
@@ -135,8 +129,7 @@
     other_onehots.append(other_place[:, None] == slot_index[None, :])
     full_embed = gathered_weight(embed_weight, branch_id, devices)
     model_width = full_embed.shape[1]
-    raw_local = encoder_rows.reshape(img_local, tokens_per * enc_width)
-    window = branch_one_padded(raw_local, 0, img_local)
+    window = branch_one_padded(encoder_rows, 0, img_local)
     own_list = [
         embed_picked(
             own_onehots, window, full_embed, pair_count, tokens_per, enc_width, model_width
@@ -155,11 +148,7 @@
     )
     place_onehot = (slot_index[:, None] == own_places[local_view][None, :]).astype(jnp.float32)
     contribution_list = [
-        jnp.dot(
-            place_onehot,
-            decoded.reshape(pair_count, tokens_per * model_width),
-            precision=lax.Precision.HIGHEST,
-        )
+        jnp.einsum("sj,jtd->std", place_onehot, decoded, precision=lax.Precision.HIGHEST)
     ]
     contributions = jnp.stack(contribution_list, axis=0)
     rim_rows = jnp.concatenate(

time: 147 us -> 133 us (0.905)
  local copies, waits for them, and re-layouts: 33.9 us -> 22.7 us
  other arithmetic: 12.3 us -> 9.56 us
    reshape x3 -> x0, local copies, waits for them, and re-layouts: 8.74 us -> none  [the longest x2 5.14 us: embed_picked(): return embedded_rows.reshape(pair_count, tokens_per, model_width)]
    dot_general x1 -> x0, local copies, waits for them, and re-layouts: 2.23 us -> none  [project(): result = jnp.dot(flattened, matrix, preferred_element_type=jnp.float32)]
    dot_general x8, matrix products: 24.6 us -> 22.4 us  [the longest x6 14.5 us: project(): jnp.einsum('btd,de->bte', values, matrix, preferred_element_type=jnp.floa...]
    unnamed x29 -> x26, local copies, waits for them, and re-layouts: 3.36 us -> 1.71 us
    dot_general x2, matrix products: 5.75 us -> 7.27 us  [attend(): jnp.einsum('bqhd,bkhd->bhqk', query_heads, key_heads, preferred_element_t...]
    convert_element_type x0 -> x1, local copies, waits for them, and re-layouts: none -> 1.49 us  [embed_picked(): return project(picked, full_embed).astype(jnp.bfloat16)]
  transfers between devices with their start and end apart: 7 -> 7, of which waited for: 4 -> 4; matrix products, arithmetic and copies ran while one was open for 14% -> 13% of each run, Pallas kernels for 0% -> 0%
where the time goes in v6:
time: 133 us; the launch traced here: 132 us
  starting transfers between devices  41.9 us (32%)
  matrix products  34.2 us (26%)
  waiting for transfers between devices  23.4 us (18%)
  local copies, waits for them, and re-layouts  22.7 us (17%)
  other arithmetic  9.56 us (7%)
    ppermute x2, starting transfers between devices, branch_one_padded(): after = lax.ppermute(initial, ('branch', 'pair'), down)  17.1 us
    all_to_all x1, starting transfers between devices, gathered_weight(): got = lax.all_to_all(spread, 'pair', 0, 0, tiled=True).reshape(-1, half)  16.8 us
    dot_general x6, matrix products, project(): jnp.einsum('btd,de->bte', values, matrix, preferred_element_type=jnp.floa...  14.5 us
    all_to_all x1, waiting for transfers between devices, gathered_weight(): got = lax.all_to_all(spread, 'pair', 0, 0, tiled=True).reshape(-1, half)  13.4 us
    ppermute x2, waiting for transfers between devices, branch_one_padded(): before = lax.ppermute(last, ('branch', 'pair'), up)  8.58 us
    dot_general x2, matrix products, attend(): jnp.einsum('bqhd,bkhd->bhqk', query_heads, key_heads, preferred_element_t...  7.27 us
    add x1, other arithmetic, body(): contributions[:, img_local:2 * img_local] + extended[:, :img_local]  4.7 us
    dot_general x2, matrix products, attend(): jnp.einsum('bhqk,bkhd->bqhd', attn_probs, value_heads, preferred_element_...  4.53 us
  transfers between devices with their start and end apart: 7, of which 4 were waited for; matrix products, arithmetic and copies ran while one was open for 13% of the time, Pallas kernels for 0%

profile of v6, /device:TPU:1, one launch (start us, length us, event | category | flops | bytes accessed | tf_op | source)
XLA Modules:
  0.0 132.1 jit_solution(18184794568220845765)
XLA Ops:
  0.0 0.0 copy-start
  0.0 0.9 constant_dynamic-slice_fusion
  0.9 0.9 broadcast_in_dim.2
  1.8 16.8 %all-to-all-start = ((bf16[128,8,384]{2,1,0:T(8,128)(2,1)}), bf16[128,8,384]{2,1,0:T(8,128)(2,1)}, u32[]{:S(2)}, u32[]{:S(2)}) async-start(bf16[128,8,384]{2,1,0:T(8,128)(2,1)} %broadcast_in_dim.2), calls=%async_computation | async-start | bytes 1572864 | tf_op jit(solution)/shard_map/all_to_all | solution.py:40
  18.6 2.4 %collective-permute-start = (bf16[2,196,1024]{2,0,1:T(2,128)(2,1)}, bf16[2,196,1024]{2,0,1:T(2,128)(2,1)}, u32[]{:S(2)}, u32[]{:S(2)}) collective-permute-start(bf16[2,196,1024]{2,0,1:T(2,128)(2,1)} %param.8), channel_id=1, source_target_pairs={{128,129},{129,130},{130,131},{131,132},{132,133},{133,134},{134,1... | collective-permute-start | bytes 2408456 | tf_op jit(solution)/shard_map/ppermute | solution.py:31
  21.0 8.3 %collective-permute-start.1 = (bf16[2,196,1024]{2,0,1:T(2,128)(2,1)}, bf16[2,196,1024]{2,0,1:T(2,128)(2,1)}, u32[]{:S(2)}, u32[]{:S(2)}) collective-permute-start(bf16[2,196,1024]{2,0,1:T(2,128)(2,1)} %param.8), channel_id=1, source_target_pairs={{129,128},{130,129},{131,130},{132,131},{133,132},{134,133},{135,1... | collective-permute-start | bytes 2408456 | tf_op jit(solution)/shard_map/ppermute | solution.py:32
  29.3 13.4 %all-to-all-done = bf16[128,8,384]{2,1,0:T(8,128)(2,1)} async-done(((bf16[128,8,384]{2,1,0:T(8,128)(2,1)}), bf16[128,8,384]{2,1,0:T(8,128)(2,1)}, u32[]{:S(2)}, u32[]{:S(2)}) %all-to-all-start) | async-done | bytes 786464 | tf_op jit(solution)/shard_map/all_to_all | solution.py:40
  42.7 3.6 %collective-permute-start.2 = (bf16[1024,384]{1,0:T(8,128)(2,1)}, bf16[1024,384]{1,0:T(8,128)(2,1)}, u32[]{:S(2)}, u32[]{:S(2)}) collective-permute-start(bf16[1024,384]{1,0:T(8,128)(2,1)} %bitcast.4), channel_id=1, source_target_pairs={{0,128},{128,0},{1,129},{129,1},{2,130},{130,2},{3,131},{131,3},{4... | collective-permute-start | bytes 2359304 | tf_op jit(solution)/shard_map/ppermute | solution.py:41
  46.3 0.0 copy-done.9
  46.4 4.4 %collective-permute-done = bf16[2,196,1024]{2,0,1:T(2,128)(2,1)} collective-permute-done((bf16[2,196,1024]{2,0,1:T(2,128)(2,1)}, bf16[2,196,1024]{2,0,1:T(2,128)(2,1)}, u32[]{:S(2)}, u32[]{:S(2)}) %collective-permute-start) | collective-permute-done | bytes 802848 | tf_op jit(solution)/shard_map/ppermute | solution.py:31
  50.7 0.0 collective-permute-done.1
  50.7 4.4 %fusion.25 = bf16[4,196,1024]{2,0,1:T(4,128)(2,1)S(1)} fusion(bf16[2,196,1024]{2,0,1:T(2,128)(2,1)} %collective-permute-done.1, bf16[2,196,1024]{2,0,1:T(2,128)(2,1)} %param.8, bf16[2,196,1024]{2,0,1:T(2,128)(2,1)} %collective-permute-done, s32[4]{0:T(128)S(1)} %fusion.62), kind=kOutput, calls=%fused_computation.36 | convolution fusion | flops 17661976 | bytes 4014096 | tf_op jit(solution)/shard_map/js,std->jtd/dot_general | solution.py:98
  55.2 0.0 collective-permute-done.2
  55.2 4.1 %convert_reduce_fusion = (f32[4,196]{1,0:T(4,128)S(1)}, bf16[4,196,768]{2,1,0:T(8,128)(2,1)S(1)}) fusion(bf16[1024,384]{1,0:T(8,128)(2,1)} %collective-permute-done.2, bf16[1024,384]{1,0:T(8,128)(2,1)} %bitcast.4, pred[]{:T(512)S(6)} %eq.35, bf16[4,196,1024]{2,0,1:T(4,128)(2,1)S(1)} %fusion.25), kind=kOutput, calls=%fused_computation.11 | convolution fusion | flops 1242008832 | bytes 4385857 | tf_op jit(solution)/shard_map/btd,de->bte/dot_general | solution.py:62
  59.3 1.5 %copy.69 = bf16[4,196,768]{2,0,1:T(4,128)(2,1)} copy(bf16[4,196,768]{2,1,0:T(8,128)(2,1)S(1)} %get-tuple-element.15) | data formatting | bytes 2408448 | tf_op jit(solution)/shard_map/convert_element_type | solution.py:105
  60.8 0.5 fusion.15
  61.3 0.0 copy-done
  61.3 3.4 %convolution_convert_fusion = bf16[4,196,2304]{2,1,0:T(8,128)(2,1)S(1)} fusion(bf16[1,768,2304]{2,1,0:T(8,128)(2,1)S(1)} %copy-done, bf16[4,196,768]{2,1,0:T(8,128)(2,1)S(1)} %get-tuple-element.15, f32[4,196]{1,0:T(4,128)S(1)} %add_rsqrt_fusion.2, f32[4,196]{1,0:T(4,128)S(1)} %broadcast_multiply_fusion.2), kind=kOutput, calls=%fused_computation.6 | convolution fusion | flops 2778746880 | bytes 8362112 | tf_op jit(solution)/shard_map/btd,de->bte/dot_general | solution.py:62
  64.8 0.0 copy-done.4
  64.8 1.9 %fusion.71 = (bf16[4,196,768]{2,1,0:T(8,128)(2,1)}, bf16[4,196,768]{2,1,0:T(8,128)(2,1)}, bf16[4,196,768]{2,1,0:T(8,128)(2,1)}) fusion(bf16[4,196,2304]{2,1,0:T(8,128)(2,1)S(1)} %convolution_convert_fusion), kind=kLoop, calls=%fused_computation.96 | loop fusion | bytes 7225344 | tf_op jit(solution)/shard_map/slice | solution.py:87
  66.6 1.6 %copy.66 = bf16[4,196,768]{1,2,0:T(8,128)(2,1)S(1)} copy(bf16[4,196,768]{2,1,0:T(8,128)(2,1)} %get-tuple-element.9) | data formatting | bytes 2408448 | tf_op jit(solution)/shard_map/slice | solution.py:87
  68.3 2.5 %copy.65 = bf16[4,196,768]{1,2,0:T(8,128)(2,1)} copy(bf16[4,196,768]{2,1,0:T(8,128)(2,1)} %get-tuple-element.10) | data formatting | bytes 2408448 | tf_op jit(solution)/shard_map/slice | solution.py:86
  70.8 2.5 %copy.64 = bf16[4,196,768]{1,2,0:T(8,128)(2,1)} copy(bf16[4,196,768]{2,1,0:T(8,128)(2,1)} %get-tuple-element.11) | data formatting | bytes 2408448 | tf_op jit(solution)/shard_map/slice | solution.py:88
  73.3 0.0 collective-permute-start.3
  73.3 3.6 %fusion = (f32[4,12,196]{2,1,0:T(8,128)S(1)}, f32[4,12,196,196]{2,3,1,0:T(8,128)S(1)}) fusion(bf16[4,196,12,64]{1,3,2,0:T(8,128)(2,1)} %bitcast.68, bf16[4,196,12,64]{1,3,2,0:T(8,128)(2,1)S(1)} %bitcast.67), kind=kOutput, calls=%fused_computation.4 | convolution fusion | flops 239706432 | bytes 9821952 | tf_op jit(solution)/shard_map/bqhd,bkhd->bhqk/dot_general | solution.py:71
  77.0 0.0 copy-done.6
  77.0 0.0 copy-start.5
  77.0 0.0 copy-start.11
  77.0 2.2 %fusion.29 = bf16[4,12,64,196]{3,2,1,0:T(8,128)(2,1)S(1)} fusion(bf16[4,196,12,64]{1,3,2,0:T(8,128)(2,1)S(1)} %bitcast.72, f32[4,12,196,196]{2,3,1,0:T(8,128)S(1)} %get-tuple-element.17, f32[4,12,196]{2,1,0:T(8,128)S(1)} %get-tuple-element.16), kind=kOutput, calls=%fused_computation.39 | convolution fusion | flops 242161920 | bytes 9821952 | tf_op jit(solution)/shard_map/bhqk,bkhd->bqhd/dot_general | solution.py:76
  79.2 0.0 copy-done.5
  79.2 0.0 copy-done.11
  79.2 1.3 %fusion.73 = (f32[4,196]{1,0:T(4,128)S(1)}, f32[4,196,768]{2,1,0:T(8,128)S(1)}) fusion(bf16[4,196,768]{1,2,0:T(8,128)(2,1)S(1)} %bitcast.75, bf16[1,768,768]{2,1,0:T(8,128)(2,1)S(1)} %copy-done.11, bf16[4,196,768]{2,1,0:T(8,128)(2,1)S(1)} %copy-done.5), kind=kOutput, calls=%fused_computation.98 | convolution fusion | flops 926649600 | bytes 5999680 | tf_op jit(solution)/shard_map/btd,de->bte/dot_general | solution.py:62
  80.5 0.0 copy-start.12
  80.6 0.4 multiply_reduce_fusion
  81.0 1.0 copy-done.2
  82.0 0.7 copy-done.12
  82.7 2.3 %convolution_convert_fusion.2 = bf16[4,196,768]{2,1,0:T(8,128)(2,1)} fusion(f32[4,196,768]{2,1,0:T(8,128)S(1)} %get-tuple-element.19, f32[4,196]{1,0:T(4,128)S(1)} %add_rsqrt_fusion.1, f32[4,196]{1,0:T(4,128)S(1)} %broadcast_multiply_fusion.1, bf16[1,768,768]{2,1,0:T(8,128)(2,1)S(1)} %copy-done.12), kind=kOutput, calls=%fused_computation.51 | convolution fusion | flops 927252480 | bytes 4798592 | tf_op jit(solution)/shard_map/btd,de->bte/dot_general | solution.py:62
  84.9 1.6 %copy.76 = bf16[4,196,768]{1,2,0:T(8,128)(2,1)S(1)} copy(bf16[4,196,768]{2,1,0:T(8,128)(2,1)} %convolution_convert_fusion.2) | data formatting | bytes 2408448 | tf_op jit(solution)/shard_map/convert_element_type | solution.py:91
  86.6 0.0 collective-permute-done.3
  86.6 0.5 convert_reduce_fusion.1
  87.1 0.0 copy-start.10
  87.2 1.2 fusion.17
  88.3 0.9 fusion.18
  89.2 0.0 copy-done.10
  89.3 2.1 %convolution_convert_fusion.1 = bf16[4,196,1536]{2,1,0:T(8,128)(2,1)S(1)} fusion(bf16[1,768,1536]{2,1,0:T(8,128)(2,1)S(1)} %copy-done.10, bf16[4,196,768]{2,0,1:T(4,128)(2,1)S(1)} %fusion.18), kind=kOutput, calls=%fused_computation.13 | convolution fusion | flops 1850892288 | bytes 5971968 | tf_op jit(solution)/shard_map/btd,de->bte/dot_general | solution.py:62
  91.3 1.6 %fusion.72 = (bf16[4,196,768]{2,1,0:T(8,128)(2,1)}, bf16[4,196,768]{2,1,0:T(8,128)(2,1)}) fusion(bf16[4,196,1536]{2,1,0:T(8,128)(2,1)S(1)} %convolution_convert_fusion.1), kind=kLoop, calls=%fused_computation.97 | loop fusion | bytes 4816896 | tf_op jit(solution)/shard_map/slice | solution.py:93
  93.0 2.5 %copy.77 = bf16[4,196,768]{1,2,0:T(8,128)(2,1)} copy(bf16[4,196,768]{2,1,0:T(8,128)(2,1)} %get-tuple-element.12) | data formatting | bytes 2408448 | tf_op jit(solution)/shard_map/slice | solution.py:93
  95.5 2.5 %copy.75 = bf16[4,196,768]{1,2,0:T(8,128)(2,1)} copy(bf16[4,196,768]{2,1,0:T(8,128)(2,1)} %get-tuple-element.13) | data formatting | bytes 2408448 | tf_op jit(solution)/shard_map/slice | solution.py:93
  98.0 3.6 %fusion.1 = (f32[4,12,196]{2,1,0:T(8,128)S(1)}, f32[4,12,196,196]{2,3,1,0:T(8,128)S(1)}) fusion(bf16[4,196,12,64]{1,3,2,0:T(8,128)(2,1)S(1)} %bitcast.66, bf16[4,196,12,64]{1,3,2,0:T(8,128)(2,1)} %bitcast.69), kind=kOutput, calls=%fused_computation.5 | convolution fusion | flops 239706432 | bytes 9821952 | tf_op jit(solution)/shard_map/bqhd,bkhd->bhqk/dot_general | solution.py:71
  101.7 0.0 copy-done.7
  101.7 0.0 copy-start.3
  101.7 0.0 copy-start.8
  101.7 2.4 %fusion.28 = bf16[4,12,64,196]{3,2,1,0:T(8,128)(2,1)S(1)} fusion(bf16[4,196,12,64]{1,3,2,0:T(8,128)(2,1)S(1)} %bitcast.73, f32[4,12,196,196]{2,3,1,0:T(8,128)S(1)} %get-tuple-element.21, f32[4,12,196]{2,1,0:T(8,128)S(1)} %get-tuple-element.20), kind=kOutput, calls=%fused_computation.38 | convolution fusion | flops 242161920 | bytes 9821952 | tf_op jit(solution)/shard_map/bhqk,bkhd->bqhd/dot_general | solution.py:76
  104.1 1.2 convolution_add_fusion
  105.4 3.5 %fusion.22 = f32[1,6,196,768]{3,1,2,0:T(8,128)S(1)} fusion(f32[4,196,768]{2,1,0:T(8,128)S(1)} %convolution_add_fusion, s32[4]{0:T(128)S(1)} %get-tuple-element.5), kind=kOutput, calls=%fused_computation.35 | convolution fusion | flops 43352088 | bytes 6021136 | tf_op jit(solution)/shard_map/sj,jtd->std/dot_general | solution.py:151
  108.9 0.8 fusion.70
  109.7 1.9 %collective-permute-start.4 = (bf16[1,2,196,768]{3,1,2,0:T(2,128)(2,1)S(1)}, bf16[1,2,196,768]{3,1,2,0:T(2,128)(2,1)S(1)}, u32[]{:S(2)}, u32[]{:S(2)}) collective-permute-start(bf16[1,2,196,768]{3,1,2,0:T(2,128)(2,1)S(1)} %get-tuple-element.7), channel_id=1, source_target_pairs={{128,129},{129,130},{130,131},{131,132},{132,133},{133,134},{134,1... | collective-permute-start | bytes 1806344 | tf_op jit(solution)/shard_map/ppermute | solution.py:31
  111.6 8.8 %collective-permute-start.5 = (bf16[1,2,196,768]{3,1,2,0:T(2,128)(2,1)S(1)}, bf16[1,2,196,768]{3,1,2,0:T(2,128)(2,1)S(1)}, u32[]{:S(2)}, u32[]{:S(2)}) collective-permute-start(bf16[1,2,196,768]{3,1,2,0:T(2,128)(2,1)S(1)} %get-tuple-element.8), channel_id=1, source_target_pairs={{129,128},{130,129},{131,130},{132,131},{133,132},{134,133},{135,1... | collective-permute-start | bytes 1806344 | tf_op jit(solution)/shard_map/ppermute | solution.py:32
  120.4 0.0 copy-start.1
  120.5 1.2 maximum_bitcast_fusion
  121.7 4.2 %collective-permute-done.4 = bf16[1,2,196,768]{3,1,2,0:T(2,128)(2,1)S(1)} collective-permute-done((bf16[1,2,196,768]{3,1,2,0:T(2,128)(2,1)S(1)}, bf16[1,2,196,768]{3,1,2,0:T(2,128)(2,1)S(1)}, u32[]{:S(2)}, u32[]{:S(2)}) %collective-permute-start.4) | collective-permute-done | bytes 602144 | tf_op jit(solution)/shard_map/ppermute | solution.py:31
  125.9 1.5 %collective-permute-done.5 = bf16[1,2,196,768]{3,1,2,0:T(2,128)(2,1)S(1)} collective-permute-done((bf16[1,2,196,768]{3,1,2,0:T(2,128)(2,1)S(1)}, bf16[1,2,196,768]{3,1,2,0:T(2,128)(2,1)S(1)}, u32[]{:S(2)}, u32[]{:S(2)}) %collective-permute-start.5) | collective-permute-done | bytes 602144 | tf_op jit(solution)/shard_map/ppermute | solution.py:32
  127.4 4.7 %fusion.51 = f32[1,2,196,768]{3,1,2,0:T(2,128)} fusion(f32[1,6,196,768]{3,1,2,0:T(8,128)S(1)} %fusion.22, bf16[1,2,196,768]{3,1,2,0:T(2,128)(2,1)S(1)} %collective-permute-done.5, bf16[1,4,196,768]{3,1,2,0:T(4,128)(2,1)S(1)} %maximum_bitcast_fusion, bf16[1,2,196,768]{3,1,2,0:T(2,128)(2,1)S(1)} %collective-permute-done.4), kind=kLoop, calls=%fused_computation.58 | loop fusion | flops 4214784 | bytes 4816896 | tf_op jit(solution)/shard_map/add | solution.py:159
  132.1 0.0 copy-done.1
  (15 shorter events, 0.1 us)
Async XLA Ops:
  0.0 61.3 %copy-start = (bf16[1,768,2304]{2,1,0:T(8,128)(2,1)S(1)}, bf16[1,768,2304]{2,1,0:T(8,128)(2,1)}, u32[]{:S(2)}) copy-start(bf16[1,768,2304]{2,1,0:T(8,128)(2,1)} %param.11) | copy-start | bytes 10616836
  0.0 46.3 %copy-start.9 = (s32[4,2]{0,1:T(2,128)S(1)}, s32[4,2]{0,1:T(2,128)}, u32[]{:S(2)}) copy-start(s32[4,2]{0,1:T(2,128)} %param.9) | copy-start | bytes 100
  1.8 40.9 %all-to-all-start = ((bf16[128,8,384]{2,1,0:T(8,128)(2,1)}), bf16[128,8,384]{2,1,0:T(8,128)(2,1)}, u32[]{:S(2)}, u32[]{:S(2)}) async-start(bf16[128,8,384]{2,1,0:T(8,128)(2,1)} %broadcast_in_dim.2), calls=%async_computation | async-start | bytes 1572864 | tf_op jit(solution)/shard_map/all_to_all | solution.py:40
  18.6 32.1 %collective-permute-start = (bf16[2,196,1024]{2,0,1:T(2,128)(2,1)}, bf16[2,196,1024]{2,0,1:T(2,128)(2,1)}, u32[]{:S(2)}, u32[]{:S(2)}) collective-permute-start(bf16[2,196,1024]{2,0,1:T(2,128)(2,1)} %param.8), channel_id=1, source_target_pairs={{128,129},{129,130},{130,131},{131,132},{132,133},{133,134},{134,1... | collective-permute-start | bytes 2408456 | tf_op jit(solution)/shard_map/ppermute | solution.py:31
  21.0 29.7 %collective-permute-start.1 = (bf16[2,196,1024]{2,0,1:T(2,128)(2,1)}, bf16[2,196,1024]{2,0,1:T(2,128)(2,1)}, u32[]{:S(2)}, u32[]{:S(2)}) collective-permute-start(bf16[2,196,1024]{2,0,1:T(2,128)(2,1)} %param.8), channel_id=1, source_target_pairs={{129,128},{130,129},{131,130},{132,131},{133,132},{134,133},{135,1... | collective-permute-start | bytes 2408456 | tf_op jit(solution)/shard_map/ppermute | solution.py:32
  42.7 12.5 %collective-permute-start.2 = (bf16[1024,384]{1,0:T(8,128)(2,1)}, bf16[1024,384]{1,0:T(8,128)(2,1)}, u32[]{:S(2)}, u32[]{:S(2)}) collective-permute-start(bf16[1024,384]{1,0:T(8,128)(2,1)} %bitcast.4), channel_id=1, source_target_pairs={{0,128},{128,0},{1,129},{129,1},{2,130},{130,2},{3,131},{131,3},{4... | collective-permute-start | bytes 2359304 | tf_op jit(solution)/shard_map/ppermute | solution.py:41
  59.3 5.5 %copy-start.4 = (bf16[4,196,768]{2,1,0:T(8,128)(2,1)}, bf16[4,196,768]{2,1,0:T(8,128)(2,1)S(1)}, u32[]{:S(2)}) copy-start(bf16[4,196,768]{2,1,0:T(8,128)(2,1)S(1)} %get-tuple-element.15) | copy-start | bytes 3612676
  73.3 13.3 %collective-permute-start.3 = (bf16[4,196,768]{2,0,1:T(4,128)(2,1)}, bf16[4,196,768]{2,0,1:T(4,128)(2,1)S(1)}, u32[]{:S(2)}, u32[]{:S(2)}) collective-permute-start(bf16[4,196,768]{2,0,1:T(4,128)(2,1)} %copy.69), channel_id=1, source_target_pairs={{0,128},{128,0},{1,129},{129,1},{2,130},{130,2},{3,131},{131,3},{4... | collective-permute-start | bytes 3612680 | tf_op jit(solution)/shard_map/ppermute | solution.py:50
  73.3 3.6 %copy-start.6 = (bf16[4,196,768]{1,2,0:T(8,128)(2,1)S(1)}, bf16[4,196,768]{1,2,0:T(8,128)(2,1)}, u32[]{:S(2)}) copy-start(bf16[4,196,768]{1,2,0:T(8,128)(2,1)} %copy.64) | copy-start | bytes 3612676
  77.0 2.2 %copy-start.5 = (bf16[4,196,768]{2,1,0:T(8,128)(2,1)S(1)}, bf16[4,196,768]{2,1,0:T(8,128)(2,1)}, u32[]{:S(2)}) copy-start(bf16[4,196,768]{2,1,0:T(8,128)(2,1)} %copy-done.4) | copy-start | bytes 3612676
  77.0 2.2 %copy-start.11 = (bf16[1,768,768]{2,1,0:T(8,128)(2,1)S(1)}, bf16[1,768,768]{2,1,0:T(8,128)(2,1)}, u32[]{:S(2)}) copy-start(bf16[1,768,768]{2,1,0:T(8,128)(2,1)} %param.12) | copy-start | bytes 3538948
  80.5 1.4 %copy-start.2 = (f32[4,196,768]{2,1,0:T(8,128)}, f32[4,196,768]{2,1,0:T(8,128)S(1)}, u32[]{:S(2)}) copy-start(f32[4,196,768]{2,1,0:T(8,128)S(1)} %get-tuple-element.19) | copy-start | bytes 7225348
  80.5 2.1 %copy-start.12 = (bf16[1,768,768]{2,1,0:T(8,128)(2,1)S(1)}, bf16[1,768,768]{2,1,0:T(8,128)(2,1)}, u32[]{:S(2)}) copy-start(bf16[1,768,768]{2,1,0:T(8,128)(2,1)} %param.13) | copy-start | bytes 3538948
  87.1 2.1 %copy-start.10 = (bf16[1,768,1536]{2,1,0:T(8,128)(2,1)S(1)}, bf16[1,768,1536]{2,1,0:T(8,128)(2,1)}, u32[]{:S(2)}) copy-start(bf16[1,768,1536]{2,1,0:T(8,128)(2,1)} %param.14) | copy-start | bytes 7077892
  98.0 3.7 %copy-start.7 = (bf16[4,196,768]{1,2,0:T(8,128)(2,1)S(1)}, bf16[4,196,768]{1,2,0:T(8,128)(2,1)}, u32[]{:S(2)}) copy-start(bf16[4,196,768]{1,2,0:T(8,128)(2,1)} %copy.75) | copy-start | bytes 3612676
  101.7 2.4 %copy-start.3 = (f32[4,196,768]{2,1,0:T(8,128)S(1)}, f32[4,196,768]{2,1,0:T(8,128)}, u32[]{:S(2)}) copy-start(f32[4,196,768]{2,1,0:T(8,128)} %copy-done.2) | copy-start | bytes 7225348
  101.7 2.4 %copy-start.8 = (bf16[1,768,768]{2,1,0:T(8,128)(2,1)S(1)}, bf16[1,768,768]{2,1,0:T(8,128)(2,1)}, u32[]{:S(2)}) copy-start(bf16[1,768,768]{2,1,0:T(8,128)(2,1)} %param.15) | copy-start | bytes 3538948
  109.7 16.2 %collective-permute-start.4 = (bf16[1,2,196,768]{3,1,2,0:T(2,128)(2,1)S(1)}, bf16[1,2,196,768]{3,1,2,0:T(2,128)(2,1)S(1)}, u32[]{:S(2)}, u32[]{:S(2)}) collective-permute-start(bf16[1,2,196,768]{3,1,2,0:T(2,128)(2,1)S(1)} %get-tuple-element.7), channel_id=1, source_target_pairs={{128,129},{129,130},{130,131},{131,132},{132,133},{133,134},{134,1... | collective-permute-start | bytes 1806344 | tf_op jit(solution)/shard_map/ppermute | solution.py:31
  111.6 15.7 %collective-permute-start.5 = (bf16[1,2,196,768]{3,1,2,0:T(2,128)(2,1)S(1)}, bf16[1,2,196,768]{3,1,2,0:T(2,128)(2,1)S(1)}, u32[]{:S(2)}, u32[]{:S(2)}) collective-permute-start(bf16[1,2,196,768]{3,1,2,0:T(2,128)(2,1)S(1)} %get-tuple-element.8), channel_id=1, source_target_pairs={{129,128},{130,129},{131,130},{132,131},{133,132},{134,133},{135,1... | collective-permute-start | bytes 1806344 | tf_op jit(solution)/shard_map/ppermute | solution.py:32
  120.4 11.6 %copy-start.1 = (bf16[1,768,2304]{2,1,0:T(8,128)(2,1)S(1)}, bf16[1,768,2304]{2,1,0:T(8,128)(2,1)}, u32[]{:S(2)}) copy-start(bf16[1,768,2304]{2,1,0:T(8,128)(2,1)} %param.11) | copy-start | bytes 10616836

commit v7 on v6

--- a/solution.py
+++ b/solution.py
@@ -146,19 +146,21 @@
         cross_kv[local_view],
         cross_out[local_view],
     )
-    place_onehot = (slot_index[:, None] == own_places[local_view][None, :]).astype(jnp.float32)
-    contribution_list = [
-        jnp.einsum("sj,jtd->std", place_onehot, decoded, precision=lax.Precision.HIGHEST)
-    ]
-    contributions = jnp.stack(contribution_list, axis=0)
-    rim_rows = jnp.concatenate(
-        [contributions[:, :img_local], contributions[:, 2 * img_local :]], axis=1
-    )
-    extended = branch_one_padded(rim_rows.astype(jnp.bfloat16), 1, img_local).astype(jnp.float32)
+    place = own_places[local_view]
+
+    chosen = (slot_index[:, None] == place[None, :]).astype(jnp.float32)
+    contributions = jnp.einsum("sj,jtd->std", chosen, decoded, precision=lax.Precision.HIGHEST)
+
+    def slot_sums(first):
+        return contributions[first : first + img_local]
+
+    peers = lax.axis_size("pair")
+    up = [(peers + i, peers + (i + 1) % peers) for i in range(peers)]
+    down = [(j, i) for i, j in up]
+    from_prev = lax.ppermute(slot_sums(2 * img_local).astype(jnp.bfloat16), ("branch", "pair"), up)
+    from_next = lax.ppermute(slot_sums(0).astype(jnp.bfloat16), ("branch", "pair"), down)
     image_sums = (
-        contributions[:, img_local : 2 * img_local]
-        + extended[:, :img_local]
-        + extended[:, 3 * img_local :]
+        slot_sums(img_local) + from_prev.astype(jnp.float32) + from_next.astype(jnp.float32)
     )
     return image_sums.reshape(views_local, img_local, tokens_per, model_width)
 

time: 133 us -> 130 us (0.977)
  other arithmetic: 9.56 us -> 6.57 us
    ppermute x0 -> x2, starting transfers between devices: none -> 10.8 us  [the longest x1 8.79 us: body(): lax.ppermute(slot_sums(0).astype(jnp.bfloat16), ('branch', 'pair'), down)]
    ppermute x2 -> x1, starting transfers between devices: 17.1 us -> 8.3 us  [branch_one_padded(): after = lax.ppermute(initial, ('branch', 'pair'), down)]
    ppermute x0 -> x2, waiting for transfers between devices: none -> 6.94 us  [the longest x1 5.46 us: body(): lax.ppermute(slot_sums(2 * img_local).astype(jnp.bfloat16), ('branch', 'p...]
    ppermute x2 -> x1, waiting for transfers between devices: 8.58 us -> 3.64 us  [branch_one_padded(): before = lax.ppermute(last, ('branch', 'pair'), up)]
    add x1 -> x0, other arithmetic: 4.7 us -> none  [body(): contributions[:, img_local:2 * img_local] + extended[:, :img_local]]
    reshape x0 -> x1, other arithmetic: none -> 2.2 us  [body(): return image_sums.reshape(views_local, img_local, tokens_per, model_width)]
    ppermute x2 -> x1, starting transfers between devices: 4.34 us -> 2.42 us  [branch_one_padded(): before = lax.ppermute(last, ('branch', 'pair'), up)]
    ppermute x2 -> x1, waiting for transfers between devices: 1.48 us -> 0.01 us  [branch_one_padded(): after = lax.ppermute(initial, ('branch', 'pair'), down)]
where the time goes in v7:
time: 130 us
  starting transfers between devices  42 us (32%)
  matrix products  34.3 us (26%)
  waiting for transfers between devices  23.9 us (18%)
  local copies, waits for them, and re-layouts  22.7 us (17%)
  other arithmetic  6.57 us (5%)
    all_to_all x1, starting transfers between devices, gathered_weight(): got = lax.all_to_all(spread, 'pair', 0, 0, tiled=True).reshape(-1, half)  16.8 us
    dot_general x6, matrix products, project(): jnp.einsum('btd,de->bte', values, matrix, preferred_element_type=jnp.floa...  14.5 us
    all_to_all x1, waiting for transfers between devices, gathered_weight(): got = lax.all_to_all(spread, 'pair', 0, 0, tiled=True).reshape(-1, half)  13.4 us
    ppermute x1, starting transfers between devices, body(): lax.ppermute(slot_sums(0).astype(jnp.bfloat16), ('branch', 'pair'), down)  8.79 us
    ppermute x1, starting transfers between devices, branch_one_padded(): after = lax.ppermute(initial, ('branch', 'pair'), down)  8.3 us
    dot_general x2, matrix products, attend(): jnp.einsum('bqhd,bkhd->bhqk', query_heads, key_heads, preferred_element_t...  7.28 us
    ppermute x1, waiting for transfers between devices, body(): lax.ppermute(slot_sums(2 * img_local).astype(jnp.bfloat16), ('branch', 'p...  5.46 us
    dot_general x2, matrix products, attend(): jnp.einsum('bhqk,bkhd->bqhd', attn_probs, value_heads, preferred_element_...  4.53 us
  transfers between devices with their start and end apart: 7, of which 4 were waited for; matrix products, arithmetic and copies ran while one was open for 13% of the time, Pallas kernels for 0%

profile of v7, /device:TPU:1, one launch (start us, length us, event | category | flops | bytes accessed | tf_op | source)
XLA Modules:
  0.0 129.8 jit_solution(16754326250729663346)
XLA Ops:
  0.0 0.0 copy-start
  0.0 0.8 constant_dynamic-slice_fusion
  0.8 0.9 broadcast_in_dim.2
  1.8 16.8 %all-to-all-start = ((bf16[128,8,384]{2,1,0:T(8,128)(2,1)}), bf16[128,8,384]{2,1,0:T(8,128)(2,1)}, u32[]{:S(2)}, u32[]{:S(2)}) async-start(bf16[128,8,384]{2,1,0:T(8,128)(2,1)} %broadcast_in_dim.2), calls=%async_computation | async-start | bytes 1572864 | tf_op jit(solution)/shard_map/all_to_all | solution.py:40
  18.6 2.4 %collective-permute-start = (bf16[2,196,1024]{2,0,1:T(2,128)(2,1)}, bf16[2,196,1024]{2,0,1:T(2,128)(2,1)}, u32[]{:S(2)}, u32[]{:S(2)}) collective-permute-start(bf16[2,196,1024]{2,0,1:T(2,128)(2,1)} %param.8), channel_id=1, source_target_pairs={{128,129},{129,130},{130,131},{131,132},{132,133},{133,134},{134,1... | collective-permute-start | bytes 2408456 | tf_op jit(solution)/shard_map/ppermute | solution.py:31
  21.0 8.3 %collective-permute-start.1 = (bf16[2,196,1024]{2,0,1:T(2,128)(2,1)}, bf16[2,196,1024]{2,0,1:T(2,128)(2,1)}, u32[]{:S(2)}, u32[]{:S(2)}) collective-permute-start(bf16[2,196,1024]{2,0,1:T(2,128)(2,1)} %param.8), channel_id=1, source_target_pairs={{129,128},{130,129},{131,130},{132,131},{133,132},{134,133},{135,1... | collective-permute-start | bytes 2408456 | tf_op jit(solution)/shard_map/ppermute | solution.py:32
  29.3 13.4 %all-to-all-done = bf16[128,8,384]{2,1,0:T(8,128)(2,1)} async-done(((bf16[128,8,384]{2,1,0:T(8,128)(2,1)}), bf16[128,8,384]{2,1,0:T(8,128)(2,1)}, u32[]{:S(2)}, u32[]{:S(2)}) %all-to-all-start) | async-done | bytes 786464 | tf_op jit(solution)/shard_map/all_to_all | solution.py:40
  42.7 3.6 %collective-permute-start.2 = (bf16[1024,384]{1,0:T(8,128)(2,1)}, bf16[1024,384]{1,0:T(8,128)(2,1)}, u32[]{:S(2)}, u32[]{:S(2)}) collective-permute-start(bf16[1024,384]{1,0:T(8,128)(2,1)} %bitcast.4), channel_id=1, source_target_pairs={{0,128},{128,0},{1,129},{129,1},{2,130},{130,2},{3,131},{131,3},{4... | collective-permute-start | bytes 2359304 | tf_op jit(solution)/shard_map/ppermute | solution.py:41
  46.3 0.8 and_select_fusion.1
  47.1 3.6 %collective-permute-done = bf16[2,196,1024]{2,0,1:T(2,128)(2,1)} collective-permute-done((bf16[2,196,1024]{2,0,1:T(2,128)(2,1)}, bf16[2,196,1024]{2,0,1:T(2,128)(2,1)}, u32[]{:S(2)}, u32[]{:S(2)}) %collective-permute-start) | collective-permute-done | bytes 802848 | tf_op jit(solution)/shard_map/ppermute | solution.py:31
  50.7 0.0 collective-permute-done.1
  50.7 4.4 %fusion.22 = bf16[4,196,1024]{2,0,1:T(4,128)(2,1)S(1)} fusion(bf16[2,196,1024]{2,0,1:T(2,128)(2,1)} %collective-permute-done.1, bf16[2,196,1024]{2,0,1:T(2,128)(2,1)} %param.8, bf16[2,196,1024]{2,0,1:T(2,128)(2,1)} %collective-permute-done, s32[4]{0:T(128)S(1)} %fusion.60), kind=kOutput, calls=%fused_computation.35 | convolution fusion | flops 17661976 | bytes 4014096 | tf_op jit(solution)/shard_map/js,std->jtd/dot_general | solution.py:98
  55.2 0.0 collective-permute-done.2
  55.2 4.1 %convert_reduce_fusion = (f32[4,196]{1,0:T(4,128)S(1)}, bf16[4,196,768]{2,1,0:T(8,128)(2,1)S(1)}) fusion(bf16[1024,384]{1,0:T(8,128)(2,1)} %collective-permute-done.2, bf16[1024,384]{1,0:T(8,128)(2,1)} %bitcast.4, pred[]{:T(512)S(6)} %eq.35, bf16[4,196,1024]{2,0,1:T(4,128)(2,1)S(1)} %fusion.22), kind=kOutput, calls=%fused_computation.11 | convolution fusion | flops 1242008832 | bytes 4385857 | tf_op jit(solution)/shard_map/btd,de->bte/dot_general | solution.py:62
  59.3 1.5 %copy.69 = bf16[4,196,768]{2,0,1:T(4,128)(2,1)} copy(bf16[4,196,768]{2,1,0:T(8,128)(2,1)S(1)} %get-tuple-element.15) | data formatting | bytes 2408448 | tf_op jit(solution)/shard_map/convert_element_type | solution.py:105
  60.8 0.5 fusion.15
  61.3 0.0 copy-done
  61.3 3.4 %convolution_convert_fusion = bf16[4,196,2304]{2,1,0:T(8,128)(2,1)S(1)} fusion(bf16[1,768,2304]{2,1,0:T(8,128)(2,1)S(1)} %copy-done, bf16[4,196,768]{2,1,0:T(8,128)(2,1)S(1)} %get-tuple-element.15, f32[4,196]{1,0:T(4,128)S(1)} %add_rsqrt_fusion.2, f32[4,196]{1,0:T(4,128)S(1)} %broadcast_multiply_fusion.2), kind=kOutput, calls=%fused_computation.6 | convolution fusion | flops 2778746880 | bytes 8362112 | tf_op jit(solution)/shard_map/btd,de->bte/dot_general | solution.py:62
  64.7 0.0 copy-done.4
  64.7 1.9 %fusion.68 = (bf16[4,196,768]{2,1,0:T(8,128)(2,1)}, bf16[4,196,768]{2,1,0:T(8,128)(2,1)}, bf16[4,196,768]{2,1,0:T(8,128)(2,1)}) fusion(bf16[4,196,2304]{2,1,0:T(8,128)(2,1)S(1)} %convolution_convert_fusion), kind=kLoop, calls=%fused_computation.90 | loop fusion | bytes 7225344 | tf_op jit(solution)/shard_map/slice | solution.py:87
  66.6 1.6 %copy.66 = bf16[4,196,768]{1,2,0:T(8,128)(2,1)S(1)} copy(bf16[4,196,768]{2,1,0:T(8,128)(2,1)} %get-tuple-element.7) | data formatting | bytes 2408448 | tf_op jit(solution)/shard_map/slice | solution.py:87
  68.3 2.5 %copy.65 = bf16[4,196,768]{1,2,0:T(8,128)(2,1)} copy(bf16[4,196,768]{2,1,0:T(8,128)(2,1)} %get-tuple-element.8) | data formatting | bytes 2408448 | tf_op jit(solution)/shard_map/slice | solution.py:86
  70.8 2.5 %copy.64 = bf16[4,196,768]{1,2,0:T(8,128)(2,1)} copy(bf16[4,196,768]{2,1,0:T(8,128)(2,1)} %get-tuple-element.9) | data formatting | bytes 2408448 | tf_op jit(solution)/shard_map/slice | solution.py:88
  73.3 0.0 collective-permute-start.3
  73.3 3.6 %fusion = (f32[4,12,196]{2,1,0:T(8,128)S(1)}, f32[4,12,196,196]{2,3,1,0:T(8,128)S(1)}) fusion(bf16[4,196,12,64]{1,3,2,0:T(8,128)(2,1)} %bitcast.66, bf16[4,196,12,64]{1,3,2,0:T(8,128)(2,1)S(1)} %bitcast.65), kind=kOutput, calls=%fused_computation.4 | convolution fusion | flops 239706432 | bytes 9821952 | tf_op jit(solution)/shard_map/bqhd,bkhd->bhqk/dot_general | solution.py:71
  77.0 0.0 copy-done.6
  77.0 0.0 copy-start.5
  77.0 0.0 copy-start.10
  77.0 2.2 %fusion.26 = bf16[4,12,64,196]{3,2,1,0:T(8,128)(2,1)S(1)} fusion(bf16[4,196,12,64]{1,3,2,0:T(8,128)(2,1)S(1)} %bitcast.68, f32[4,12,196,196]{2,3,1,0:T(8,128)S(1)} %get-tuple-element.17, f32[4,12,196]{2,1,0:T(8,128)S(1)} %get-tuple-element.16), kind=kOutput, calls=%fused_computation.38 | convolution fusion | flops 242161920 | bytes 9821952 | tf_op jit(solution)/shard_map/bhqk,bkhd->bqhd/dot_general | solution.py:76
  79.2 0.0 copy-done.5
  79.2 0.0 copy-done.10
  79.2 1.3 %fusion.71 = (f32[4,196]{1,0:T(4,128)S(1)}, f32[4,196,768]{2,1,0:T(8,128)S(1)}) fusion(bf16[4,196,768]{1,2,0:T(8,128)(2,1)S(1)} %bitcast.71, bf16[1,768,768]{2,1,0:T(8,128)(2,1)S(1)} %copy-done.10, bf16[4,196,768]{2,1,0:T(8,128)(2,1)S(1)} %copy-done.5), kind=kOutput, calls=%fused_computation.93 | convolution fusion | flops 926649600 | bytes 5999680 | tf_op jit(solution)/shard_map/btd,de->bte/dot_general | solution.py:62
  80.5 0.0 copy-start.11
  80.6 0.4 multiply_reduce_fusion
  81.0 1.0 copy-done.2
  82.0 0.7 copy-done.11
  82.7 2.3 %convolution_convert_fusion.2 = bf16[4,196,768]{2,1,0:T(8,128)(2,1)} fusion(f32[4,196,768]{2,1,0:T(8,128)S(1)} %get-tuple-element.19, f32[4,196]{1,0:T(4,128)S(1)} %add_rsqrt_fusion.1, f32[4,196]{1,0:T(4,128)S(1)} %broadcast_multiply_fusion.1, bf16[1,768,768]{2,1,0:T(8,128)(2,1)S(1)} %copy-done.11), kind=kOutput, calls=%fused_computation.50 | convolution fusion | flops 927252480 | bytes 4798592 | tf_op jit(solution)/shard_map/btd,de->bte/dot_general | solution.py:62
  84.9 1.6 %copy.76 = bf16[4,196,768]{1,2,0:T(8,128)(2,1)S(1)} copy(bf16[4,196,768]{2,1,0:T(8,128)(2,1)} %convolution_convert_fusion.2) | data formatting | bytes 2408448 | tf_op jit(solution)/shard_map/convert_element_type | solution.py:91
  86.6 0.0 collective-permute-done.3
  86.6 0.5 convert_reduce_fusion.1
  87.1 0.0 copy-start.9
  87.2 1.2 fusion.17
  88.3 0.9 fusion.18
  89.2 0.0 copy-done.9
  89.3 2.1 %convolution_convert_fusion.1 = bf16[4,196,1536]{2,1,0:T(8,128)(2,1)S(1)} fusion(bf16[1,768,1536]{2,1,0:T(8,128)(2,1)S(1)} %copy-done.9, bf16[4,196,768]{2,0,1:T(4,128)(2,1)S(1)} %fusion.18), kind=kOutput, calls=%fused_computation.13 | convolution fusion | flops 1850892288 | bytes 5971968 | tf_op jit(solution)/shard_map/btd,de->bte/dot_general | solution.py:62
  91.3 1.6 %fusion.69 = (bf16[4,196,768]{2,1,0:T(8,128)(2,1)}, bf16[4,196,768]{2,1,0:T(8,128)(2,1)}) fusion(bf16[4,196,1536]{2,1,0:T(8,128)(2,1)S(1)} %convolution_convert_fusion.1), kind=kLoop, calls=%fused_computation.91 | loop fusion | bytes 4816896 | tf_op jit(solution)/shard_map/slice | solution.py:93
  93.0 2.5 %copy.77 = bf16[4,196,768]{1,2,0:T(8,128)(2,1)} copy(bf16[4,196,768]{2,1,0:T(8,128)(2,1)} %get-tuple-element.10) | data formatting | bytes 2408448 | tf_op jit(solution)/shard_map/slice | solution.py:93
  95.5 2.5 %copy.75 = bf16[4,196,768]{1,2,0:T(8,128)(2,1)} copy(bf16[4,196,768]{2,1,0:T(8,128)(2,1)} %get-tuple-element.11) | data formatting | bytes 2408448 | tf_op jit(solution)/shard_map/slice | solution.py:93
  98.0 3.6 %fusion.1 = (f32[4,12,196]{2,1,0:T(8,128)S(1)}, f32[4,12,196,196]{2,3,1,0:T(8,128)S(1)}) fusion(bf16[4,196,12,64]{1,3,2,0:T(8,128)(2,1)S(1)} %bitcast.64, bf16[4,196,12,64]{1,3,2,0:T(8,128)(2,1)} %bitcast.67), kind=kOutput, calls=%fused_computation.5 | convolution fusion | flops 239706432 | bytes 9821952 | tf_op jit(solution)/shard_map/bqhd,bkhd->bhqk/dot_general | solution.py:71
  101.7 0.0 copy-done.7
  101.7 0.0 copy-start.3
  101.7 0.0 copy-start.8
  101.7 2.4 %fusion.25 = bf16[4,12,64,196]{3,2,1,0:T(8,128)(2,1)S(1)} fusion(bf16[4,196,12,64]{1,3,2,0:T(8,128)(2,1)S(1)} %bitcast.69, f32[4,12,196,196]{2,3,1,0:T(8,128)S(1)} %get-tuple-element.21, f32[4,12,196]{2,1,0:T(8,128)S(1)} %get-tuple-element.20), kind=kOutput, calls=%fused_computation.37 | convolution fusion | flops 242161920 | bytes 9821952 | tf_op jit(solution)/shard_map/bhqk,bkhd->bqhd/dot_general | solution.py:76
  104.1 0.0 copy-done.3
  104.1 0.0 copy-done.8
  104.1 1.2 convolution_add_fusion
  105.4 3.6 %fusion.72 = (bf16[6,196,768]{2,0,1:T(8,128)(2,1)S(1)}, f32[6,196,768]{2,0,1:T(8,128)S(1)}) fusion(f32[4,196,768]{2,1,0:T(8,128)S(1)} %convolution_add_fusion, s32[4]{0:T(128)S(1)} %get-tuple-element.5), kind=kOutput, calls=%fused_computation.94 | convolution fusion | flops 44255256 | bytes 7827472 | tf_op jit(solution)/shard_map/sj,jtd->std/dot_general | solution.py:152
  108.9 0.0 copy-start.1
  108.9 0.8 fusion.70
  109.8 2.1 %collective-permute-start.4 = (bf16[2,196,768]{2,0,1:T(2,128)(2,1)S(1)}, bf16[2,196,768]{2,0,1:T(2,128)(2,1)S(1)}, u32[]{:S(2)}, u32[]{:S(2)}) collective-permute-start(bf16[2,196,768]{2,0,1:T(2,128)(2,1)S(1)} %get-tuple-element.12), channel_id=1, source_target_pairs={{128,129},{129,130},{130,131},{131,132},{132,133},{133,134},{134,1... | collective-permute-start | bytes 1806344 | tf_op jit(solution)/shard_map/ppermute | solution.py:160
  111.8 8.8 %collective-permute-start.5 = (bf16[2,196,768]{2,0,1:T(2,128)(2,1)S(1)}, bf16[2,196,768]{2,0,1:T(2,128)(2,1)S(1)}, u32[]{:S(2)}, u32[]{:S(2)}) collective-permute-start(bf16[2,196,768]{2,0,1:T(2,128)(2,1)S(1)} %get-tuple-element.13), channel_id=1, source_target_pairs={{129,128},{130,129},{131,130},{132,131},{133,132},{134,133},{135,1... | collective-permute-start | bytes 1806344 | tf_op jit(solution)/shard_map/ppermute | solution.py:161
  120.6 5.5 %collective-permute-done.4 = bf16[2,196,768]{2,0,1:T(2,128)(2,1)S(1)} collective-permute-done((bf16[2,196,768]{2,0,1:T(2,128)(2,1)S(1)}, bf16[2,196,768]{2,0,1:T(2,128)(2,1)S(1)}, u32[]{:S(2)}, u32[]{:S(2)}) %collective-permute-start.4) | collective-permute-done | bytes 602144 | tf_op jit(solution)/shard_map/ppermute | solution.py:160
  126.1 1.5 %collective-permute-done.5 = bf16[2,196,768]{2,0,1:T(2,128)(2,1)S(1)} collective-permute-done((bf16[2,196,768]{2,0,1:T(2,128)(2,1)S(1)}, bf16[2,196,768]{2,0,1:T(2,128)(2,1)S(1)}, u32[]{:S(2)}, u32[]{:S(2)}) %collective-permute-start.5) | collective-permute-done | bytes 602144 | tf_op jit(solution)/shard_map/ppermute | solution.py:161
  127.6 2.2 %fusion.49 = f32[1,2,196,768]{3,1,2,0:T(2,128)} fusion(f32[6,196,768]{2,0,1:T(8,128)S(1)} %get-tuple-element.23, bf16[2,196,768]{2,0,1:T(2,128)(2,1)S(1)} %collective-permute-done.5, bf16[2,196,768]{2,0,1:T(2,128)(2,1)S(1)} %collective-permute-done.4), kind=kLoop, calls=%fused_computation.58 | loop fusion | flops 1204224 | bytes 3612672 | tf_op jit(solution)/shard_map/reshape | solution.py:165
  (12 shorter events, 0.1 us)
Async XLA Ops:
  0.0 61.3 %copy-start = (bf16[1,768,2304]{2,1,0:T(8,128)(2,1)S(1)}, bf16[1,768,2304]{2,1,0:T(8,128)(2,1)}, u32[]{:S(2)}) copy-start(bf16[1,768,2304]{2,1,0:T(8,128)(2,1)} %param.11) | copy-start | bytes 10616836
  1.8 40.9 %all-to-all-start = ((bf16[128,8,384]{2,1,0:T(8,128)(2,1)}), bf16[128,8,384]{2,1,0:T(8,128)(2,1)}, u32[]{:S(2)}, u32[]{:S(2)}) async-start(bf16[128,8,384]{2,1,0:T(8,128)(2,1)} %broadcast_in_dim.2), calls=%async_computation | async-start | bytes 1572864 | tf_op jit(solution)/shard_map/all_to_all | solution.py:40
  18.6 32.1 %collective-permute-start = (bf16[2,196,1024]{2,0,1:T(2,128)(2,1)}, bf16[2,196,1024]{2,0,1:T(2,128)(2,1)}, u32[]{:S(2)}, u32[]{:S(2)}) collective-permute-start(bf16[2,196,1024]{2,0,1:T(2,128)(2,1)} %param.8), channel_id=1, source_target_pairs={{128,129},{129,130},{130,131},{131,132},{132,133},{133,134},{134,1... | collective-permute-start | bytes 2408456 | tf_op jit(solution)/shard_map/ppermute | solution.py:31
  21.0 29.7 %collective-permute-start.1 = (bf16[2,196,1024]{2,0,1:T(2,128)(2,1)}, bf16[2,196,1024]{2,0,1:T(2,128)(2,1)}, u32[]{:S(2)}, u32[]{:S(2)}) collective-permute-start(bf16[2,196,1024]{2,0,1:T(2,128)(2,1)} %param.8), channel_id=1, source_target_pairs={{129,128},{130,129},{131,130},{132,131},{133,132},{134,133},{135,1... | collective-permute-start | bytes 2408456 | tf_op jit(solution)/shard_map/ppermute | solution.py:32
  42.7 12.5 %collective-permute-start.2 = (bf16[1024,384]{1,0:T(8,128)(2,1)}, bf16[1024,384]{1,0:T(8,128)(2,1)}, u32[]{:S(2)}, u32[]{:S(2)}) collective-permute-start(bf16[1024,384]{1,0:T(8,128)(2,1)} %bitcast.4), channel_id=1, source_target_pairs={{0,128},{128,0},{1,129},{129,1},{2,130},{130,2},{3,131},{131,3},{4... | collective-permute-start | bytes 2359304 | tf_op jit(solution)/shard_map/ppermute | solution.py:41
  59.3 5.5 %copy-start.4 = (bf16[4,196,768]{2,1,0:T(8,128)(2,1)}, bf16[4,196,768]{2,1,0:T(8,128)(2,1)S(1)}, u32[]{:S(2)}) copy-start(bf16[4,196,768]{2,1,0:T(8,128)(2,1)S(1)} %get-tuple-element.15) | copy-start | bytes 3612676
  73.3 13.3 %collective-permute-start.3 = (bf16[4,196,768]{2,0,1:T(4,128)(2,1)}, bf16[4,196,768]{2,0,1:T(4,128)(2,1)S(1)}, u32[]{:S(2)}, u32[]{:S(2)}) collective-permute-start(bf16[4,196,768]{2,0,1:T(4,128)(2,1)} %copy.69), channel_id=1, source_target_pairs={{0,128},{128,0},{1,129},{129,1},{2,130},{130,2},{3,131},{131,3},{4... | collective-permute-start | bytes 3612680 | tf_op jit(solution)/shard_map/ppermute | solution.py:50
  73.3 3.7 %copy-start.6 = (bf16[4,196,768]{1,2,0:T(8,128)(2,1)S(1)}, bf16[4,196,768]{1,2,0:T(8,128)(2,1)}, u32[]{:S(2)}) copy-start(bf16[4,196,768]{1,2,0:T(8,128)(2,1)} %copy.64) | copy-start | bytes 3612676
  77.0 2.2 %copy-start.5 = (bf16[4,196,768]{2,1,0:T(8,128)(2,1)S(1)}, bf16[4,196,768]{2,1,0:T(8,128)(2,1)}, u32[]{:S(2)}) copy-start(bf16[4,196,768]{2,1,0:T(8,128)(2,1)} %copy-done.4) | copy-start | bytes 3612676
  77.0 2.2 %copy-start.10 = (bf16[1,768,768]{2,1,0:T(8,128)(2,1)S(1)}, bf16[1,768,768]{2,1,0:T(8,128)(2,1)}, u32[]{:S(2)}) copy-start(bf16[1,768,768]{2,1,0:T(8,128)(2,1)} %param.12) | copy-start | bytes 3538948
  80.5 1.4 %copy-start.2 = (f32[4,196,768]{2,1,0:T(8,128)}, f32[4,196,768]{2,1,0:T(8,128)S(1)}, u32[]{:S(2)}) copy-start(f32[4,196,768]{2,1,0:T(8,128)S(1)} %get-tuple-element.19) | copy-start | bytes 7225348
  80.5 2.1 %copy-start.11 = (bf16[1,768,768]{2,1,0:T(8,128)(2,1)S(1)}, bf16[1,768,768]{2,1,0:T(8,128)(2,1)}, u32[]{:S(2)}) copy-start(bf16[1,768,768]{2,1,0:T(8,128)(2,1)} %param.13) | copy-start | bytes 3538948
  87.1 2.1 %copy-start.9 = (bf16[1,768,1536]{2,1,0:T(8,128)(2,1)S(1)}, bf16[1,768,1536]{2,1,0:T(8,128)(2,1)}, u32[]{:S(2)}) copy-start(bf16[1,768,1536]{2,1,0:T(8,128)(2,1)} %param.14) | copy-start | bytes 7077892
  98.0 3.7 %copy-start.7 = (bf16[4,196,768]{1,2,0:T(8,128)(2,1)S(1)}, bf16[4,196,768]{1,2,0:T(8,128)(2,1)}, u32[]{:S(2)}) copy-start(bf16[4,196,768]{1,2,0:T(8,128)(2,1)} %copy.75) | copy-start | bytes 3612676
  101.7 2.4 %copy-start.3 = (f32[4,196,768]{2,1,0:T(8,128)S(1)}, f32[4,196,768]{2,1,0:T(8,128)}, u32[]{:S(2)}) copy-start(f32[4,196,768]{2,1,0:T(8,128)} %copy-done.2) | copy-start | bytes 7225348
  101.7 2.4 %copy-start.8 = (bf16[1,768,768]{2,1,0:T(8,128)(2,1)S(1)}, bf16[1,768,768]{2,1,0:T(8,128)(2,1)}, u32[]{:S(2)}) copy-start(bf16[1,768,768]{2,1,0:T(8,128)(2,1)} %param.15) | copy-start | bytes 3538948
  108.9 20.9 %copy-start.1 = (bf16[1,768,2304]{2,1,0:T(8,128)(2,1)S(1)}, bf16[1,768,2304]{2,1,0:T(8,128)(2,1)}, u32[]{:S(2)}) copy-start(bf16[1,768,2304]{2,1,0:T(8,128)(2,1)} %param.11) | copy-start | bytes 10616836
  109.8 16.3 %collective-permute-start.4 = (bf16[2,196,768]{2,0,1:T(2,128)(2,1)S(1)}, bf16[2,196,768]{2,0,1:T(2,128)(2,1)S(1)}, u32[]{:S(2)}, u32[]{:S(2)}) collective-permute-start(bf16[2,196,768]{2,0,1:T(2,128)(2,1)S(1)} %get-tuple-element.12), channel_id=1, source_target_pairs={{128,129},{129,130},{130,131},{131,132},{132,133},{133,134},{134,1... | collective-permute-start | bytes 1806344 | tf_op jit(solution)/shard_map/ppermute | solution.py:160
  111.8 15.7 %collective-permute-start.5 = (bf16[2,196,768]{2,0,1:T(2,128)(2,1)S(1)}, bf16[2,196,768]{2,0,1:T(2,128)(2,1)S(1)}, u32[]{:S(2)}, u32[]{:S(2)}) collective-permute-start(bf16[2,196,768]{2,0,1:T(2,128)(2,1)S(1)} %get-tuple-element.13), channel_id=1, source_target_pairs={{129,128},{130,129},{131,130},{132,131},{133,132},{134,133},{135,1... | collective-permute-start | bytes 1806344 | tf_op jit(solution)/shard_map/ppermute | solution.py:161

commit v8 on v7

--- a/solution.py
+++ b/solution.py
@@ -157,7 +157,14 @@
     peers = lax.axis_size("pair")
     up = [(peers + i, peers + (i + 1) % peers) for i in range(peers)]
     down = [(j, i) for i, j in up]
-    from_prev = lax.ppermute(slot_sums(2 * img_local).astype(jnp.bfloat16), ("branch", "pair"), up)
+    handed = lax.ppermute(
+        slot_sums(2 * img_local).astype(jnp.bfloat16),
+        ("branch", "pair"),
+        [(peers + i, i) for i in range(peers)],
+    )
+    from_prev = lax.ppermute(
+        handed, ("branch", "pair"), [(i, peers + (i + 1) % peers) for i in range(peers)]
+    )
     from_next = lax.ppermute(slot_sums(0).astype(jnp.bfloat16), ("branch", "pair"), down)
     image_sums = (
         slot_sums(img_local) + from_prev.astype(jnp.float32) + from_next.astype(jnp.float32)

time: 130 us -> 135 us (1.038)
  waiting for transfers between devices: 23.9 us -> 32.5 us
  starting transfers between devices: 42 us -> 38.1 us
    ppermute x0 -> x1, waiting for transfers between devices: none -> 9.11 us  [body(): lax.ppermute(handed, ('branch', 'pair'), [(i, peers + (i + 1) % peers) fo...]
    ppermute x1, starting transfers between devices: 8.79 us -> 3.09 us  [body(): lax.ppermute(slot_sums(0).astype(jnp.bfloat16), ('branch', 'pair'), down)]
    ppermute x1, waiting for transfers between devices: 5.46 us -> 0.01 us  [body(): lax.ppermute(slot_sums(2 * img_local).astype(jnp.bfloat16), ('branch', 'p...]
    ppermute x1, waiting for transfers between devices: 1.48 us -> 6.35 us  [body(): lax.ppermute(slot_sums(0).astype(jnp.bfloat16), ('branch', 'pair'), down)]
  transfers between devices with their start and end apart: 7 -> 8, of which waited for: 4 -> 4; matrix products, arithmetic and copies ran while one was open for 13% -> 12% of each run, Pallas kernels for 0% -> 0%
where the time goes in v8:
time: 135 us
  starting transfers between devices  38.1 us (28%)
  matrix products  34.3 us (25%)
  waiting for transfers between devices  32.5 us (24%)
  local copies, waits for them, and re-layouts  22.7 us (17%)
  other arithmetic  6.61 us (5%)
    all_to_all x1, starting transfers between devices, gathered_weight(): got = lax.all_to_all(spread, 'pair', 0, 0, tiled=True).reshape(-1, half)  16.8 us
    dot_general x6, matrix products, project(): jnp.einsum('btd,de->bte', values, matrix, preferred_element_type=jnp.floa...  14.5 us
    all_to_all x1, waiting for transfers between devices, gathered_weight(): got = lax.all_to_all(spread, 'pair', 0, 0, tiled=True).reshape(-1, half)  13.4 us
    ppermute x1, waiting for transfers between devices, body(): lax.ppermute(handed, ('branch', 'pair'), [(i, peers + (i + 1) % peers) fo...  9.11 us
    ppermute x1, starting transfers between devices, branch_one_padded(): after = lax.ppermute(initial, ('branch', 'pair'), down)  8.3 us
    dot_general x2, matrix products, attend(): jnp.einsum('bqhd,bkhd->bhqk', query_heads, key_heads, preferred_element_t...  7.27 us
    ppermute x1, waiting for transfers between devices, body(): lax.ppermute(slot_sums(0).astype(jnp.bfloat16), ('branch', 'pair'), down)  6.35 us
    dot_general x2, matrix products, attend(): jnp.einsum('bhqk,bkhd->bqhd', attn_probs, value_heads, preferred_element_...  4.53 us
  transfers between devices with their start and end apart: 8, of which 4 were waited for; matrix products, arithmetic and copies ran while one was open for 12% of the time, Pallas kernels for 0%

profile of v8, /device:TPU:1, one launch (start us, length us, event | category | flops | bytes accessed | tf_op | source)
XLA Modules:
  0.0 134.5 jit_solution(15314745039462135411)
XLA Ops:
  0.0 0.0 copy-start
  0.0 0.8 constant_dynamic-slice_fusion
  0.8 0.9 broadcast_in_dim.2
  1.8 16.8 %all-to-all-start = ((bf16[128,8,384]{2,1,0:T(8,128)(2,1)}), bf16[128,8,384]{2,1,0:T(8,128)(2,1)}, u32[]{:S(2)}, u32[]{:S(2)}) async-start(bf16[128,8,384]{2,1,0:T(8,128)(2,1)} %broadcast_in_dim.2), calls=%async_computation | async-start | bytes 1572864 | tf_op jit(solution)/shard_map/all_to_all | solution.py:40
  18.6 2.4 %collective-permute-start = (bf16[2,196,1024]{2,0,1:T(2,128)(2,1)}, bf16[2,196,1024]{2,0,1:T(2,128)(2,1)}, u32[]{:S(2)}, u32[]{:S(2)}) collective-permute-start(bf16[2,196,1024]{2,0,1:T(2,128)(2,1)} %param.8), channel_id=1, source_target_pairs={{128,129},{129,130},{130,131},{131,132},{132,133},{133,134},{134,1... | collective-permute-start | bytes 2408456 | tf_op jit(solution)/shard_map/ppermute | solution.py:31
  21.0 8.3 %collective-permute-start.1 = (bf16[2,196,1024]{2,0,1:T(2,128)(2,1)}, bf16[2,196,1024]{2,0,1:T(2,128)(2,1)}, u32[]{:S(2)}, u32[]{:S(2)}) collective-permute-start(bf16[2,196,1024]{2,0,1:T(2,128)(2,1)} %param.8), channel_id=1, source_target_pairs={{129,128},{130,129},{131,130},{132,131},{133,132},{134,133},{135,1... | collective-permute-start | bytes 2408456 | tf_op jit(solution)/shard_map/ppermute | solution.py:32
  29.3 13.4 %all-to-all-done = bf16[128,8,384]{2,1,0:T(8,128)(2,1)} async-done(((bf16[128,8,384]{2,1,0:T(8,128)(2,1)}), bf16[128,8,384]{2,1,0:T(8,128)(2,1)}, u32[]{:S(2)}, u32[]{:S(2)}) %all-to-all-start) | async-done | bytes 786464 | tf_op jit(solution)/shard_map/all_to_all | solution.py:40
  42.7 3.6 %collective-permute-start.2 = (bf16[1024,384]{1,0:T(8,128)(2,1)}, bf16[1024,384]{1,0:T(8,128)(2,1)}, u32[]{:S(2)}, u32[]{:S(2)}) collective-permute-start(bf16[1024,384]{1,0:T(8,128)(2,1)} %bitcast.4), channel_id=1, source_target_pairs={{0,128},{128,0},{1,129},{129,1},{2,130},{130,2},{3,131},{131,3},{4... | collective-permute-start | bytes 2359304 | tf_op jit(solution)/shard_map/ppermute | solution.py:41
  46.3 0.8 and_select_fusion.1
  47.1 3.6 %collective-permute-done = bf16[2,196,1024]{2,0,1:T(2,128)(2,1)} collective-permute-done((bf16[2,196,1024]{2,0,1:T(2,128)(2,1)}, bf16[2,196,1024]{2,0,1:T(2,128)(2,1)}, u32[]{:S(2)}, u32[]{:S(2)}) %collective-permute-start) | collective-permute-done | bytes 802848 | tf_op jit(solution)/shard_map/ppermute | solution.py:31
  50.7 0.0 collective-permute-done.1
  50.7 4.4 %fusion.22 = bf16[4,196,1024]{2,0,1:T(4,128)(2,1)S(1)} fusion(bf16[2,196,1024]{2,0,1:T(2,128)(2,1)} %collective-permute-done.1, bf16[2,196,1024]{2,0,1:T(2,128)(2,1)} %param.8, bf16[2,196,1024]{2,0,1:T(2,128)(2,1)} %collective-permute-done, s32[4]{0:T(128)S(1)} %fusion.60), kind=kOutput, calls=%fused_computation.35 | convolution fusion | flops 17661976 | bytes 4014096 | tf_op jit(solution)/shard_map/js,std->jtd/dot_general | solution.py:98
  55.2 0.0 collective-permute-done.2
  55.2 4.1 %convert_reduce_fusion = (f32[4,196]{1,0:T(4,128)S(1)}, bf16[4,196,768]{2,1,0:T(8,128)(2,1)S(1)}) fusion(bf16[1024,384]{1,0:T(8,128)(2,1)} %collective-permute-done.2, bf16[1024,384]{1,0:T(8,128)(2,1)} %bitcast.4, pred[]{:T(512)S(6)} %eq.35, bf16[4,196,1024]{2,0,1:T(4,128)(2,1)S(1)} %fusion.22), kind=kOutput, calls=%fused_computation.11 | convolution fusion | flops 1242008832 | bytes 4385857 | tf_op jit(solution)/shard_map/btd,de->bte/dot_general | solution.py:62
  59.3 1.5 %copy.69 = bf16[4,196,768]{2,0,1:T(4,128)(2,1)} copy(bf16[4,196,768]{2,1,0:T(8,128)(2,1)S(1)} %get-tuple-element.15) | data formatting | bytes 2408448 | tf_op jit(solution)/shard_map/convert_element_type | solution.py:105
  60.8 0.5 fusion.15
  61.3 0.0 copy-done
  61.3 3.4 %convolution_convert_fusion = bf16[4,196,2304]{2,1,0:T(8,128)(2,1)S(1)} fusion(bf16[1,768,2304]{2,1,0:T(8,128)(2,1)S(1)} %copy-done, bf16[4,196,768]{2,1,0:T(8,128)(2,1)S(1)} %get-tuple-element.15, f32[4,196]{1,0:T(4,128)S(1)} %add_rsqrt_fusion.2, f32[4,196]{1,0:T(4,128)S(1)} %broadcast_multiply_fusion.2), kind=kOutput, calls=%fused_computation.6 | convolution fusion | flops 2778746880 | bytes 8362112 | tf_op jit(solution)/shard_map/btd,de->bte/dot_general | solution.py:62
  64.7 0.0 copy-done.4
  64.7 1.9 %fusion.68 = (bf16[4,196,768]{2,1,0:T(8,128)(2,1)}, bf16[4,196,768]{2,1,0:T(8,128)(2,1)}, bf16[4,196,768]{2,1,0:T(8,128)(2,1)}) fusion(bf16[4,196,2304]{2,1,0:T(8,128)(2,1)S(1)} %convolution_convert_fusion), kind=kLoop, calls=%fused_computation.90 | loop fusion | bytes 7225344 | tf_op jit(solution)/shard_map/slice | solution.py:87
  66.6 1.6 %copy.66 = bf16[4,196,768]{1,2,0:T(8,128)(2,1)S(1)} copy(bf16[4,196,768]{2,1,0:T(8,128)(2,1)} %get-tuple-element.7) | data formatting | bytes 2408448 | tf_op jit(solution)/shard_map/slice | solution.py:87
  68.3 2.5 %copy.65 = bf16[4,196,768]{1,2,0:T(8,128)(2,1)} copy(bf16[4,196,768]{2,1,0:T(8,128)(2,1)} %get-tuple-element.8) | data formatting | bytes 2408448 | tf_op jit(solution)/shard_map/slice | solution.py:86
  70.8 2.5 %copy.64 = bf16[4,196,768]{1,2,0:T(8,128)(2,1)} copy(bf16[4,196,768]{2,1,0:T(8,128)(2,1)} %get-tuple-element.9) | data formatting | bytes 2408448 | tf_op jit(solution)/shard_map/slice | solution.py:88
  73.3 0.0 collective-permute-start.3
  73.3 3.6 %fusion = (f32[4,12,196]{2,1,0:T(8,128)S(1)}, f32[4,12,196,196]{2,3,1,0:T(8,128)S(1)}) fusion(bf16[4,196,12,64]{1,3,2,0:T(8,128)(2,1)} %bitcast.66, bf16[4,196,12,64]{1,3,2,0:T(8,128)(2,1)S(1)} %bitcast.65), kind=kOutput, calls=%fused_computation.4 | convolution fusion | flops 239706432 | bytes 9821952 | tf_op jit(solution)/shard_map/bqhd,bkhd->bhqk/dot_general | solution.py:71
  77.0 0.0 copy-done.6
  77.0 0.0 copy-start.5
  77.0 0.0 copy-start.10
  77.0 2.2 %fusion.26 = bf16[4,12,64,196]{3,2,1,0:T(8,128)(2,1)S(1)} fusion(bf16[4,196,12,64]{1,3,2,0:T(8,128)(2,1)S(1)} %bitcast.68, f32[4,12,196,196]{2,3,1,0:T(8,128)S(1)} %get-tuple-element.17, f32[4,12,196]{2,1,0:T(8,128)S(1)} %get-tuple-element.16), kind=kOutput, calls=%fused_computation.38 | convolution fusion | flops 242161920 | bytes 9821952 | tf_op jit(solution)/shard_map/bhqk,bkhd->bqhd/dot_general | solution.py:76
  79.2 0.0 copy-done.5
  79.2 0.0 copy-done.10
  79.2 1.3 fusion.71
  80.5 0.0 copy-start.11
  80.6 0.4 multiply_reduce_fusion
  81.0 1.0 copy-done.2
  82.0 0.7 copy-done.11
  82.7 2.3 %convolution_convert_fusion.2 = bf16[4,196,768]{2,1,0:T(8,128)(2,1)} fusion(f32[4,196,768]{2,1,0:T(8,128)S(1)} %get-tuple-element.19, f32[4,196]{1,0:T(4,128)S(1)} %add_rsqrt_fusion.1, f32[4,196]{1,0:T(4,128)S(1)} %broadcast_multiply_fusion.1, bf16[1,768,768]{2,1,0:T(8,128)(2,1)S(1)} %copy-done.11), kind=kOutput, calls=%fused_computation.50 | convolution fusion | flops 927252480 | bytes 4798592 | tf_op jit(solution)/shard_map/btd,de->bte/dot_general | solution.py:62
  84.9 1.6 %copy.76 = bf16[4,196,768]{1,2,0:T(8,128)(2,1)S(1)} copy(bf16[4,196,768]{2,1,0:T(8,128)(2,1)} %convolution_convert_fusion.2) | data formatting | bytes 2408448 | tf_op jit(solution)/shard_map/convert_element_type | solution.py:91
  86.6 0.0 collective-permute-done.3
  86.6 0.5 convert_reduce_fusion.1
  87.1 0.0 copy-start.9
  87.2 1.2 fusion.17
  88.3 0.9 fusion.18
  89.2 0.0 copy-done.9
  89.3 2.1 %convolution_convert_fusion.1 = bf16[4,196,1536]{2,1,0:T(8,128)(2,1)S(1)} fusion(bf16[1,768,1536]{2,1,0:T(8,128)(2,1)S(1)} %copy-done.9, bf16[4,196,768]{2,0,1:T(4,128)(2,1)S(1)} %fusion.18), kind=kOutput, calls=%fused_computation.13 | convolution fusion | flops 1850892288 | bytes 5971968 | tf_op jit(solution)/shard_map/btd,de->bte/dot_general | solution.py:62
  91.3 1.6 %fusion.69 = (bf16[4,196,768]{2,1,0:T(8,128)(2,1)}, bf16[4,196,768]{2,1,0:T(8,128)(2,1)}) fusion(bf16[4,196,1536]{2,1,0:T(8,128)(2,1)S(1)} %convolution_convert_fusion.1), kind=kLoop, calls=%fused_computation.91 | loop fusion | bytes 4816896 | tf_op jit(solution)/shard_map/slice | solution.py:93
  93.0 2.5 %copy.77 = bf16[4,196,768]{1,2,0:T(8,128)(2,1)} copy(bf16[4,196,768]{2,1,0:T(8,128)(2,1)} %get-tuple-element.10) | data formatting | bytes 2408448 | tf_op jit(solution)/shard_map/slice | solution.py:93
  95.5 2.6 %copy.75 = bf16[4,196,768]{1,2,0:T(8,128)(2,1)} copy(bf16[4,196,768]{2,1,0:T(8,128)(2,1)} %get-tuple-element.11) | data formatting | bytes 2408448 | tf_op jit(solution)/shard_map/slice | solution.py:93
  98.1 3.6 %fusion.1 = (f32[4,12,196]{2,1,0:T(8,128)S(1)}, f32[4,12,196,196]{2,3,1,0:T(8,128)S(1)}) fusion(bf16[4,196,12,64]{1,3,2,0:T(8,128)(2,1)S(1)} %bitcast.64, bf16[4,196,12,64]{1,3,2,0:T(8,128)(2,1)} %bitcast.67), kind=kOutput, calls=%fused_computation.5 | convolution fusion | flops 239706432 | bytes 9821952 | tf_op jit(solution)/shard_map/bqhd,bkhd->bhqk/dot_general | solution.py:71
  101.7 0.0 copy-done.7
  101.7 0.0 copy-start.3
  101.7 0.0 copy-start.8
  101.7 2.4 %fusion.25 = bf16[4,12,64,196]{3,2,1,0:T(8,128)(2,1)S(1)} fusion(bf16[4,196,12,64]{1,3,2,0:T(8,128)(2,1)S(1)} %bitcast.69, f32[4,12,196,196]{2,3,1,0:T(8,128)S(1)} %get-tuple-element.21, f32[4,12,196]{2,1,0:T(8,128)S(1)} %get-tuple-element.20), kind=kOutput, calls=%fused_computation.37 | convolution fusion | flops 242161920 | bytes 9821952 | tf_op jit(solution)/shard_map/bhqk,bkhd->bqhd/dot_general | solution.py:76
  104.1 1.2 convolution_add_fusion
  105.4 3.6 %fusion.72 = (bf16[6,196,768]{2,0,1:T(8,128)(2,1)S(1)}, f32[6,196,768]{2,0,1:T(8,128)S(1)}) fusion(f32[4,196,768]{2,1,0:T(8,128)S(1)} %convolution_add_fusion, s32[4]{0:T(128)S(1)} %get-tuple-element.5), kind=kOutput, calls=%fused_computation.94 | convolution fusion | flops 44255256 | bytes 7827472 | tf_op jit(solution)/shard_map/sj,jtd->std/dot_general | solution.py:152
  109.0 0.0 copy-start.1
  109.0 0.8 fusion.70
  109.8 2.6 %collective-permute-start.4 = (bf16[2,196,768]{2,0,1:T(2,128)(2,1)S(1)}, bf16[2,196,768]{2,0,1:T(2,128)(2,1)S(1)}, u32[]{:S(2)}, u32[]{:S(2)}) collective-permute-start(bf16[2,196,768]{2,0,1:T(2,128)(2,1)S(1)} %get-tuple-element.12), channel_id=1, source_target_pairs={{128,0},{129,1},{130,2},{131,3},{132,4},{133,5},{134,6},{135,7},{1... | collective-permute-start | bytes 1806344 | tf_op jit(solution)/shard_map/ppermute | solution.py:160
  112.4 3.1 %collective-permute-start.6 = (bf16[2,196,768]{2,0,1:T(2,128)(2,1)S(1)}, bf16[2,196,768]{2,0,1:T(2,128)(2,1)S(1)}, u32[]{:S(2)}, u32[]{:S(2)}) collective-permute-start(bf16[2,196,768]{2,0,1:T(2,128)(2,1)S(1)} %get-tuple-element.13), channel_id=1, source_target_pairs={{129,128},{130,129},{131,130},{132,131},{133,132},{134,133},{135,1... | collective-permute-start | bytes 1806344 | tf_op jit(solution)/shard_map/ppermute | solution.py:168
  115.5 0.0 collective-permute-done.4
  115.5 1.3 collective-permute-start.5
  116.8 6.4 %collective-permute-done.6 = bf16[2,196,768]{2,0,1:T(2,128)(2,1)S(1)} collective-permute-done((bf16[2,196,768]{2,0,1:T(2,128)(2,1)S(1)}, bf16[2,196,768]{2,0,1:T(2,128)(2,1)S(1)}, u32[]{:S(2)}, u32[]{:S(2)}) %collective-permute-start.6) | collective-permute-done | bytes 602144 | tf_op jit(solution)/shard_map/ppermute | solution.py:168
  123.2 9.1 %collective-permute-done.5 = bf16[2,196,768]{2,0,1:T(2,128)(2,1)S(1)} collective-permute-done((bf16[2,196,768]{2,0,1:T(2,128)(2,1)S(1)}, bf16[2,196,768]{2,0,1:T(2,128)(2,1)S(1)}, u32[]{:S(2)}, u32[]{:S(2)}) %collective-permute-start.5) | collective-permute-done | bytes 602144 | tf_op jit(solution)/shard_map/ppermute | solution.py:165
  132.3 2.2 %fusion.49 = f32[1,2,196,768]{3,1,2,0:T(2,128)} fusion(f32[6,196,768]{2,0,1:T(8,128)S(1)} %get-tuple-element.23, bf16[2,196,768]{2,0,1:T(2,128)(2,1)S(1)} %collective-permute-done.6, bf16[2,196,768]{2,0,1:T(2,128)(2,1)S(1)} %collective-permute-done.5), kind=kLoop, calls=%fused_computation.58 | loop fusion | flops 1204224 | bytes 3612672 | tf_op jit(solution)/shard_map/reshape | solution.py:172
  (14 shorter events, 0.1 us)
Async XLA Ops:
  0.0 61.3 %copy-start = (bf16[1,768,2304]{2,1,0:T(8,128)(2,1)S(1)}, bf16[1,768,2304]{2,1,0:T(8,128)(2,1)}, u32[]{:S(2)}) copy-start(bf16[1,768,2304]{2,1,0:T(8,128)(2,1)} %param.11) | copy-start | bytes 10616836
  1.8 40.9 %all-to-all-start = ((bf16[128,8,384]{2,1,0:T(8,128)(2,1)}), bf16[128,8,384]{2,1,0:T(8,128)(2,1)}, u32[]{:S(2)}, u32[]{:S(2)}) async-start(bf16[128,8,384]{2,1,0:T(8,128)(2,1)} %broadcast_in_dim.2), calls=%async_computation | async-start | bytes 1572864 | tf_op jit(solution)/shard_map/all_to_all | solution.py:40
  18.6 32.1 %collective-permute-start = (bf16[2,196,1024]{2,0,1:T(2,128)(2,1)}, bf16[2,196,1024]{2,0,1:T(2,128)(2,1)}, u32[]{:S(2)}, u32[]{:S(2)}) collective-permute-start(bf16[2,196,1024]{2,0,1:T(2,128)(2,1)} %param.8), channel_id=1, source_target_pairs={{128,129},{129,130},{130,131},{131,132},{132,133},{133,134},{134,1... | collective-permute-start | bytes 2408456 | tf_op jit(solution)/shard_map/ppermute | solution.py:31
  21.0 29.7 %collective-permute-start.1 = (bf16[2,196,1024]{2,0,1:T(2,128)(2,1)}, bf16[2,196,1024]{2,0,1:T(2,128)(2,1)}, u32[]{:S(2)}, u32[]{:S(2)}) collective-permute-start(bf16[2,196,1024]{2,0,1:T(2,128)(2,1)} %param.8), channel_id=1, source_target_pairs={{129,128},{130,129},{131,130},{132,131},{133,132},{134,133},{135,1... | collective-permute-start | bytes 2408456 | tf_op jit(solution)/shard_map/ppermute | solution.py:32
  42.7 12.5 %collective-permute-start.2 = (bf16[1024,384]{1,0:T(8,128)(2,1)}, bf16[1024,384]{1,0:T(8,128)(2,1)}, u32[]{:S(2)}, u32[]{:S(2)}) collective-permute-start(bf16[1024,384]{1,0:T(8,128)(2,1)} %bitcast.4), channel_id=1, source_target_pairs={{0,128},{128,0},{1,129},{129,1},{2,130},{130,2},{3,131},{131,3},{4... | collective-permute-start | bytes 2359304 | tf_op jit(solution)/shard_map/ppermute | solution.py:41
  59.3 5.5 %copy-start.4 = (bf16[4,196,768]{2,1,0:T(8,128)(2,1)}, bf16[4,196,768]{2,1,0:T(8,128)(2,1)S(1)}, u32[]{:S(2)}) copy-start(bf16[4,196,768]{2,1,0:T(8,128)(2,1)S(1)} %get-tuple-element.15) | copy-start | bytes 3612676
  73.3 13.3 %collective-permute-start.3 = (bf16[4,196,768]{2,0,1:T(4,128)(2,1)}, bf16[4,196,768]{2,0,1:T(4,128)(2,1)S(1)}, u32[]{:S(2)}, u32[]{:S(2)}) collective-permute-start(bf16[4,196,768]{2,0,1:T(4,128)(2,1)} %copy.69), channel_id=1, source_target_pairs={{0,128},{128,0},{1,129},{129,1},{2,130},{130,2},{3,131},{131,3},{4... | collective-permute-start | bytes 3612680 | tf_op jit(solution)/shard_map/ppermute | solution.py:50
  73.3 3.6 %copy-start.6 = (bf16[4,196,768]{1,2,0:T(8,128)(2,1)S(1)}, bf16[4,196,768]{1,2,0:T(8,128)(2,1)}, u32[]{:S(2)}) copy-start(bf16[4,196,768]{1,2,0:T(8,128)(2,1)} %copy.64) | copy-start | bytes 3612676
  77.0 2.2 %copy-start.5 = (bf16[4,196,768]{2,1,0:T(8,128)(2,1)S(1)}, bf16[4,196,768]{2,1,0:T(8,128)(2,1)}, u32[]{:S(2)}) copy-start(bf16[4,196,768]{2,1,0:T(8,128)(2,1)} %copy-done.4) | copy-start | bytes 3612676
  77.0 2.2 %copy-start.10 = (bf16[1,768,768]{2,1,0:T(8,128)(2,1)S(1)}, bf16[1,768,768]{2,1,0:T(8,128)(2,1)}, u32[]{:S(2)}) copy-start(bf16[1,768,768]{2,1,0:T(8,128)(2,1)} %param.12) | copy-start | bytes 3538948
  80.5 1.5 %copy-start.2 = (f32[4,196,768]{2,1,0:T(8,128)}, f32[4,196,768]{2,1,0:T(8,128)S(1)}, u32[]{:S(2)}) copy-start(f32[4,196,768]{2,1,0:T(8,128)S(1)} %get-tuple-element.19) | copy-start | bytes 7225348
  80.5 2.1 %copy-start.11 = (bf16[1,768,768]{2,1,0:T(8,128)(2,1)S(1)}, bf16[1,768,768]{2,1,0:T(8,128)(2,1)}, u32[]{:S(2)}) copy-start(bf16[1,768,768]{2,1,0:T(8,128)(2,1)} %param.13) | copy-start | bytes 3538948
  87.1 2.1 %copy-start.9 = (bf16[1,768,1536]{2,1,0:T(8,128)(2,1)S(1)}, bf16[1,768,1536]{2,1,0:T(8,128)(2,1)}, u32[]{:S(2)}) copy-start(bf16[1,768,1536]{2,1,0:T(8,128)(2,1)} %param.14) | copy-start | bytes 7077892
  98.1 3.7 %copy-start.7 = (bf16[4,196,768]{1,2,0:T(8,128)(2,1)S(1)}, bf16[4,196,768]{1,2,0:T(8,128)(2,1)}, u32[]{:S(2)}) copy-start(bf16[4,196,768]{1,2,0:T(8,128)(2,1)} %copy.75) | copy-start | bytes 3612676
  101.7 2.4 %copy-start.3 = (f32[4,196,768]{2,1,0:T(8,128)S(1)}, f32[4,196,768]{2,1,0:T(8,128)}, u32[]{:S(2)}) copy-start(f32[4,196,768]{2,1,0:T(8,128)} %copy-done.2) | copy-start | bytes 7225348
  101.7 2.4 %copy-start.8 = (bf16[1,768,768]{2,1,0:T(8,128)(2,1)S(1)}, bf16[1,768,768]{2,1,0:T(8,128)(2,1)}, u32[]{:S(2)}) copy-start(bf16[1,768,768]{2,1,0:T(8,128)(2,1)} %param.15) | copy-start | bytes 3538948
  109.0 25.5 %copy-start.1 = (bf16[1,768,2304]{2,1,0:T(8,128)(2,1)S(1)}, bf16[1,768,2304]{2,1,0:T(8,128)(2,1)}, u32[]{:S(2)}) copy-start(bf16[1,768,2304]{2,1,0:T(8,128)(2,1)} %param.11) | copy-start | bytes 10616836
  109.8 5.7 %collective-permute-start.4 = (bf16[2,196,768]{2,0,1:T(2,128)(2,1)S(1)}, bf16[2,196,768]{2,0,1:T(2,128)(2,1)S(1)}, u32[]{:S(2)}, u32[]{:S(2)}) collective-permute-start(bf16[2,196,768]{2,0,1:T(2,128)(2,1)S(1)} %get-tuple-element.12), channel_id=1, source_target_pairs={{128,0},{129,1},{130,2},{131,3},{132,4},{133,5},{134,6},{135,7},{1... | collective-permute-start | bytes 1806344 | tf_op jit(solution)/shard_map/ppermute | solution.py:160
  112.4 10.8 %collective-permute-start.6 = (bf16[2,196,768]{2,0,1:T(2,128)(2,1)S(1)}, bf16[2,196,768]{2,0,1:T(2,128)(2,1)S(1)}, u32[]{:S(2)}, u32[]{:S(2)}) collective-permute-start(bf16[2,196,768]{2,0,1:T(2,128)(2,1)S(1)} %get-tuple-element.13), channel_id=1, source_target_pairs={{129,128},{130,129},{131,130},{132,131},{133,132},{134,133},{135,1... | collective-permute-start | bytes 1806344 | tf_op jit(solution)/shard_map/ppermute | solution.py:168
  115.5 16.8 %collective-permute-start.5 = (bf16[2,196,768]{2,0,1:T(2,128)(2,1)S(1)}, bf16[2,196,768]{2,0,1:T(2,128)(2,1)S(1)}, u32[]{:S(2)}, u32[]{:S(2)}) collective-permute-start(bf16[2,196,768]{2,0,1:T(2,128)(2,1)S(1)} %collective-permute-done.4), channel_id=1, source_target_pairs={{0,129},{1,130},{2,131},{3,132},{4,133},{5,134},{6,135},{7,136},{8... | collective-permute-start | bytes 1806344 | tf_op jit(solution)/shard_map/ppermute | solution.py:165

commit v9 on v7

--- a/solution.py
+++ b/solution.py
@@ -6,19 +6,6 @@
 from jax.sharding import PartitionSpec as P
 
 HEADS = 12
-
-
-def padded(x, sides, width):
-    for axis, dim in sides:
-        peers, length = (lax.axis_size(axis), x.shape[dim])
-        up = [(i, (i + 1) % peers) for i in range(peers)]
-        down = [(j, i) for i, j in up]
-        last = lax.slice_in_dim(x, length - width, length, axis=dim)
-        initial = lax.slice_in_dim(x, 0, width, axis=dim)
-        before = lax.ppermute(last, axis, up)
-        after = lax.ppermute(initial, axis, down)
-        x = jnp.concatenate([before, x, after], axis=dim)
-    return x
 
 
 def branch_one_padded(x, dim, width):
@@ -100,7 +87,7 @@
     ).astype(jnp.bfloat16)
 
 
-def embed_picked(onehot, window, full_embed, pair_count, tokens_per, enc_width, model_width):
+def embed_picked(onehot, window, full_embed):
     picked = select_rows(onehot, window)
     return project(picked, full_embed).astype(jnp.bfloat16)
 
@@ -108,8 +95,6 @@
 def body(encoder_rows, pair_list, embed_weight, self_qkv, self_out, cross_q, cross_kv, cross_out):
     img_local = encoder_rows.shape[0]
     tokens_per = encoder_rows.shape[1]
-    enc_width = encoder_rows.shape[2]
-    pair_count = pair_list.shape[0]
     views_local = self_qkv.shape[0]
     devices = lax.axis_size("pair")
     device_id = lax.axis_index("pair")
@@ -117,7 +102,6 @@
     image_total = img_local * devices
     window_start = (device_id - 1) * img_local
     slot_index = jnp.arange(3 * img_local, dtype=jnp.int32)
-    other_onehots = []
     local_view = 0
     view_id = branch_id * views_local + local_view
     own_ids = jnp.where(view_id == 0, pair_list[:, 0], pair_list[:, 1])
@@ -126,15 +110,10 @@
     other_place = jnp.mod(other_ids - window_start, image_total)
     own_places = [own_place]
     own_onehots = own_place[:, None] == slot_index[None, :]
-    other_onehots.append(other_place[:, None] == slot_index[None, :])
     full_embed = gathered_weight(embed_weight, branch_id, devices)
     model_width = full_embed.shape[1]
     window = branch_one_padded(encoder_rows, 0, img_local)
-    own_list = [
-        embed_picked(
-            own_onehots, window, full_embed, pair_count, tokens_per, enc_width, model_width
-        )
-    ]
+    own_list = [embed_picked(own_onehots, window, full_embed)]
     partner_list = [swapped(own_list[0], "branch", 0)]
     local_view = 0
     decoded = attention_part(

time: 130 us -> 130 us (level)
  no operation moved by 1% of the time
where the time goes in v9:
time: 130 us
  starting transfers between devices  42 us (32%)
  matrix products  34.3 us (26%)
  waiting for transfers between devices  23.9 us (18%)
  local copies, waits for them, and re-layouts  22.7 us (17%)
  other arithmetic  6.57 us (5%)
    all_to_all x1, starting transfers between devices, gathered_weight(): got = lax.all_to_all(spread, 'pair', 0, 0, tiled=True).reshape(-1, half)  16.8 us
    dot_general x6, matrix products, project(): jnp.einsum('btd,de->bte', values, matrix, preferred_element_type=jnp.floa...  14.5 us
    all_to_all x1, waiting for transfers between devices, gathered_weight(): got = lax.all_to_all(spread, 'pair', 0, 0, tiled=True).reshape(-1, half)  13.4 us
    ppermute x1, starting transfers between devices, body(): lax.ppermute(slot_sums(0).astype(jnp.bfloat16), ('branch', 'pair'), down)  8.79 us
    ppermute x1, starting transfers between devices, branch_one_padded(): after = lax.ppermute(initial, ('branch', 'pair'), down)  8.3 us
    dot_general x2, matrix products, attend(): jnp.einsum('bqhd,bkhd->bhqk', query_heads, key_heads, preferred_element_t...  7.28 us
    ppermute x1, waiting for transfers between devices, body(): lax.ppermute(slot_sums(2 * img_local).astype(jnp.bfloat16), ('branch', 'p...  5.46 us
    dot_general x2, matrix products, attend(): jnp.einsum('bhqk,bkhd->bqhd', attn_probs, value_heads, preferred_element_...  4.53 us
  transfers between devices with their start and end apart: 7, of which 4 were waited for; matrix products, arithmetic and copies ran while one was open for 13% of the time, Pallas kernels for 0%

profile of v9, /device:TPU:1, one launch (start us, length us, event | category | flops | bytes accessed | tf_op | source)
XLA Modules:
  0.0 129.8 jit_solution(16754326250729663346)
XLA Ops:
  0.0 0.0 copy-start
  0.0 0.8 constant_dynamic-slice_fusion
  0.8 0.9 broadcast_in_dim.2
  1.8 16.8 %all-to-all-start = ((bf16[128,8,384]{2,1,0:T(8,128)(2,1)}), bf16[128,8,384]{2,1,0:T(8,128)(2,1)}, u32[]{:S(2)}, u32[]{:S(2)}) async-start(bf16[128,8,384]{2,1,0:T(8,128)(2,1)} %broadcast_in_dim.2), calls=%async_computation | async-start | bytes 1572864 | tf_op jit(solution)/shard_map/all_to_all | solution.py:27
  18.6 2.4 %collective-permute-start = (bf16[2,196,1024]{2,0,1:T(2,128)(2,1)}, bf16[2,196,1024]{2,0,1:T(2,128)(2,1)}, u32[]{:S(2)}, u32[]{:S(2)}) collective-permute-start(bf16[2,196,1024]{2,0,1:T(2,128)(2,1)} %param.8), channel_id=1, source_target_pairs={{128,129},{129,130},{130,131},{131,132},{132,133},{133,134},{134,1... | collective-permute-start | bytes 2408456 | tf_op jit(solution)/shard_map/ppermute | solution.py:18
  21.0 8.3 %collective-permute-start.1 = (bf16[2,196,1024]{2,0,1:T(2,128)(2,1)}, bf16[2,196,1024]{2,0,1:T(2,128)(2,1)}, u32[]{:S(2)}, u32[]{:S(2)}) collective-permute-start(bf16[2,196,1024]{2,0,1:T(2,128)(2,1)} %param.8), channel_id=1, source_target_pairs={{129,128},{130,129},{131,130},{132,131},{133,132},{134,133},{135,1... | collective-permute-start | bytes 2408456 | tf_op jit(solution)/shard_map/ppermute | solution.py:19
  29.3 13.4 %all-to-all-done = bf16[128,8,384]{2,1,0:T(8,128)(2,1)} async-done(((bf16[128,8,384]{2,1,0:T(8,128)(2,1)}), bf16[128,8,384]{2,1,0:T(8,128)(2,1)}, u32[]{:S(2)}, u32[]{:S(2)}) %all-to-all-start) | async-done | bytes 786464 | tf_op jit(solution)/shard_map/all_to_all | solution.py:27
  42.7 3.6 %collective-permute-start.2 = (bf16[1024,384]{1,0:T(8,128)(2,1)}, bf16[1024,384]{1,0:T(8,128)(2,1)}, u32[]{:S(2)}, u32[]{:S(2)}) collective-permute-start(bf16[1024,384]{1,0:T(8,128)(2,1)} %bitcast.4), channel_id=1, source_target_pairs={{0,128},{128,0},{1,129},{129,1},{2,130},{130,2},{3,131},{131,3},{4... | collective-permute-start | bytes 2359304 | tf_op jit(solution)/shard_map/ppermute | solution.py:28
  46.3 0.8 and_select_fusion.1
  47.1 3.6 %collective-permute-done = bf16[2,196,1024]{2,0,1:T(2,128)(2,1)} collective-permute-done((bf16[2,196,1024]{2,0,1:T(2,128)(2,1)}, bf16[2,196,1024]{2,0,1:T(2,128)(2,1)}, u32[]{:S(2)}, u32[]{:S(2)}) %collective-permute-start) | collective-permute-done | bytes 802848 | tf_op jit(solution)/shard_map/ppermute | solution.py:18
  50.7 0.0 collective-permute-done.1
  50.7 4.4 %fusion.22 = bf16[4,196,1024]{2,0,1:T(4,128)(2,1)S(1)} fusion(bf16[2,196,1024]{2,0,1:T(2,128)(2,1)} %collective-permute-done.1, bf16[2,196,1024]{2,0,1:T(2,128)(2,1)} %param.8, bf16[2,196,1024]{2,0,1:T(2,128)(2,1)} %collective-permute-done, s32[4]{0:T(128)S(1)} %fusion.60), kind=kOutput, calls=%fused_computation.35 | convolution fusion | flops 17661976 | bytes 4014096 | tf_op jit(solution)/shard_map/js,std->jtd/dot_general | solution.py:85
  55.2 0.0 collective-permute-done.2
  55.2 4.1 %convert_reduce_fusion = (f32[4,196]{1,0:T(4,128)S(1)}, bf16[4,196,768]{2,1,0:T(8,128)(2,1)S(1)}) fusion(bf16[1024,384]{1,0:T(8,128)(2,1)} %collective-permute-done.2, bf16[1024,384]{1,0:T(8,128)(2,1)} %bitcast.4, pred[]{:T(512)S(6)} %eq.35, bf16[4,196,1024]{2,0,1:T(4,128)(2,1)S(1)} %fusion.22), kind=kOutput, calls=%fused_computation.11 | convolution fusion | flops 1242008832 | bytes 4385857 | tf_op jit(solution)/shard_map/btd,de->bte/dot_general | solution.py:49
  59.3 1.5 %copy.69 = bf16[4,196,768]{2,0,1:T(4,128)(2,1)} copy(bf16[4,196,768]{2,1,0:T(8,128)(2,1)S(1)} %get-tuple-element.15) | data formatting | bytes 2408448 | tf_op jit(solution)/shard_map/convert_element_type | solution.py:92
  60.8 0.5 fusion.15
  61.3 0.0 copy-done
  61.3 3.4 %convolution_convert_fusion = bf16[4,196,2304]{2,1,0:T(8,128)(2,1)S(1)} fusion(bf16[1,768,2304]{2,1,0:T(8,128)(2,1)S(1)} %copy-done, bf16[4,196,768]{2,1,0:T(8,128)(2,1)S(1)} %get-tuple-element.15, f32[4,196]{1,0:T(4,128)S(1)} %add_rsqrt_fusion.2, f32[4,196]{1,0:T(4,128)S(1)} %broadcast_multiply_fusion.2), kind=kOutput, calls=%fused_computation.6 | convolution fusion | flops 2778746880 | bytes 8362112 | tf_op jit(solution)/shard_map/btd,de->bte/dot_general | solution.py:49
  64.7 0.0 copy-done.4
  64.7 1.9 %fusion.68 = (bf16[4,196,768]{2,1,0:T(8,128)(2,1)}, bf16[4,196,768]{2,1,0:T(8,128)(2,1)}, bf16[4,196,768]{2,1,0:T(8,128)(2,1)}) fusion(bf16[4,196,2304]{2,1,0:T(8,128)(2,1)S(1)} %convolution_convert_fusion), kind=kLoop, calls=%fused_computation.90 | loop fusion | bytes 7225344 | tf_op jit(solution)/shard_map/slice | solution.py:74
  66.6 1.6 %copy.66 = bf16[4,196,768]{1,2,0:T(8,128)(2,1)S(1)} copy(bf16[4,196,768]{2,1,0:T(8,128)(2,1)} %get-tuple-element.7) | data formatting | bytes 2408448 | tf_op jit(solution)/shard_map/slice | solution.py:74
  68.3 2.5 %copy.65 = bf16[4,196,768]{1,2,0:T(8,128)(2,1)} copy(bf16[4,196,768]{2,1,0:T(8,128)(2,1)} %get-tuple-element.8) | data formatting | bytes 2408448 | tf_op jit(solution)/shard_map/slice | solution.py:73
  70.8 2.5 %copy.64 = bf16[4,196,768]{1,2,0:T(8,128)(2,1)} copy(bf16[4,196,768]{2,1,0:T(8,128)(2,1)} %get-tuple-element.9) | data formatting | bytes 2408448 | tf_op jit(solution)/shard_map/slice | solution.py:75
  73.3 0.0 collective-permute-start.3
  73.3 3.6 %fusion = (f32[4,12,196]{2,1,0:T(8,128)S(1)}, f32[4,12,196,196]{2,3,1,0:T(8,128)S(1)}) fusion(bf16[4,196,12,64]{1,3,2,0:T(8,128)(2,1)} %bitcast.66, bf16[4,196,12,64]{1,3,2,0:T(8,128)(2,1)S(1)} %bitcast.65), kind=kOutput, calls=%fused_computation.4 | convolution fusion | flops 239706432 | bytes 9821952 | tf_op jit(solution)/shard_map/bqhd,bkhd->bhqk/dot_general | solution.py:58
  77.0 0.0 copy-done.6
  77.0 0.0 copy-start.5
  77.0 0.0 copy-start.10
  77.0 2.2 %fusion.26 = bf16[4,12,64,196]{3,2,1,0:T(8,128)(2,1)S(1)} fusion(bf16[4,196,12,64]{1,3,2,0:T(8,128)(2,1)S(1)} %bitcast.68, f32[4,12,196,196]{2,3,1,0:T(8,128)S(1)} %get-tuple-element.17, f32[4,12,196]{2,1,0:T(8,128)S(1)} %get-tuple-element.16), kind=kOutput, calls=%fused_computation.38 | convolution fusion | flops 242161920 | bytes 9821952 | tf_op jit(solution)/shard_map/bhqk,bkhd->bqhd/dot_general | solution.py:63
  79.2 0.0 copy-done.5
  79.2 0.0 copy-done.10
  79.2 1.3 %fusion.71 = (f32[4,196]{1,0:T(4,128)S(1)}, f32[4,196,768]{2,1,0:T(8,128)S(1)}) fusion(bf16[4,196,768]{1,2,0:T(8,128)(2,1)S(1)} %bitcast.71, bf16[1,768,768]{2,1,0:T(8,128)(2,1)S(1)} %copy-done.10, bf16[4,196,768]{2,1,0:T(8,128)(2,1)S(1)} %copy-done.5), kind=kOutput, calls=%fused_computation.93 | convolution fusion | flops 926649600 | bytes 5999680 | tf_op jit(solution)/shard_map/btd,de->bte/dot_general | solution.py:49
  80.5 0.0 copy-start.11
  80.6 0.4 multiply_reduce_fusion
  81.0 1.0 copy-done.2
  82.0 0.7 copy-done.11
  82.7 2.3 %convolution_convert_fusion.2 = bf16[4,196,768]{2,1,0:T(8,128)(2,1)} fusion(f32[4,196,768]{2,1,0:T(8,128)S(1)} %get-tuple-element.19, f32[4,196]{1,0:T(4,128)S(1)} %add_rsqrt_fusion.1, f32[4,196]{1,0:T(4,128)S(1)} %broadcast_multiply_fusion.1, bf16[1,768,768]{2,1,0:T(8,128)(2,1)S(1)} %copy-done.11), kind=kOutput, calls=%fused_computation.50 | convolution fusion | flops 927252480 | bytes 4798592 | tf_op jit(solution)/shard_map/btd,de->bte/dot_general | solution.py:49
  84.9 1.6 %copy.76 = bf16[4,196,768]{1,2,0:T(8,128)(2,1)S(1)} copy(bf16[4,196,768]{2,1,0:T(8,128)(2,1)} %convolution_convert_fusion.2) | data formatting | bytes 2408448 | tf_op jit(solution)/shard_map/convert_element_type | solution.py:78
  86.6 0.0 collective-permute-done.3
  86.6 0.5 convert_reduce_fusion.1
  87.1 0.0 copy-start.9
  87.2 1.2 fusion.17
  88.3 0.9 fusion.18
  89.2 0.0 copy-done.9
  89.3 2.1 %convolution_convert_fusion.1 = bf16[4,196,1536]{2,1,0:T(8,128)(2,1)S(1)} fusion(bf16[1,768,1536]{2,1,0:T(8,128)(2,1)S(1)} %copy-done.9, bf16[4,196,768]{2,0,1:T(4,128)(2,1)S(1)} %fusion.18), kind=kOutput, calls=%fused_computation.13 | convolution fusion | flops 1850892288 | bytes 5971968 | tf_op jit(solution)/shard_map/btd,de->bte/dot_general | solution.py:49
  91.3 1.6 %fusion.69 = (bf16[4,196,768]{2,1,0:T(8,128)(2,1)}, bf16[4,196,768]{2,1,0:T(8,128)(2,1)}) fusion(bf16[4,196,1536]{2,1,0:T(8,128)(2,1)S(1)} %convolution_convert_fusion.1), kind=kLoop, calls=%fused_computation.91 | loop fusion | bytes 4816896 | tf_op jit(solution)/shard_map/slice | solution.py:80
  93.0 2.5 %copy.77 = bf16[4,196,768]{1,2,0:T(8,128)(2,1)} copy(bf16[4,196,768]{2,1,0:T(8,128)(2,1)} %get-tuple-element.10) | data formatting | bytes 2408448 | tf_op jit(solution)/shard_map/slice | solution.py:80
  95.5 2.5 %copy.75 = bf16[4,196,768]{1,2,0:T(8,128)(2,1)} copy(bf16[4,196,768]{2,1,0:T(8,128)(2,1)} %get-tuple-element.11) | data formatting | bytes 2408448 | tf_op jit(solution)/shard_map/slice | solution.py:80
  98.0 3.6 %fusion.1 = (f32[4,12,196]{2,1,0:T(8,128)S(1)}, f32[4,12,196,196]{2,3,1,0:T(8,128)S(1)}) fusion(bf16[4,196,12,64]{1,3,2,0:T(8,128)(2,1)S(1)} %bitcast.64, bf16[4,196,12,64]{1,3,2,0:T(8,128)(2,1)} %bitcast.67), kind=kOutput, calls=%fused_computation.5 | convolution fusion | flops 239706432 | bytes 9821952 | tf_op jit(solution)/shard_map/bqhd,bkhd->bhqk/dot_general | solution.py:58
  101.7 0.0 copy-done.7
  101.7 0.0 copy-start.3
  101.7 0.0 copy-start.8
  101.7 2.4 %fusion.25 = bf16[4,12,64,196]{3,2,1,0:T(8,128)(2,1)S(1)} fusion(bf16[4,196,12,64]{1,3,2,0:T(8,128)(2,1)S(1)} %bitcast.69, f32[4,12,196,196]{2,3,1,0:T(8,128)S(1)} %get-tuple-element.21, f32[4,12,196]{2,1,0:T(8,128)S(1)} %get-tuple-element.20), kind=kOutput, calls=%fused_computation.37 | convolution fusion | flops 242161920 | bytes 9821952 | tf_op jit(solution)/shard_map/bhqk,bkhd->bqhd/dot_general | solution.py:63
  104.1 0.0 copy-done.3
  104.1 0.0 copy-done.8
  104.1 1.2 convolution_add_fusion
  105.4 3.6 %fusion.72 = (bf16[6,196,768]{2,0,1:T(8,128)(2,1)S(1)}, f32[6,196,768]{2,0,1:T(8,128)S(1)}) fusion(f32[4,196,768]{2,1,0:T(8,128)S(1)} %convolution_add_fusion, s32[4]{0:T(128)S(1)} %get-tuple-element.5), kind=kOutput, calls=%fused_computation.94 | convolution fusion | flops 44255256 | bytes 7827472 | tf_op jit(solution)/shard_map/sj,jtd->std/dot_general | solution.py:131
  108.9 0.0 copy-start.1
  108.9 0.8 fusion.70
  109.8 2.1 %collective-permute-start.4 = (bf16[2,196,768]{2,0,1:T(2,128)(2,1)S(1)}, bf16[2,196,768]{2,0,1:T(2,128)(2,1)S(1)}, u32[]{:S(2)}, u32[]{:S(2)}) collective-permute-start(bf16[2,196,768]{2,0,1:T(2,128)(2,1)S(1)} %get-tuple-element.12), channel_id=1, source_target_pairs={{128,129},{129,130},{130,131},{131,132},{132,133},{133,134},{134,1... | collective-permute-start | bytes 1806344 | tf_op jit(solution)/shard_map/ppermute | solution.py:139
  111.8 8.8 %collective-permute-start.5 = (bf16[2,196,768]{2,0,1:T(2,128)(2,1)S(1)}, bf16[2,196,768]{2,0,1:T(2,128)(2,1)S(1)}, u32[]{:S(2)}, u32[]{:S(2)}) collective-permute-start(bf16[2,196,768]{2,0,1:T(2,128)(2,1)S(1)} %get-tuple-element.13), channel_id=1, source_target_pairs={{129,128},{130,129},{131,130},{132,131},{133,132},{134,133},{135,1... | collective-permute-start | bytes 1806344 | tf_op jit(solution)/shard_map/ppermute | solution.py:140
  120.6 5.5 %collective-permute-done.4 = bf16[2,196,768]{2,0,1:T(2,128)(2,1)S(1)} collective-permute-done((bf16[2,196,768]{2,0,1:T(2,128)(2,1)S(1)}, bf16[2,196,768]{2,0,1:T(2,128)(2,1)S(1)}, u32[]{:S(2)}, u32[]{:S(2)}) %collective-permute-start.4) | collective-permute-done | bytes 602144 | tf_op jit(solution)/shard_map/ppermute | solution.py:139
  126.1 1.5 %collective-permute-done.5 = bf16[2,196,768]{2,0,1:T(2,128)(2,1)S(1)} collective-permute-done((bf16[2,196,768]{2,0,1:T(2,128)(2,1)S(1)}, bf16[2,196,768]{2,0,1:T(2,128)(2,1)S(1)}, u32[]{:S(2)}, u32[]{:S(2)}) %collective-permute-start.5) | collective-permute-done | bytes 602144 | tf_op jit(solution)/shard_map/ppermute | solution.py:140
  127.6 2.2 %fusion.49 = f32[1,2,196,768]{3,1,2,0:T(2,128)} fusion(f32[6,196,768]{2,0,1:T(8,128)S(1)} %get-tuple-element.23, bf16[2,196,768]{2,0,1:T(2,128)(2,1)S(1)} %collective-permute-done.5, bf16[2,196,768]{2,0,1:T(2,128)(2,1)S(1)} %collective-permute-done.4), kind=kLoop, calls=%fused_computation.58 | loop fusion | flops 1204224 | bytes 3612672 | tf_op jit(solution)/shard_map/reshape | solution.py:144
  (12 shorter events, 0.1 us)
Async XLA Ops:
  0.0 61.3 %copy-start = (bf16[1,768,2304]{2,1,0:T(8,128)(2,1)S(1)}, bf16[1,768,2304]{2,1,0:T(8,128)(2,1)}, u32[]{:S(2)}) copy-start(bf16[1,768,2304]{2,1,0:T(8,128)(2,1)} %param.11) | copy-start | bytes 10616836
  1.8 40.9 %all-to-all-start = ((bf16[128,8,384]{2,1,0:T(8,128)(2,1)}), bf16[128,8,384]{2,1,0:T(8,128)(2,1)}, u32[]{:S(2)}, u32[]{:S(2)}) async-start(bf16[128,8,384]{2,1,0:T(8,128)(2,1)} %broadcast_in_dim.2), calls=%async_computation | async-start | bytes 1572864 | tf_op jit(solution)/shard_map/all_to_all | solution.py:27
  18.6 32.1 %collective-permute-start = (bf16[2,196,1024]{2,0,1:T(2,128)(2,1)}, bf16[2,196,1024]{2,0,1:T(2,128)(2,1)}, u32[]{:S(2)}, u32[]{:S(2)}) collective-permute-start(bf16[2,196,1024]{2,0,1:T(2,128)(2,1)} %param.8), channel_id=1, source_target_pairs={{128,129},{129,130},{130,131},{131,132},{132,133},{133,134},{134,1... | collective-permute-start | bytes 2408456 | tf_op jit(solution)/shard_map/ppermute | solution.py:18
  21.0 29.7 %collective-permute-start.1 = (bf16[2,196,1024]{2,0,1:T(2,128)(2,1)}, bf16[2,196,1024]{2,0,1:T(2,128)(2,1)}, u32[]{:S(2)}, u32[]{:S(2)}) collective-permute-start(bf16[2,196,1024]{2,0,1:T(2,128)(2,1)} %param.8), channel_id=1, source_target_pairs={{129,128},{130,129},{131,130},{132,131},{133,132},{134,133},{135,1... | collective-permute-start | bytes 2408456 | tf_op jit(solution)/shard_map/ppermute | solution.py:19
  42.7 12.5 %collective-permute-start.2 = (bf16[1024,384]{1,0:T(8,128)(2,1)}, bf16[1024,384]{1,0:T(8,128)(2,1)}, u32[]{:S(2)}, u32[]{:S(2)}) collective-permute-start(bf16[1024,384]{1,0:T(8,128)(2,1)} %bitcast.4), channel_id=1, source_target_pairs={{0,128},{128,0},{1,129},{129,1},{2,130},{130,2},{3,131},{131,3},{4... | collective-permute-start | bytes 2359304 | tf_op jit(solution)/shard_map/ppermute | solution.py:28
  59.3 5.5 %copy-start.4 = (bf16[4,196,768]{2,1,0:T(8,128)(2,1)}, bf16[4,196,768]{2,1,0:T(8,128)(2,1)S(1)}, u32[]{:S(2)}) copy-start(bf16[4,196,768]{2,1,0:T(8,128)(2,1)S(1)} %get-tuple-element.15) | copy-start | bytes 3612676
  73.3 13.3 %collective-permute-start.3 = (bf16[4,196,768]{2,0,1:T(4,128)(2,1)}, bf16[4,196,768]{2,0,1:T(4,128)(2,1)S(1)}, u32[]{:S(2)}, u32[]{:S(2)}) collective-permute-start(bf16[4,196,768]{2,0,1:T(4,128)(2,1)} %copy.69), channel_id=1, source_target_pairs={{0,128},{128,0},{1,129},{129,1},{2,130},{130,2},{3,131},{131,3},{4... | collective-permute-start | bytes 3612680 | tf_op jit(solution)/shard_map/ppermute | solution.py:37
  73.3 3.7 %copy-start.6 = (bf16[4,196,768]{1,2,0:T(8,128)(2,1)S(1)}, bf16[4,196,768]{1,2,0:T(8,128)(2,1)}, u32[]{:S(2)}) copy-start(bf16[4,196,768]{1,2,0:T(8,128)(2,1)} %copy.64) | copy-start | bytes 3612676
  77.0 2.2 %copy-start.5 = (bf16[4,196,768]{2,1,0:T(8,128)(2,1)S(1)}, bf16[4,196,768]{2,1,0:T(8,128)(2,1)}, u32[]{:S(2)}) copy-start(bf16[4,196,768]{2,1,0:T(8,128)(2,1)} %copy-done.4) | copy-start | bytes 3612676
  77.0 2.2 %copy-start.10 = (bf16[1,768,768]{2,1,0:T(8,128)(2,1)S(1)}, bf16[1,768,768]{2,1,0:T(8,128)(2,1)}, u32[]{:S(2)}) copy-start(bf16[1,768,768]{2,1,0:T(8,128)(2,1)} %param.12) | copy-start | bytes 3538948
  80.5 1.4 %copy-start.2 = (f32[4,196,768]{2,1,0:T(8,128)}, f32[4,196,768]{2,1,0:T(8,128)S(1)}, u32[]{:S(2)}) copy-start(f32[4,196,768]{2,1,0:T(8,128)S(1)} %get-tuple-element.19) | copy-start | bytes 7225348
  80.5 2.1 %copy-start.11 = (bf16[1,768,768]{2,1,0:T(8,128)(2,1)S(1)}, bf16[1,768,768]{2,1,0:T(8,128)(2,1)}, u32[]{:S(2)}) copy-start(bf16[1,768,768]{2,1,0:T(8,128)(2,1)} %param.13) | copy-start | bytes 3538948
  87.1 2.1 %copy-start.9 = (bf16[1,768,1536]{2,1,0:T(8,128)(2,1)S(1)}, bf16[1,768,1536]{2,1,0:T(8,128)(2,1)}, u32[]{:S(2)}) copy-start(bf16[1,768,1536]{2,1,0:T(8,128)(2,1)} %param.14) | copy-start | bytes 7077892
  98.0 3.7 %copy-start.7 = (bf16[4,196,768]{1,2,0:T(8,128)(2,1)S(1)}, bf16[4,196,768]{1,2,0:T(8,128)(2,1)}, u32[]{:S(2)}) copy-start(bf16[4,196,768]{1,2,0:T(8,128)(2,1)} %copy.75) | copy-start | bytes 3612676
  101.7 2.4 %copy-start.3 = (f32[4,196,768]{2,1,0:T(8,128)S(1)}, f32[4,196,768]{2,1,0:T(8,128)}, u32[]{:S(2)}) copy-start(f32[4,196,768]{2,1,0:T(8,128)} %copy-done.2) | copy-start | bytes 7225348
  101.7 2.4 %copy-start.8 = (bf16[1,768,768]{2,1,0:T(8,128)(2,1)S(1)}, bf16[1,768,768]{2,1,0:T(8,128)(2,1)}, u32[]{:S(2)}) copy-start(bf16[1,768,768]{2,1,0:T(8,128)(2,1)} %param.15) | copy-start | bytes 3538948
  108.9 20.9 %copy-start.1 = (bf16[1,768,2304]{2,1,0:T(8,128)(2,1)S(1)}, bf16[1,768,2304]{2,1,0:T(8,128)(2,1)}, u32[]{:S(2)}) copy-start(bf16[1,768,2304]{2,1,0:T(8,128)(2,1)} %param.11) | copy-start | bytes 10616836
  109.8 16.3 %collective-permute-start.4 = (bf16[2,196,768]{2,0,1:T(2,128)(2,1)S(1)}, bf16[2,196,768]{2,0,1:T(2,128)(2,1)S(1)}, u32[]{:S(2)}, u32[]{:S(2)}) collective-permute-start(bf16[2,196,768]{2,0,1:T(2,128)(2,1)S(1)} %get-tuple-element.12), channel_id=1, source_target_pairs={{128,129},{129,130},{130,131},{131,132},{132,133},{133,134},{134,1... | collective-permute-start | bytes 1806344 | tf_op jit(solution)/shard_map/ppermute | solution.py:139
  111.8 15.7 %collective-permute-start.5 = (bf16[2,196,768]{2,0,1:T(2,128)(2,1)S(1)}, bf16[2,196,768]{2,0,1:T(2,128)(2,1)S(1)}, u32[]{:S(2)}, u32[]{:S(2)}) collective-permute-start(bf16[2,196,768]{2,0,1:T(2,128)(2,1)S(1)} %get-tuple-element.13), channel_id=1, source_target_pairs={{129,128},{130,129},{131,130},{132,131},{133,132},{134,133},{135,1... | collective-permute-start | bytes 1806344 | tf_op jit(solution)/shard_map/ppermute | solution.py:140

commit v10 on v9

--- a/solution.py
+++ b/solution.py
@@ -8,16 +8,13 @@
 HEADS = 12
 
 
-def branch_one_padded(x, dim, width):
-    peers, length = (lax.axis_size("pair"), x.shape[dim])
-    base = peers
-    up = [(base + i, base + (i + 1) % peers) for i in range(peers)]
-    down = [(j, i) for i, j in up]
-    last = lax.slice_in_dim(x, length - width, length, axis=dim)
-    initial = lax.slice_in_dim(x, 0, width, axis=dim)
-    before = lax.ppermute(last, ("branch", "pair"), up)
-    after = lax.ppermute(initial, ("branch", "pair"), down)
-    return jnp.concatenate([before, x, after], axis=dim)
+def split_source_padded(x, width):
+    peers, length = (lax.axis_size("pair"), x.shape[0])
+    from_core_zero = [(i, peers + (i + 1) % peers) for i in range(peers)]
+    from_core_one = [(peers + (i + 1) % peers, peers + i) for i in range(peers)]
+    before = lax.ppermute(x[length - width :], ("branch", "pair"), from_core_zero)
+    after = lax.ppermute(x[:width], ("branch", "pair"), from_core_one)
+    return jnp.concatenate([before, x, after], axis=0)
 
 
 def gathered_weight(weight, branch_id, devices):
@@ -112,7 +109,7 @@
     own_onehots = own_place[:, None] == slot_index[None, :]
     full_embed = gathered_weight(embed_weight, branch_id, devices)
     model_width = full_embed.shape[1]
-    window = branch_one_padded(encoder_rows, 0, img_local)
+    window = split_source_padded(encoder_rows, img_local)
     own_list = [embed_picked(own_onehots, window, full_embed)]
     partner_list = [swapped(own_list[0], "branch", 0)]
     local_view = 0

time: 130 us -> 130 us (level)
  waiting for transfers between devices: 23.9 us -> 25.8 us
  starting transfers between devices: 42 us -> 40.1 us
where the time goes in v10:
time: 130 us
  starting transfers between devices  40.1 us (31%)
  matrix products  34.3 us (26%)
  waiting for transfers between devices  25.8 us (20%)
  local copies, waits for them, and re-layouts  22.7 us (17%)
  other arithmetic  6.57 us (5%)
    all_to_all x1, starting transfers between devices, gathered_weight(): got = lax.all_to_all(spread, 'pair', 0, 0, tiled=True).reshape(-1, half)  16.8 us
    dot_general x6, matrix products, project(): jnp.einsum('btd,de->bte', values, matrix, preferred_element_type=jnp.floa...  14.5 us
    all_to_all x1, waiting for transfers between devices, gathered_weight(): got = lax.all_to_all(spread, 'pair', 0, 0, tiled=True).reshape(-1, half)  14.5 us
    ppermute x1, starting transfers between devices, body(): lax.ppermute(slot_sums(0).astype(jnp.bfloat16), ('branch', 'pair'), down)  8.79 us
    ppermute x1, starting transfers between devices, split_source_padded(): after = lax.ppermute(x[:width], ('branch', 'pair'), from_core_one)  8.6 us
    dot_general x2, matrix products, attend(): jnp.einsum('bqhd,bkhd->bhqk', query_heads, key_heads, preferred_element_t...  7.28 us
    ppermute x1, waiting for transfers between devices, body(): lax.ppermute(slot_sums(2 * img_local).astype(jnp.bfloat16), ('branch', 'p...  5.46 us
    dot_general x2, matrix products, attend(): jnp.einsum('bhqk,bkhd->bqhd', attn_probs, value_heads, preferred_element_...  4.53 us
  transfers between devices with their start and end apart: 7, of which 4 were waited for; matrix products, arithmetic and copies ran while one was open for 13% of the time, Pallas kernels for 0%

profile of v10, /device:TPU:1, one launch (start us, length us, event | category | flops | bytes accessed | tf_op | source)
XLA Modules:
  0.0 129.8 jit_solution(5608908400749424686)
XLA Ops:
  0.0 0.0 copy-start
  0.0 0.8 constant_dynamic-slice_fusion
  0.8 0.9 broadcast_in_dim.2
  1.8 16.8 %all-to-all-start = ((bf16[128,8,384]{2,1,0:T(8,128)(2,1)}), bf16[128,8,384]{2,1,0:T(8,128)(2,1)}, u32[]{:S(2)}, u32[]{:S(2)}) async-start(bf16[128,8,384]{2,1,0:T(8,128)(2,1)} %broadcast_in_dim.2), calls=%async_computation | async-start | bytes 1572864 | tf_op jit(solution)/shard_map/all_to_all | solution.py:24
  18.6 1.3 collective-permute-start
  19.9 8.6 %collective-permute-start.1 = (bf16[2,196,1024]{2,0,1:T(2,128)(2,1)}, bf16[2,196,1024]{2,0,1:T(2,128)(2,1)}, u32[]{:S(2)}, u32[]{:S(2)}) collective-permute-start(bf16[2,196,1024]{2,0,1:T(2,128)(2,1)} %param.8), channel_id=1, source_target_pairs={{129,128},{130,129},{131,130},{132,131},{133,132},{134,133},{135,1... | collective-permute-start | bytes 2408456 | tf_op jit(solution)/shard_map/ppermute | solution.py:16
  28.5 14.5 %all-to-all-done = bf16[128,8,384]{2,1,0:T(8,128)(2,1)} async-done(((bf16[128,8,384]{2,1,0:T(8,128)(2,1)}), bf16[128,8,384]{2,1,0:T(8,128)(2,1)}, u32[]{:S(2)}, u32[]{:S(2)}) %all-to-all-start) | async-done | bytes 786464 | tf_op jit(solution)/shard_map/all_to_all | solution.py:24
  43.0 2.6 %collective-permute-start.2 = (bf16[1024,384]{1,0:T(8,128)(2,1)}, bf16[1024,384]{1,0:T(8,128)(2,1)}, u32[]{:S(2)}, u32[]{:S(2)}) collective-permute-start(bf16[1024,384]{1,0:T(8,128)(2,1)} %bitcast.4), channel_id=1, source_target_pairs={{0,128},{128,0},{1,129},{129,1},{2,130},{130,2},{3,131},{131,3},{4... | collective-permute-start | bytes 2359304 | tf_op jit(solution)/shard_map/ppermute | solution.py:25
  45.5 0.8 and_select_fusion.1
  46.3 4.4 %collective-permute-done = bf16[2,196,1024]{2,0,1:T(2,128)(2,1)} collective-permute-done((bf16[2,196,1024]{2,0,1:T(2,128)(2,1)}, bf16[2,196,1024]{2,0,1:T(2,128)(2,1)}, u32[]{:S(2)}, u32[]{:S(2)}) %collective-permute-start) | collective-permute-done | bytes 802848 | tf_op jit(solution)/shard_map/ppermute | solution.py:15
  50.7 0.0 collective-permute-done.1
  50.7 4.4 %fusion.22 = bf16[4,196,1024]{2,0,1:T(4,128)(2,1)S(1)} fusion(bf16[2,196,1024]{2,0,1:T(2,128)(2,1)} %collective-permute-done.1, bf16[2,196,1024]{2,0,1:T(2,128)(2,1)} %param.8, bf16[2,196,1024]{2,0,1:T(2,128)(2,1)} %collective-permute-done, s32[4]{0:T(128)S(1)} %fusion.60), kind=kOutput, calls=%fused_computation.35 | convolution fusion | flops 17661976 | bytes 4014096 | tf_op jit(solution)/shard_map/js,std->jtd/dot_general | solution.py:82
  55.2 0.0 collective-permute-done.2
  55.2 4.1 %convert_reduce_fusion = (f32[4,196]{1,0:T(4,128)S(1)}, bf16[4,196,768]{2,1,0:T(8,128)(2,1)S(1)}) fusion(bf16[1024,384]{1,0:T(8,128)(2,1)} %collective-permute-done.2, bf16[1024,384]{1,0:T(8,128)(2,1)} %bitcast.4, pred[]{:T(512)S(6)} %eq.35, bf16[4,196,1024]{2,0,1:T(4,128)(2,1)S(1)} %fusion.22), kind=kOutput, calls=%fused_computation.11 | convolution fusion | flops 1242008832 | bytes 4385857 | tf_op jit(solution)/shard_map/btd,de->bte/dot_general | solution.py:46
  59.3 1.5 %copy.69 = bf16[4,196,768]{2,0,1:T(4,128)(2,1)} copy(bf16[4,196,768]{2,1,0:T(8,128)(2,1)S(1)} %get-tuple-element.15) | data formatting | bytes 2408448 | tf_op jit(solution)/shard_map/convert_element_type | solution.py:89
  60.8 0.5 fusion.15
  61.3 0.0 copy-done
  61.3 3.4 %convolution_convert_fusion = bf16[4,196,2304]{2,1,0:T(8,128)(2,1)S(1)} fusion(bf16[1,768,2304]{2,1,0:T(8,128)(2,1)S(1)} %copy-done, bf16[4,196,768]{2,1,0:T(8,128)(2,1)S(1)} %get-tuple-element.15, f32[4,196]{1,0:T(4,128)S(1)} %add_rsqrt_fusion.2, f32[4,196]{1,0:T(4,128)S(1)} %broadcast_multiply_fusion.2), kind=kOutput, calls=%fused_computation.6 | convolution fusion | flops 2778746880 | bytes 8362112 | tf_op jit(solution)/shard_map/btd,de->bte/dot_general | solution.py:46
  64.7 0.0 copy-done.4
  64.7 1.9 %fusion.68 = (bf16[4,196,768]{2,1,0:T(8,128)(2,1)}, bf16[4,196,768]{2,1,0:T(8,128)(2,1)}, bf16[4,196,768]{2,1,0:T(8,128)(2,1)}) fusion(bf16[4,196,2304]{2,1,0:T(8,128)(2,1)S(1)} %convolution_convert_fusion), kind=kLoop, calls=%fused_computation.90 | loop fusion | bytes 7225344 | tf_op jit(solution)/shard_map/slice | solution.py:71
  66.6 1.6 %copy.66 = bf16[4,196,768]{1,2,0:T(8,128)(2,1)S(1)} copy(bf16[4,196,768]{2,1,0:T(8,128)(2,1)} %get-tuple-element.7) | data formatting | bytes 2408448 | tf_op jit(solution)/shard_map/slice | solution.py:71
  68.3 2.5 %copy.65 = bf16[4,196,768]{1,2,0:T(8,128)(2,1)} copy(bf16[4,196,768]{2,1,0:T(8,128)(2,1)} %get-tuple-element.8) | data formatting | bytes 2408448 | tf_op jit(solution)/shard_map/slice | solution.py:70
  70.8 2.5 %copy.64 = bf16[4,196,768]{1,2,0:T(8,128)(2,1)} copy(bf16[4,196,768]{2,1,0:T(8,128)(2,1)} %get-tuple-element.9) | data formatting | bytes 2408448 | tf_op jit(solution)/shard_map/slice | solution.py:72
  73.3 0.0 collective-permute-start.3
  73.3 3.6 %fusion = (f32[4,12,196]{2,1,0:T(8,128)S(1)}, f32[4,12,196,196]{2,3,1,0:T(8,128)S(1)}) fusion(bf16[4,196,12,64]{1,3,2,0:T(8,128)(2,1)} %bitcast.66, bf16[4,196,12,64]{1,3,2,0:T(8,128)(2,1)S(1)} %bitcast.65), kind=kOutput, calls=%fused_computation.4 | convolution fusion | flops 239706432 | bytes 9821952 | tf_op jit(solution)/shard_map/bqhd,bkhd->bhqk/dot_general | solution.py:55
  77.0 0.0 copy-done.6
  77.0 0.0 copy-start.5
  77.0 0.0 copy-start.10
  77.0 2.2 %fusion.26 = bf16[4,12,64,196]{3,2,1,0:T(8,128)(2,1)S(1)} fusion(bf16[4,196,12,64]{1,3,2,0:T(8,128)(2,1)S(1)} %bitcast.68, f32[4,12,196,196]{2,3,1,0:T(8,128)S(1)} %get-tuple-element.17, f32[4,12,196]{2,1,0:T(8,128)S(1)} %get-tuple-element.16), kind=kOutput, calls=%fused_computation.38 | convolution fusion | flops 242161920 | bytes 9821952 | tf_op jit(solution)/shard_map/bhqk,bkhd->bqhd/dot_general | solution.py:60
  79.2 0.0 copy-done.5
  79.2 0.0 copy-done.10
  79.2 1.3 %fusion.71 = (f32[4,196]{1,0:T(4,128)S(1)}, f32[4,196,768]{2,1,0:T(8,128)S(1)}) fusion(bf16[4,196,768]{1,2,0:T(8,128)(2,1)S(1)} %bitcast.71, bf16[1,768,768]{2,1,0:T(8,128)(2,1)S(1)} %copy-done.10, bf16[4,196,768]{2,1,0:T(8,128)(2,1)S(1)} %copy-done.5), kind=kOutput, calls=%fused_computation.93 | convolution fusion | flops 926649600 | bytes 5999680 | tf_op jit(solution)/shard_map/btd,de->bte/dot_general | solution.py:46
  80.5 0.0 copy-start.11
  80.6 0.4 multiply_reduce_fusion
  81.0 1.0 copy-done.2
  82.0 0.7 copy-done.11
  82.7 2.3 %convolution_convert_fusion.2 = bf16[4,196,768]{2,1,0:T(8,128)(2,1)} fusion(f32[4,196,768]{2,1,0:T(8,128)S(1)} %get-tuple-element.19, f32[4,196]{1,0:T(4,128)S(1)} %add_rsqrt_fusion.1, f32[4,196]{1,0:T(4,128)S(1)} %broadcast_multiply_fusion.1, bf16[1,768,768]{2,1,0:T(8,128)(2,1)S(1)} %copy-done.11), kind=kOutput, calls=%fused_computation.50 | convolution fusion | flops 927252480 | bytes 4798592 | tf_op jit(solution)/shard_map/btd,de->bte/dot_general | solution.py:46
  84.9 1.6 %copy.76 = bf16[4,196,768]{1,2,0:T(8,128)(2,1)S(1)} copy(bf16[4,196,768]{2,1,0:T(8,128)(2,1)} %convolution_convert_fusion.2) | data formatting | bytes 2408448 | tf_op jit(solution)/shard_map/convert_element_type | solution.py:75
  86.6 0.0 collective-permute-done.3
  86.6 0.5 convert_reduce_fusion.1
  87.1 0.0 copy-start.9
  87.2 1.2 fusion.17
  88.3 0.9 fusion.18
  89.2 0.0 copy-done.9
  89.3 2.1 %convolution_convert_fusion.1 = bf16[4,196,1536]{2,1,0:T(8,128)(2,1)S(1)} fusion(bf16[1,768,1536]{2,1,0:T(8,128)(2,1)S(1)} %copy-done.9, bf16[4,196,768]{2,0,1:T(4,128)(2,1)S(1)} %fusion.18), kind=kOutput, calls=%fused_computation.13 | convolution fusion | flops 1850892288 | bytes 5971968 | tf_op jit(solution)/shard_map/btd,de->bte/dot_general | solution.py:46
  91.3 1.6 %fusion.69 = (bf16[4,196,768]{2,1,0:T(8,128)(2,1)}, bf16[4,196,768]{2,1,0:T(8,128)(2,1)}) fusion(bf16[4,196,1536]{2,1,0:T(8,128)(2,1)S(1)} %convolution_convert_fusion.1), kind=kLoop, calls=%fused_computation.91 | loop fusion | bytes 4816896 | tf_op jit(solution)/shard_map/slice | solution.py:77
  93.0 2.5 %copy.77 = bf16[4,196,768]{1,2,0:T(8,128)(2,1)} copy(bf16[4,196,768]{2,1,0:T(8,128)(2,1)} %get-tuple-element.10) | data formatting | bytes 2408448 | tf_op jit(solution)/shard_map/slice | solution.py:77
  95.5 2.5 %copy.75 = bf16[4,196,768]{1,2,0:T(8,128)(2,1)} copy(bf16[4,196,768]{2,1,0:T(8,128)(2,1)} %get-tuple-element.11) | data formatting | bytes 2408448 | tf_op jit(solution)/shard_map/slice | solution.py:77
  98.0 3.6 %fusion.1 = (f32[4,12,196]{2,1,0:T(8,128)S(1)}, f32[4,12,196,196]{2,3,1,0:T(8,128)S(1)}) fusion(bf16[4,196,12,64]{1,3,2,0:T(8,128)(2,1)S(1)} %bitcast.64, bf16[4,196,12,64]{1,3,2,0:T(8,128)(2,1)} %bitcast.67), kind=kOutput, calls=%fused_computation.5 | convolution fusion | flops 239706432 | bytes 9821952 | tf_op jit(solution)/shard_map/bqhd,bkhd->bhqk/dot_general | solution.py:55
  101.7 0.0 copy-done.7
  101.7 0.0 copy-start.3
  101.7 0.0 copy-start.8
  101.7 2.4 %fusion.25 = bf16[4,12,64,196]{3,2,1,0:T(8,128)(2,1)S(1)} fusion(bf16[4,196,12,64]{1,3,2,0:T(8,128)(2,1)S(1)} %bitcast.69, f32[4,12,196,196]{2,3,1,0:T(8,128)S(1)} %get-tuple-element.21, f32[4,12,196]{2,1,0:T(8,128)S(1)} %get-tuple-element.20), kind=kOutput, calls=%fused_computation.37 | convolution fusion | flops 242161920 | bytes 9821952 | tf_op jit(solution)/shard_map/bhqk,bkhd->bqhd/dot_general | solution.py:60
  104.1 0.0 copy-done.3
  104.1 0.0 copy-done.8
  104.1 1.2 convolution_add_fusion
  105.4 3.6 %fusion.72 = (bf16[6,196,768]{2,0,1:T(8,128)(2,1)S(1)}, f32[6,196,768]{2,0,1:T(8,128)S(1)}) fusion(f32[4,196,768]{2,1,0:T(8,128)S(1)} %convolution_add_fusion, s32[4]{0:T(128)S(1)} %get-tuple-element.5), kind=kOutput, calls=%fused_computation.94 | convolution fusion | flops 44255256 | bytes 7827472 | tf_op jit(solution)/shard_map/sj,jtd->std/dot_general | solution.py:128
  108.9 0.0 copy-start.1
  108.9 0.8 fusion.70
  109.8 2.1 %collective-permute-start.4 = (bf16[2,196,768]{2,0,1:T(2,128)(2,1)S(1)}, bf16[2,196,768]{2,0,1:T(2,128)(2,1)S(1)}, u32[]{:S(2)}, u32[]{:S(2)}) collective-permute-start(bf16[2,196,768]{2,0,1:T(2,128)(2,1)S(1)} %get-tuple-element.12), channel_id=1, source_target_pairs={{128,129},{129,130},{130,131},{131,132},{132,133},{133,134},{134,1... | collective-permute-start | bytes 1806344 | tf_op jit(solution)/shard_map/ppermute | solution.py:136
  111.8 8.8 %collective-permute-start.5 = (bf16[2,196,768]{2,0,1:T(2,128)(2,1)S(1)}, bf16[2,196,768]{2,0,1:T(2,128)(2,1)S(1)}, u32[]{:S(2)}, u32[]{:S(2)}) collective-permute-start(bf16[2,196,768]{2,0,1:T(2,128)(2,1)S(1)} %get-tuple-element.13), channel_id=1, source_target_pairs={{129,128},{130,129},{131,130},{132,131},{133,132},{134,133},{135,1... | collective-permute-start | bytes 1806344 | tf_op jit(solution)/shard_map/ppermute | solution.py:137
  120.6 5.5 %collective-permute-done.4 = bf16[2,196,768]{2,0,1:T(2,128)(2,1)S(1)} collective-permute-done((bf16[2,196,768]{2,0,1:T(2,128)(2,1)S(1)}, bf16[2,196,768]{2,0,1:T(2,128)(2,1)S(1)}, u32[]{:S(2)}, u32[]{:S(2)}) %collective-permute-start.4) | collective-permute-done | bytes 602144 | tf_op jit(solution)/shard_map/ppermute | solution.py:136
  126.1 1.5 %collective-permute-done.5 = bf16[2,196,768]{2,0,1:T(2,128)(2,1)S(1)} collective-permute-done((bf16[2,196,768]{2,0,1:T(2,128)(2,1)S(1)}, bf16[2,196,768]{2,0,1:T(2,128)(2,1)S(1)}, u32[]{:S(2)}, u32[]{:S(2)}) %collective-permute-start.5) | collective-permute-done | bytes 602144 | tf_op jit(solution)/shard_map/ppermute | solution.py:137
  127.6 2.2 %fusion.49 = f32[1,2,196,768]{3,1,2,0:T(2,128)} fusion(f32[6,196,768]{2,0,1:T(8,128)S(1)} %get-tuple-element.23, bf16[2,196,768]{2,0,1:T(2,128)(2,1)S(1)} %collective-permute-done.5, bf16[2,196,768]{2,0,1:T(2,128)(2,1)S(1)} %collective-permute-done.4), kind=kLoop, calls=%fused_computation.58 | loop fusion | flops 1204224 | bytes 3612672 | tf_op jit(solution)/shard_map/reshape | solution.py:141
  (12 shorter events, 0.1 us)
Async XLA Ops:
  0.0 61.3 %copy-start = (bf16[1,768,2304]{2,1,0:T(8,128)(2,1)S(1)}, bf16[1,768,2304]{2,1,0:T(8,128)(2,1)}, u32[]{:S(2)}) copy-start(bf16[1,768,2304]{2,1,0:T(8,128)(2,1)} %param.11) | copy-start | bytes 10616836
  1.8 41.2 %all-to-all-start = ((bf16[128,8,384]{2,1,0:T(8,128)(2,1)}), bf16[128,8,384]{2,1,0:T(8,128)(2,1)}, u32[]{:S(2)}, u32[]{:S(2)}) async-start(bf16[128,8,384]{2,1,0:T(8,128)(2,1)} %broadcast_in_dim.2), calls=%async_computation | async-start | bytes 1572864 | tf_op jit(solution)/shard_map/all_to_all | solution.py:24
  18.6 32.1 %collective-permute-start = (bf16[2,196,1024]{2,0,1:T(2,128)(2,1)}, bf16[2,196,1024]{2,0,1:T(2,128)(2,1)}, u32[]{:S(2)}, u32[]{:S(2)}) collective-permute-start(bf16[2,196,1024]{2,0,1:T(2,128)(2,1)} %param.8), channel_id=1, source_target_pairs={{0,129},{1,130},{2,131},{3,132},{4,133},{5,134},{6,135},{7,136},{8... | collective-permute-start | bytes 2408456 | tf_op jit(solution)/shard_map/ppermute | solution.py:15
  19.9 30.8 %collective-permute-start.1 = (bf16[2,196,1024]{2,0,1:T(2,128)(2,1)}, bf16[2,196,1024]{2,0,1:T(2,128)(2,1)}, u32[]{:S(2)}, u32[]{:S(2)}) collective-permute-start(bf16[2,196,1024]{2,0,1:T(2,128)(2,1)} %param.8), channel_id=1, source_target_pairs={{129,128},{130,129},{131,130},{132,131},{133,132},{134,133},{135,1... | collective-permute-start | bytes 2408456 | tf_op jit(solution)/shard_map/ppermute | solution.py:16
  43.0 12.2 %collective-permute-start.2 = (bf16[1024,384]{1,0:T(8,128)(2,1)}, bf16[1024,384]{1,0:T(8,128)(2,1)}, u32[]{:S(2)}, u32[]{:S(2)}) collective-permute-start(bf16[1024,384]{1,0:T(8,128)(2,1)} %bitcast.4), channel_id=1, source_target_pairs={{0,128},{128,0},{1,129},{129,1},{2,130},{130,2},{3,131},{131,3},{4... | collective-permute-start | bytes 2359304 | tf_op jit(solution)/shard_map/ppermute | solution.py:25
  59.3 5.5 %copy-start.4 = (bf16[4,196,768]{2,1,0:T(8,128)(2,1)}, bf16[4,196,768]{2,1,0:T(8,128)(2,1)S(1)}, u32[]{:S(2)}) copy-start(bf16[4,196,768]{2,1,0:T(8,128)(2,1)S(1)} %get-tuple-element.15) | copy-start | bytes 3612676
  73.3 13.3 %collective-permute-start.3 = (bf16[4,196,768]{2,0,1:T(4,128)(2,1)}, bf16[4,196,768]{2,0,1:T(4,128)(2,1)S(1)}, u32[]{:S(2)}, u32[]{:S(2)}) collective-permute-start(bf16[4,196,768]{2,0,1:T(4,128)(2,1)} %copy.69), channel_id=1, source_target_pairs={{0,128},{128,0},{1,129},{129,1},{2,130},{130,2},{3,131},{131,3},{4... | collective-permute-start | bytes 3612680 | tf_op jit(solution)/shard_map/ppermute | solution.py:34
  73.3 3.7 %copy-start.6 = (bf16[4,196,768]{1,2,0:T(8,128)(2,1)S(1)}, bf16[4,196,768]{1,2,0:T(8,128)(2,1)}, u32[]{:S(2)}) copy-start(bf16[4,196,768]{1,2,0:T(8,128)(2,1)} %copy.64) | copy-start | bytes 3612676
  77.0 2.2 %copy-start.5 = (bf16[4,196,768]{2,1,0:T(8,128)(2,1)S(1)}, bf16[4,196,768]{2,1,0:T(8,128)(2,1)}, u32[]{:S(2)}) copy-start(bf16[4,196,768]{2,1,0:T(8,128)(2,1)} %copy-done.4) | copy-start | bytes 3612676
  77.0 2.2 %copy-start.10 = (bf16[1,768,768]{2,1,0:T(8,128)(2,1)S(1)}, bf16[1,768,768]{2,1,0:T(8,128)(2,1)}, u32[]{:S(2)}) copy-start(bf16[1,768,768]{2,1,0:T(8,128)(2,1)} %param.12) | copy-start | bytes 3538948
  80.5 1.4 %copy-start.2 = (f32[4,196,768]{2,1,0:T(8,128)}, f32[4,196,768]{2,1,0:T(8,128)S(1)}, u32[]{:S(2)}) copy-start(f32[4,196,768]{2,1,0:T(8,128)S(1)} %get-tuple-element.19) | copy-start | bytes 7225348
  80.5 2.1 %copy-start.11 = (bf16[1,768,768]{2,1,0:T(8,128)(2,1)S(1)}, bf16[1,768,768]{2,1,0:T(8,128)(2,1)}, u32[]{:S(2)}) copy-start(bf16[1,768,768]{2,1,0:T(8,128)(2,1)} %param.13) | copy-start | bytes 3538948
  87.1 2.1 %copy-start.9 = (bf16[1,768,1536]{2,1,0:T(8,128)(2,1)S(1)}, bf16[1,768,1536]{2,1,0:T(8,128)(2,1)}, u32[]{:S(2)}) copy-start(bf16[1,768,1536]{2,1,0:T(8,128)(2,1)} %param.14) | copy-start | bytes 7077892
  98.0 3.7 %copy-start.7 = (bf16[4,196,768]{1,2,0:T(8,128)(2,1)S(1)}, bf16[4,196,768]{1,2,0:T(8,128)(2,1)}, u32[]{:S(2)}) copy-start(bf16[4,196,768]{1,2,0:T(8,128)(2,1)} %copy.75) | copy-start | bytes 3612676
  101.7 2.4 %copy-start.3 = (f32[4,196,768]{2,1,0:T(8,128)S(1)}, f32[4,196,768]{2,1,0:T(8,128)}, u32[]{:S(2)}) copy-start(f32[4,196,768]{2,1,0:T(8,128)} %copy-done.2) | copy-start | bytes 7225348
  101.7 2.4 %copy-start.8 = (bf16[1,768,768]{2,1,0:T(8,128)(2,1)S(1)}, bf16[1,768,768]{2,1,0:T(8,128)(2,1)}, u32[]{:S(2)}) copy-start(bf16[1,768,768]{2,1,0:T(8,128)(2,1)} %param.15) | copy-start | bytes 3538948
  108.9 20.9 %copy-start.1 = (bf16[1,768,2304]{2,1,0:T(8,128)(2,1)S(1)}, bf16[1,768,2304]{2,1,0:T(8,128)(2,1)}, u32[]{:S(2)}) copy-start(bf16[1,768,2304]{2,1,0:T(8,128)(2,1)} %param.11) | copy-start | bytes 10616836
  109.8 16.3 %collective-permute-start.4 = (bf16[2,196,768]{2,0,1:T(2,128)(2,1)S(1)}, bf16[2,196,768]{2,0,1:T(2,128)(2,1)S(1)}, u32[]{:S(2)}, u32[]{:S(2)}) collective-permute-start(bf16[2,196,768]{2,0,1:T(2,128)(2,1)S(1)} %get-tuple-element.12), channel_id=1, source_target_pairs={{128,129},{129,130},{130,131},{131,132},{132,133},{133,134},{134,1... | collective-permute-start | bytes 1806344 | tf_op jit(solution)/shard_map/ppermute | solution.py:136
  111.8 15.7 %collective-permute-start.5 = (bf16[2,196,768]{2,0,1:T(2,128)(2,1)S(1)}, bf16[2,196,768]{2,0,1:T(2,128)(2,1)S(1)}, u32[]{:S(2)}, u32[]{:S(2)}) collective-permute-start(bf16[2,196,768]{2,0,1:T(2,128)(2,1)S(1)} %get-tuple-element.13), channel_id=1, source_target_pairs={{129,128},{130,129},{131,130},{132,131},{133,132},{134,133},{135,1... | collective-permute-start | bytes 1806344 | tf_op jit(solution)/shard_map/ppermute | solution.py:137

commit v11 on v10

--- a/solution.py
+++ b/solution.py
@@ -125,7 +125,10 @@
     place = own_places[local_view]
 
     chosen = (slot_index[:, None] == place[None, :]).astype(jnp.float32)
-    contributions = jnp.einsum("sj,jtd->std", chosen, decoded, precision=lax.Precision.HIGHEST)
+    contributions = sum(
+        jnp.where(chosen[:, j, None, None] > 0, decoded[j][None], 0.0)
+        for j in range(decoded.shape[0])
+    )
 
     def slot_sums(first):
         return contributions[first : first + img_local]

time: 130 us -> 128 us (0.985)
  matrix products: 34.3 us -> 30.2 us
  other arithmetic: 6.57 us -> 8.42 us
    dot_general x1 -> x0, matrix products: 3.57 us -> none  [body(): jnp.einsum('sj,jtd->std', chosen, decoded, precision=lax.Precision.HIGHEST)]
    another operation x0 -> x1, other arithmetic: none -> 1.76 us
where the time goes in v11:
time: 128 us
  starting transfers between devices  40.1 us (31%)
  matrix products  30.2 us (24%)
  waiting for transfers between devices  25.7 us (20%)
  local copies, waits for them, and re-layouts  22.9 us (18%)
  other arithmetic  8.42 us (7%)
    all_to_all x1, starting transfers between devices, gathered_weight(): got = lax.all_to_all(spread, 'pair', 0, 0, tiled=True).reshape(-1, half)  16.8 us
    dot_general x6, matrix products, project(): jnp.einsum('btd,de->bte', values, matrix, preferred_element_type=jnp.floa...  14 us
    all_to_all x1, waiting for transfers between devices, gathered_weight(): got = lax.all_to_all(spread, 'pair', 0, 0, tiled=True).reshape(-1, half)  13.7 us
    ppermute x1, starting transfers between devices, body(): lax.ppermute(slot_sums(0).astype(jnp.bfloat16), ('branch', 'pair'), down)  8.79 us
    ppermute x1, starting transfers between devices, split_source_padded(): after = lax.ppermute(x[:width], ('branch', 'pair'), from_core_one)  8.6 us
    dot_general x2, matrix products, attend(): jnp.einsum('bqhd,bkhd->bhqk', query_heads, key_heads, preferred_element_t...  7.27 us
    ppermute x1, waiting for transfers between devices, body(): lax.ppermute(slot_sums(2 * img_local).astype(jnp.bfloat16), ('branch', 'p...  5.46 us
    ppermute x1, waiting for transfers between devices, split_source_padded(): lax.ppermute(x[length - width:], ('branch', 'pair'), from_core_zero)  5.11 us
  transfers between devices with their start and end apart: 7, of which 4 were waited for; matrix products, arithmetic and copies ran while one was open for 13% of the time, Pallas kernels for 0%

profile of v11, /device:TPU:1, one launch (start us, length us, event | category | flops | bytes accessed | tf_op | source)
XLA Modules:
  0.0 127.7 jit_solution(3862162919532376206)
XLA Ops:
  0.0 0.0 copy-start
  0.0 0.8 constant_dynamic-slice_fusion
  0.8 0.9 broadcast_in_dim.80
  1.8 16.8 %all-to-all-start = ((bf16[128,8,384]{2,1,0:T(8,128)(2,1)}), bf16[128,8,384]{2,1,0:T(8,128)(2,1)}, u32[]{:S(2)}, u32[]{:S(2)}) async-start(bf16[128,8,384]{2,1,0:T(8,128)(2,1)} %broadcast_in_dim.80), calls=%async_computation | async-start | bytes 1572864 | tf_op jit(solution)/shard_map/all_to_all | solution.py:24
  18.6 1.3 %collective-permute-start = (bf16[2,196,1024]{2,0,1:T(2,128)(2,1)}, bf16[2,196,1024]{2,0,1:T(2,128)(2,1)}, u32[]{:S(2)}, u32[]{:S(2)}) collective-permute-start(bf16[2,196,1024]{2,0,1:T(2,128)(2,1)} %param.8), channel_id=1, source_target_pairs={{0,129},{1,130},{2,131},{3,132},{4,133},{5,134},{6,135},{7,136},{8... | collective-permute-start | bytes 2408456 | tf_op jit(solution)/shard_map/ppermute | solution.py:15
  19.9 8.6 %collective-permute-start.1 = (bf16[2,196,1024]{2,0,1:T(2,128)(2,1)}, bf16[2,196,1024]{2,0,1:T(2,128)(2,1)}, u32[]{:S(2)}, u32[]{:S(2)}) collective-permute-start(bf16[2,196,1024]{2,0,1:T(2,128)(2,1)} %param.8), channel_id=1, source_target_pairs={{129,128},{130,129},{131,130},{132,131},{133,132},{134,133},{135,1... | collective-permute-start | bytes 2408456 | tf_op jit(solution)/shard_map/ppermute | solution.py:16
  28.5 0.8 and_select_fusion.1
  29.3 13.7 %all-to-all-done = bf16[128,8,384]{2,1,0:T(8,128)(2,1)} async-done(((bf16[128,8,384]{2,1,0:T(8,128)(2,1)}), bf16[128,8,384]{2,1,0:T(8,128)(2,1)}, u32[]{:S(2)}, u32[]{:S(2)}) %all-to-all-start) | async-done | bytes 786464 | tf_op jit(solution)/shard_map/all_to_all | solution.py:24
  43.0 2.6 %collective-permute-start.2 = (bf16[1024,384]{1,0:T(8,128)(2,1)}, bf16[1024,384]{1,0:T(8,128)(2,1)S(1)}, u32[]{:S(2)}, u32[]{:S(2)}) collective-permute-start(bf16[1024,384]{1,0:T(8,128)(2,1)} %bitcast.4), channel_id=1, source_target_pairs={{0,128},{128,0},{1,129},{129,1},{2,130},{130,2},{3,131},{131,3},{4... | collective-permute-start | bytes 2359304 | tf_op jit(solution)/shard_map/ppermute | solution.py:25
  45.5 0.1 fusion.51
  45.6 5.1 %collective-permute-done = bf16[2,196,1024]{2,0,1:T(2,128)(2,1)} collective-permute-done((bf16[2,196,1024]{2,0,1:T(2,128)(2,1)}, bf16[2,196,1024]{2,0,1:T(2,128)(2,1)}, u32[]{:S(2)}, u32[]{:S(2)}) %collective-permute-start) | collective-permute-done | bytes 802848 | tf_op jit(solution)/shard_map/ppermute | solution.py:15
  50.7 0.0 collective-permute-done.1
  50.7 4.4 %fusion.20 = bf16[4,196,1024]{2,0,1:T(4,128)(2,1)S(1)} fusion(bf16[2,196,1024]{2,0,1:T(2,128)(2,1)} %collective-permute-done.1, bf16[2,196,1024]{2,0,1:T(2,128)(2,1)} %param.8, bf16[2,196,1024]{2,0,1:T(2,128)(2,1)} %collective-permute-done, s32[4]{0:T(128)S(1)} %fusion.56), kind=kOutput, calls=%fused_computation.34 | convolution fusion | flops 17661976 | bytes 4014096 | tf_op jit(solution)/shard_map/js,std->jtd/dot_general | solution.py:82
  55.2 0.0 collective-permute-done.2
  55.2 3.6 %convert_reduce_fusion = (f32[4,196]{1,0:T(4,128)S(1)}, bf16[4,196,768]{2,1,0:T(8,128)(2,1)S(1)}) fusion(bf16[1024,384]{1,0:T(8,128)(2,1)S(1)} %collective-permute-done.2, bf16[1024,384]{1,0:T(8,128)(2,1)} %bitcast.4, pred[]{:T(512)S(6)} %eq.35, bf16[4,196,1024]{2,0,1:T(4,128)(2,1)S(1)} %fusion.20), kind=kOutput, calls=%fused_computation.12 | convolution fusion | flops 1242008832 | bytes 4385857 | tf_op jit(solution)/shard_map/btd,de->bte/dot_general | solution.py:46
  58.8 1.5 %copy.67 = bf16[4,196,768]{2,0,1:T(4,128)(2,1)} copy(bf16[4,196,768]{2,1,0:T(8,128)(2,1)S(1)} %get-tuple-element.25) | data formatting | bytes 2408448 | tf_op jit(solution)/shard_map/convert_element_type | solution.py:89
  60.3 0.5 fusion.15
  60.8 0.0 copy-done
  60.8 3.4 %convolution_convert_fusion = bf16[4,196,2304]{2,1,0:T(8,128)(2,1)S(1)} fusion(bf16[1,768,2304]{2,1,0:T(8,128)(2,1)S(1)} %copy-done, bf16[4,196,768]{2,1,0:T(8,128)(2,1)S(1)} %get-tuple-element.25, f32[4,196]{1,0:T(4,128)S(1)} %add_rsqrt_fusion.2, f32[4,196]{1,0:T(4,128)S(1)} %broadcast_multiply_fusion.2), kind=kOutput, calls=%fused_computation.6 | convolution fusion | flops 2778746880 | bytes 8362112 | tf_op jit(solution)/shard_map/btd,de->bte/dot_general | solution.py:46
  64.2 0.0 copy-done.4
  64.3 1.9 %fusion.65 = (bf16[4,196,768]{2,1,0:T(8,128)(2,1)}, bf16[4,196,768]{2,1,0:T(8,128)(2,1)}, bf16[4,196,768]{2,1,0:T(8,128)(2,1)}) fusion(bf16[4,196,2304]{2,1,0:T(8,128)(2,1)S(1)} %convolution_convert_fusion), kind=kLoop, calls=%fused_computation.97 | loop fusion | bytes 7225344 | tf_op jit(solution)/shard_map/slice | solution.py:71
  66.1 1.6 %copy.64 = bf16[4,196,768]{1,2,0:T(8,128)(2,1)S(1)} copy(bf16[4,196,768]{2,1,0:T(8,128)(2,1)} %get-tuple-element.7) | data formatting | bytes 2408448 | tf_op jit(solution)/shard_map/slice | solution.py:71
  67.8 2.5 %copy.63 = bf16[4,196,768]{1,2,0:T(8,128)(2,1)} copy(bf16[4,196,768]{2,1,0:T(8,128)(2,1)} %get-tuple-element.8) | data formatting | bytes 2408448 | tf_op jit(solution)/shard_map/slice | solution.py:70
  70.3 2.5 %copy.62 = bf16[4,196,768]{1,2,0:T(8,128)(2,1)} copy(bf16[4,196,768]{2,1,0:T(8,128)(2,1)} %get-tuple-element.9) | data formatting | bytes 2408448 | tf_op jit(solution)/shard_map/slice | solution.py:72
  72.8 0.0 collective-permute-start.3
  72.8 3.6 %fusion = (f32[4,12,196]{2,1,0:T(8,128)S(1)}, f32[4,12,196,196]{2,3,1,0:T(8,128)S(1)}) fusion(bf16[4,196,12,64]{1,3,2,0:T(8,128)(2,1)} %bitcast.77, bf16[4,196,12,64]{1,3,2,0:T(8,128)(2,1)S(1)} %bitcast.76), kind=kOutput, calls=%fused_computation.4 | convolution fusion | flops 239706432 | bytes 9821952 | tf_op jit(solution)/shard_map/bqhd,bkhd->bhqk/dot_general | solution.py:55
  76.5 0.0 copy-done.6
  76.5 0.0 copy-start.5
  76.5 0.0 copy-start.10
  76.5 2.2 %fusion.24 = bf16[4,12,64,196]{3,2,1,0:T(8,128)(2,1)S(1)} fusion(bf16[4,196,12,64]{1,3,2,0:T(8,128)(2,1)S(1)} %bitcast.79, f32[4,12,196,196]{2,3,1,0:T(8,128)S(1)} %get-tuple-element.27, f32[4,12,196]{2,1,0:T(8,128)S(1)} %get-tuple-element.26), kind=kOutput, calls=%fused_computation.37 | convolution fusion | flops 242161920 | bytes 9821952 | tf_op jit(solution)/shard_map/bhqk,bkhd->bqhd/dot_general | solution.py:60
  78.7 0.0 copy-done.5
  78.7 0.0 copy-done.10
  78.7 1.3 %fusion.68 = (f32[4,196]{1,0:T(4,128)S(1)}, f32[4,196,768]{2,1,0:T(8,128)S(1)}) fusion(bf16[4,196,768]{1,2,0:T(8,128)(2,1)S(1)} %bitcast.82, bf16[1,768,768]{2,1,0:T(8,128)(2,1)S(1)} %copy-done.10, bf16[4,196,768]{2,1,0:T(8,128)(2,1)S(1)} %copy-done.5), kind=kOutput, calls=%fused_computation.100 | convolution fusion | flops 926649600 | bytes 5999680 | tf_op jit(solution)/shard_map/btd,de->bte/dot_general | solution.py:46
  80.0 0.0 copy-start.11
  80.1 0.4 multiply_reduce_fusion
  80.5 1.0 copy-done.2
  81.5 0.7 copy-done.11
  82.2 2.3 %convolution_convert_fusion.2 = bf16[4,196,768]{2,1,0:T(8,128)(2,1)} fusion(f32[4,196,768]{2,1,0:T(8,128)S(1)} %get-tuple-element.29, f32[4,196]{1,0:T(4,128)S(1)} %add_rsqrt_fusion.1, f32[4,196]{1,0:T(4,128)S(1)} %broadcast_multiply_fusion.1, bf16[1,768,768]{2,1,0:T(8,128)(2,1)S(1)} %copy-done.11), kind=kOutput, calls=%fused_computation.49 | convolution fusion | flops 927252480 | bytes 4798592 | tf_op jit(solution)/shard_map/btd,de->bte/dot_general | solution.py:46
  84.4 1.6 %copy.74 = bf16[4,196,768]{1,2,0:T(8,128)(2,1)S(1)} copy(bf16[4,196,768]{2,1,0:T(8,128)(2,1)} %convolution_convert_fusion.2) | data formatting | bytes 2408448 | tf_op jit(solution)/shard_map/convert_element_type | solution.py:75
  86.1 0.0 collective-permute-done.3
  86.1 0.5 convert_reduce_fusion.1
  86.6 0.0 copy-start.9
  86.7 1.2 fusion.17
  87.8 0.9 fusion.18
  88.8 2.1 %convolution_convert_fusion.1 = bf16[4,196,1536]{2,1,0:T(8,128)(2,1)S(1)} fusion(bf16[1,768,1536]{2,1,0:T(8,128)(2,1)S(1)} %copy-done.9, bf16[4,196,768]{2,0,1:T(4,128)(2,1)S(1)} %fusion.18), kind=kOutput, calls=%fused_computation.14 | convolution fusion | flops 1850892288 | bytes 5971968 | tf_op jit(solution)/shard_map/btd,de->bte/dot_general | solution.py:46
  90.9 1.6 %fusion.66 = (bf16[4,196,768]{2,1,0:T(8,128)(2,1)}, bf16[4,196,768]{2,1,0:T(8,128)(2,1)}) fusion(bf16[4,196,1536]{2,1,0:T(8,128)(2,1)S(1)} %convolution_convert_fusion.1), kind=kLoop, calls=%fused_computation.98 | loop fusion | bytes 4816896 | tf_op jit(solution)/shard_map/slice | solution.py:77
  92.4 2.5 %copy.75 = bf16[4,196,768]{1,2,0:T(8,128)(2,1)} copy(bf16[4,196,768]{2,1,0:T(8,128)(2,1)} %get-tuple-element.16) | data formatting | bytes 2408448 | tf_op jit(solution)/shard_map/slice | solution.py:77
  95.0 2.5 %copy.73 = bf16[4,196,768]{1,2,0:T(8,128)(2,1)} copy(bf16[4,196,768]{2,1,0:T(8,128)(2,1)} %get-tuple-element.17) | data formatting | bytes 2408448 | tf_op jit(solution)/shard_map/slice | solution.py:77
  97.5 3.6 %fusion.1 = (f32[4,12,196]{2,1,0:T(8,128)S(1)}, f32[4,12,196,196]{2,3,1,0:T(8,128)S(1)}) fusion(bf16[4,196,12,64]{1,3,2,0:T(8,128)(2,1)S(1)} %bitcast.75, bf16[4,196,12,64]{1,3,2,0:T(8,128)(2,1)} %bitcast.78), kind=kOutput, calls=%fused_computation.5 | convolution fusion | flops 239706432 | bytes 9821952 | tf_op jit(solution)/shard_map/bqhd,bkhd->bhqk/dot_general | solution.py:55
  101.2 0.0 copy-start.8
  101.2 2.4 %fusion.23 = bf16[4,12,64,196]{3,2,1,0:T(8,128)(2,1)S(1)} fusion(bf16[4,196,12,64]{1,3,2,0:T(8,128)(2,1)S(1)} %bitcast.80, f32[4,12,196,196]{2,3,1,0:T(8,128)S(1)} %get-tuple-element.31, f32[4,12,196]{2,1,0:T(8,128)S(1)} %get-tuple-element.30), kind=kOutput, calls=%fused_computation.36 | convolution fusion | flops 242161920 | bytes 9821952 | tf_op jit(solution)/shard_map/bhqk,bkhd->bqhd/dot_general | solution.py:60
  103.6 0.0 copy-done.3
  103.6 0.0 copy-done.8
  103.6 1.2 convolution_add_fusion
  104.9 0.2 slice_bitcast_fusion.3
  105.0 1.8 %fusion.63 = (bf16[6,196,768]{2,0,1:T(8,128)(2,1)S(1)}, f32[6,196,768]{2,0,1:T(8,128)S(1)}) fusion(f32[196,768]{1,0:T(8,128)S(1)} %get-tuple-element.13, pred[6]{0:T(512)(128)(4,1)S(1)} %get-tuple-element.21, f32[196,768]{1,0:T(8,128)S(1)} %get-tuple-element.14, pred[6]{0:T(512)(128)(4,1)S(1)} %get-tuple-element.22, f32[196,768]{1,0:T(8,128)S(1)} %get-tuple-element.15, ...), kind=kLoop, calls=%fused_computation.96 | loop fusion | flops 7225344 | bytes 7827480 | tf_op jit(solution)/shard_map/convert.1
  106.8 0.0 copy-start.1
  106.8 0.8 fusion.67
  107.7 2.1 %collective-permute-start.4 = (bf16[2,196,768]{2,0,1:T(2,128)(2,1)S(1)}, bf16[2,196,768]{2,0,1:T(2,128)(2,1)S(1)}, u32[]{:S(2)}, u32[]{:S(2)}) collective-permute-start(bf16[2,196,768]{2,0,1:T(2,128)(2,1)S(1)} %get-tuple-element.18), channel_id=1, source_target_pairs={{128,129},{129,130},{130,131},{131,132},{132,133},{133,134},{134,1... | collective-permute-start | bytes 1806344 | tf_op jit(solution)/shard_map/ppermute | solution.py:139
  109.7 8.8 %collective-permute-start.5 = (bf16[2,196,768]{2,0,1:T(2,128)(2,1)S(1)}, bf16[2,196,768]{2,0,1:T(2,128)(2,1)S(1)}, u32[]{:S(2)}, u32[]{:S(2)}) collective-permute-start(bf16[2,196,768]{2,0,1:T(2,128)(2,1)S(1)} %get-tuple-element.19), channel_id=1, source_target_pairs={{129,128},{130,129},{131,130},{132,131},{133,132},{134,133},{135,1... | collective-permute-start | bytes 1806344 | tf_op jit(solution)/shard_map/ppermute | solution.py:140
  118.5 5.5 %collective-permute-done.4 = bf16[2,196,768]{2,0,1:T(2,128)(2,1)S(1)} collective-permute-done((bf16[2,196,768]{2,0,1:T(2,128)(2,1)S(1)}, bf16[2,196,768]{2,0,1:T(2,128)(2,1)S(1)}, u32[]{:S(2)}, u32[]{:S(2)}) %collective-permute-start.4) | collective-permute-done | bytes 602144 | tf_op jit(solution)/shard_map/ppermute | solution.py:139
  124.0 1.5 %collective-permute-done.5 = bf16[2,196,768]{2,0,1:T(2,128)(2,1)S(1)} collective-permute-done((bf16[2,196,768]{2,0,1:T(2,128)(2,1)S(1)}, bf16[2,196,768]{2,0,1:T(2,128)(2,1)S(1)}, u32[]{:S(2)}, u32[]{:S(2)}) %collective-permute-start.5) | collective-permute-done | bytes 602144 | tf_op jit(solution)/shard_map/ppermute | solution.py:140
  125.5 2.2 %fusion.47 = f32[1,2,196,768]{3,1,2,0:T(2,128)} fusion(f32[6,196,768]{2,0,1:T(8,128)S(1)} %get-tuple-element.11, bf16[2,196,768]{2,0,1:T(2,128)(2,1)S(1)} %collective-permute-done.5, bf16[2,196,768]{2,0,1:T(2,128)(2,1)S(1)} %collective-permute-done.4), kind=kLoop, calls=%fused_computation.57 | loop fusion | flops 1204224 | bytes 3612672 | tf_op jit(solution)/shard_map/reshape | solution.py:144
  127.7 0.0 copy-done.1
  (15 shorter events, 0.1 us)
Async XLA Ops:
  0.0 60.8 %copy-start = (bf16[1,768,2304]{2,1,0:T(8,128)(2,1)S(1)}, bf16[1,768,2304]{2,1,0:T(8,128)(2,1)}, u32[]{:S(2)}) copy-start(bf16[1,768,2304]{2,1,0:T(8,128)(2,1)} %param.11) | copy-start | bytes 10616836
  1.8 41.2 %all-to-all-start = ((bf16[128,8,384]{2,1,0:T(8,128)(2,1)}), bf16[128,8,384]{2,1,0:T(8,128)(2,1)}, u32[]{:S(2)}, u32[]{:S(2)}) async-start(bf16[128,8,384]{2,1,0:T(8,128)(2,1)} %broadcast_in_dim.80), calls=%async_computation | async-start | bytes 1572864 | tf_op jit(solution)/shard_map/all_to_all | solution.py:24
  18.6 32.1 %collective-permute-start = (bf16[2,196,1024]{2,0,1:T(2,128)(2,1)}, bf16[2,196,1024]{2,0,1:T(2,128)(2,1)}, u32[]{:S(2)}, u32[]{:S(2)}) collective-permute-start(bf16[2,196,1024]{2,0,1:T(2,128)(2,1)} %param.8), channel_id=1, source_target_pairs={{0,129},{1,130},{2,131},{3,132},{4,133},{5,134},{6,135},{7,136},{8... | collective-permute-start | bytes 2408456 | tf_op jit(solution)/shard_map/ppermute | solution.py:15
  19.9 30.8 %collective-permute-start.1 = (bf16[2,196,1024]{2,0,1:T(2,128)(2,1)}, bf16[2,196,1024]{2,0,1:T(2,128)(2,1)}, u32[]{:S(2)}, u32[]{:S(2)}) collective-permute-start(bf16[2,196,1024]{2,0,1:T(2,128)(2,1)} %param.8), channel_id=1, source_target_pairs={{129,128},{130,129},{131,130},{132,131},{133,132},{134,133},{135,1... | collective-permute-start | bytes 2408456 | tf_op jit(solution)/shard_map/ppermute | solution.py:16
  43.0 12.2 %collective-permute-start.2 = (bf16[1024,384]{1,0:T(8,128)(2,1)}, bf16[1024,384]{1,0:T(8,128)(2,1)S(1)}, u32[]{:S(2)}, u32[]{:S(2)}) collective-permute-start(bf16[1024,384]{1,0:T(8,128)(2,1)} %bitcast.4), channel_id=1, source_target_pairs={{0,128},{128,0},{1,129},{129,1},{2,130},{130,2},{3,131},{131,3},{4... | collective-permute-start | bytes 2359304 | tf_op jit(solution)/shard_map/ppermute | solution.py:25
  58.8 5.5 %copy-start.4 = (bf16[4,196,768]{2,1,0:T(8,128)(2,1)}, bf16[4,196,768]{2,1,0:T(8,128)(2,1)S(1)}, u32[]{:S(2)}) copy-start(bf16[4,196,768]{2,1,0:T(8,128)(2,1)S(1)} %get-tuple-element.25) | copy-start | bytes 3612676
  72.8 13.2 %collective-permute-start.3 = (bf16[4,196,768]{2,0,1:T(4,128)(2,1)}, bf16[4,196,768]{2,0,1:T(4,128)(2,1)S(1)}, u32[]{:S(2)}, u32[]{:S(2)}) collective-permute-start(bf16[4,196,768]{2,0,1:T(4,128)(2,1)} %copy.67), channel_id=1, source_target_pairs={{0,128},{128,0},{1,129},{129,1},{2,130},{130,2},{3,131},{131,3},{4... | collective-permute-start | bytes 3612680 | tf_op jit(solution)/shard_map/ppermute | solution.py:34
  72.8 3.6 %copy-start.6 = (bf16[4,196,768]{1,2,0:T(8,128)(2,1)S(1)}, bf16[4,196,768]{1,2,0:T(8,128)(2,1)}, u32[]{:S(2)}) copy-start(bf16[4,196,768]{1,2,0:T(8,128)(2,1)} %copy.62) | copy-start | bytes 3612676
  76.5 2.2 %copy-start.5 = (bf16[4,196,768]{2,1,0:T(8,128)(2,1)S(1)}, bf16[4,196,768]{2,1,0:T(8,128)(2,1)}, u32[]{:S(2)}) copy-start(bf16[4,196,768]{2,1,0:T(8,128)(2,1)} %copy-done.4) | copy-start | bytes 3612676
  76.5 2.2 %copy-start.10 = (bf16[1,768,768]{2,1,0:T(8,128)(2,1)S(1)}, bf16[1,768,768]{2,1,0:T(8,128)(2,1)}, u32[]{:S(2)}) copy-start(bf16[1,768,768]{2,1,0:T(8,128)(2,1)} %param.12) | copy-start | bytes 3538948
  80.0 1.5 %copy-start.2 = (f32[4,196,768]{2,1,0:T(8,128)}, f32[4,196,768]{2,1,0:T(8,128)S(1)}, u32[]{:S(2)}) copy-start(f32[4,196,768]{2,1,0:T(8,128)S(1)} %get-tuple-element.29) | copy-start | bytes 7225348
  80.0 2.1 %copy-start.11 = (bf16[1,768,768]{2,1,0:T(8,128)(2,1)S(1)}, bf16[1,768,768]{2,1,0:T(8,128)(2,1)}, u32[]{:S(2)}) copy-start(bf16[1,768,768]{2,1,0:T(8,128)(2,1)} %param.13) | copy-start | bytes 3538948
  86.6 2.1 %copy-start.9 = (bf16[1,768,1536]{2,1,0:T(8,128)(2,1)S(1)}, bf16[1,768,1536]{2,1,0:T(8,128)(2,1)}, u32[]{:S(2)}) copy-start(bf16[1,768,1536]{2,1,0:T(8,128)(2,1)} %param.14) | copy-start | bytes 7077892
  97.5 3.7 %copy-start.7 = (bf16[4,196,768]{1,2,0:T(8,128)(2,1)S(1)}, bf16[4,196,768]{1,2,0:T(8,128)(2,1)}, u32[]{:S(2)}) copy-start(bf16[4,196,768]{1,2,0:T(8,128)(2,1)} %copy.73) | copy-start | bytes 3612676
  101.2 2.4 %copy-start.3 = (f32[4,196,768]{2,1,0:T(8,128)S(1)}, f32[4,196,768]{2,1,0:T(8,128)}, u32[]{:S(2)}) copy-start(f32[4,196,768]{2,1,0:T(8,128)} %copy-done.2) | copy-start | bytes 7225348
  101.2 2.4 %copy-start.8 = (bf16[1,768,768]{2,1,0:T(8,128)(2,1)S(1)}, bf16[1,768,768]{2,1,0:T(8,128)(2,1)}, u32[]{:S(2)}) copy-start(bf16[1,768,768]{2,1,0:T(8,128)(2,1)} %param.15) | copy-start | bytes 3538948
  106.8 20.9 %copy-start.1 = (bf16[1,768,2304]{2,1,0:T(8,128)(2,1)S(1)}, bf16[1,768,2304]{2,1,0:T(8,128)(2,1)}, u32[]{:S(2)}) copy-start(bf16[1,768,2304]{2,1,0:T(8,128)(2,1)} %param.11) | copy-start | bytes 10616836
  107.7 16.3 %collective-permute-start.4 = (bf16[2,196,768]{2,0,1:T(2,128)(2,1)S(1)}, bf16[2,196,768]{2,0,1:T(2,128)(2,1)S(1)}, u32[]{:S(2)}, u32[]{:S(2)}) collective-permute-start(bf16[2,196,768]{2,0,1:T(2,128)(2,1)S(1)} %get-tuple-element.18), channel_id=1, source_target_pairs={{128,129},{129,130},{130,131},{131,132},{132,133},{133,134},{134,1... | collective-permute-start | bytes 1806344 | tf_op jit(solution)/shard_map/ppermute | solution.py:139
  109.7 15.7 %collective-permute-start.5 = (bf16[2,196,768]{2,0,1:T(2,128)(2,1)S(1)}, bf16[2,196,768]{2,0,1:T(2,128)(2,1)S(1)}, u32[]{:S(2)}, u32[]{:S(2)}) collective-permute-start(bf16[2,196,768]{2,0,1:T(2,128)(2,1)S(1)} %get-tuple-element.19), channel_id=1, source_target_pairs={{129,128},{130,129},{131,130},{132,131},{133,132},{134,133},{135,1... | collective-permute-start | bytes 1806344 | tf_op jit(solution)/shard_map/ppermute | solution.py:140

commit v12 on v11

--- a/solution.py
+++ b/solution.py
@@ -23,9 +23,7 @@
     spread = jnp.broadcast_to(mine[None], (devices,) + mine.shape)
     got = lax.all_to_all(spread, "pair", 0, 0, tiled=True).reshape(-1, half)
     other = lax.ppermute(got, "branch", [(0, 1), (1, 0)])
-    return jnp.where(
-        branch_id == 0, jnp.concatenate([got, other], 1), jnp.concatenate([other, got], 1)
-    )
+    return got, other
 
 
 def swapped(value, axis, bit):
@@ -86,7 +84,12 @@
 
 def embed_picked(onehot, window, full_embed):
     picked = select_rows(onehot, window)
-    return project(picked, full_embed).astype(jnp.bfloat16)
+    got, other, branch_id = full_embed
+    mine = project(picked, got).astype(jnp.bfloat16)
+    theirs = project(picked, other).astype(jnp.bfloat16)
+    return jnp.where(
+        branch_id == 0, jnp.concatenate([mine, theirs], -1), jnp.concatenate([theirs, mine], -1)
+    )
 
 
 def body(encoder_rows, pair_list, embed_weight, self_qkv, self_out, cross_q, cross_kv, cross_out):
@@ -107,8 +110,8 @@
     other_place = jnp.mod(other_ids - window_start, image_total)
     own_places = [own_place]
     own_onehots = own_place[:, None] == slot_index[None, :]
-    full_embed = gathered_weight(embed_weight, branch_id, devices)
-    model_width = full_embed.shape[1]
+    full_embed = gathered_weight(embed_weight, branch_id, devices) + (branch_id,)
+    model_width = 2 * full_embed[0].shape[1]
     window = split_source_padded(encoder_rows, img_local)
     own_list = [embed_picked(own_onehots, window, full_embed)]
     partner_list = [swapped(own_list[0], "branch", 0)]

time: 128 us -> 128 us (level)
  other arithmetic: 8.42 us -> 9.94 us
    convert_element_type x1 -> x0, local copies, waits for them, and re-layouts: 1.49 us -> none  [embed_picked(): return project(picked, full_embed).astype(jnp.bfloat16)]
    select_n x0 -> x1, local copies, waits for them, and re-layouts: none -> 1.49 us  [embed_picked(): jnp.where(branch_id == 0, jnp.concatenate([mine, theirs], -1), jnp.concat...]
    dot_general x6 -> x7, matrix products: 14 us -> 13.7 us  [project(): jnp.einsum('btd,de->bte', values, matrix, preferred_element_type=jnp.floa...]
  transfers between devices with their start and end apart: 7 -> 7, of which waited for: 4 -> 4; matrix products, arithmetic and copies ran while one was open for 13% -> 16% of each run, Pallas kernels for 0% -> 0%
where the time goes in v12:
time: 128 us
  starting transfers between devices  40.1 us (31%)
  matrix products  30 us (23%)
  waiting for transfers between devices  24.6 us (19%)
  local copies, waits for them, and re-layouts  22.9 us (18%)
  other arithmetic  9.94 us (8%)
    all_to_all x1, starting transfers between devices, gathered_weight(): got = lax.all_to_all(spread, 'pair', 0, 0, tiled=True).reshape(-1, half)  16.8 us
    dot_general x7, matrix products, project(): jnp.einsum('btd,de->bte', values, matrix, preferred_element_type=jnp.floa...  13.7 us
    all_to_all x1, waiting for transfers between devices, gathered_weight(): got = lax.all_to_all(spread, 'pair', 0, 0, tiled=True).reshape(-1, half)  13.1 us
    ppermute x1, starting transfers between devices, body(): lax.ppermute(slot_sums(0).astype(jnp.bfloat16), ('branch', 'pair'), down)  8.79 us
    ppermute x1, starting transfers between devices, split_source_padded(): after = lax.ppermute(x[:width], ('branch', 'pair'), from_core_one)  8.6 us
    dot_general x2, matrix products, attend(): jnp.einsum('bqhd,bkhd->bhqk', query_heads, key_heads, preferred_element_t...  7.3 us
    ppermute x1, waiting for transfers between devices, body(): lax.ppermute(slot_sums(2 * img_local).astype(jnp.bfloat16), ('branch', 'p...  5.46 us
    ppermute x1, waiting for transfers between devices, split_source_padded(): lax.ppermute(x[length - width:], ('branch', 'pair'), from_core_zero)  4.57 us
  transfers between devices with their start and end apart: 7, of which 4 were waited for; matrix products, arithmetic and copies ran while one was open for 16% of the time, Pallas kernels for 0%

profile of v12, /device:TPU:1, one launch (start us, length us, event | category | flops | bytes accessed | tf_op | source)
XLA Modules:
  0.0 127.8 jit_solution(8238726972194601807)
XLA Ops:
  0.0 0.0 copy-start
  0.0 0.8 constant_dynamic-slice_fusion
  0.8 0.9 broadcast_in_dim.80
  1.8 16.8 %all-to-all-start = ((bf16[128,8,384]{2,1,0:T(8,128)(2,1)}), bf16[128,8,384]{2,1,0:T(8,128)(2,1)}, u32[]{:S(2)}, u32[]{:S(2)}) async-start(bf16[128,8,384]{2,1,0:T(8,128)(2,1)} %broadcast_in_dim.80), calls=%async_computation | async-start | bytes 1572864 | tf_op jit(solution)/shard_map/all_to_all | solution.py:24
  18.6 1.3 %collective-permute-start = (bf16[2,196,1024]{2,0,1:T(2,128)(2,1)}, bf16[2,196,1024]{2,0,1:T(2,128)(2,1)}, u32[]{:S(2)}, u32[]{:S(2)}) collective-permute-start(bf16[2,196,1024]{2,0,1:T(2,128)(2,1)} %param.8), channel_id=1, source_target_pairs={{0,129},{1,130},{2,131},{3,132},{4,133},{5,134},{6,135},{7,136},{8... | collective-permute-start | bytes 2408456 | tf_op jit(solution)/shard_map/ppermute | solution.py:15
  19.9 8.6 %collective-permute-start.1 = (bf16[2,196,1024]{2,0,1:T(2,128)(2,1)}, bf16[2,196,1024]{2,0,1:T(2,128)(2,1)}, u32[]{:S(2)}, u32[]{:S(2)}) collective-permute-start(bf16[2,196,1024]{2,0,1:T(2,128)(2,1)} %param.8), channel_id=1, source_target_pairs={{129,128},{130,129},{131,130},{132,131},{133,132},{134,133},{135,1... | collective-permute-start | bytes 2408456 | tf_op jit(solution)/shard_map/ppermute | solution.py:16
  28.5 1.3 %and_select_fusion.1 = (s32[4]{0:T(128)S(1)}, s32[4,1]{0,1:T(1,128)}) fusion(s32[]{:T(128)S(6)} %mul.45, s32[4,2]{0,1:T(2,128)} %param.9, pred[]{:T(512)S(6)} %eq.35), kind=kLoop, calls=%fused_computation.82 | loop fusion | flops 52 | bytes 69 | tf_op jit(solution)/shard_map/jit(remainder)/select_n | solution.py:109
  29.8 0.1 fusion.48
  29.9 13.1 %all-to-all-done = bf16[128,8,384]{2,1,0:T(8,128)(2,1)} async-done(((bf16[128,8,384]{2,1,0:T(8,128)(2,1)}), bf16[128,8,384]{2,1,0:T(8,128)(2,1)}, u32[]{:S(2)}, u32[]{:S(2)}) %all-to-all-start) | async-done | bytes 786464 | tf_op jit(solution)/shard_map/all_to_all | solution.py:24
  43.0 2.6 %collective-permute-start.2 = (bf16[1024,384]{1,0:T(8,128)(2,1)}, bf16[1024,384]{1,0:T(8,128)(2,1)S(1)}, u32[]{:S(2)}, u32[]{:S(2)}) collective-permute-start(bf16[1024,384]{1,0:T(8,128)(2,1)} %bitcast.4), channel_id=1, source_target_pairs={{0,128},{128,0},{1,129},{129,1},{2,130},{130,2},{3,131},{131,3},{4... | collective-permute-start | bytes 2359304 | tf_op jit(solution)/shard_map/ppermute | solution.py:25
  45.5 0.6 fusion.53
  46.2 4.6 %collective-permute-done = bf16[2,196,1024]{2,0,1:T(2,128)(2,1)} collective-permute-done((bf16[2,196,1024]{2,0,1:T(2,128)(2,1)}, bf16[2,196,1024]{2,0,1:T(2,128)(2,1)}, u32[]{:S(2)}, u32[]{:S(2)}) %collective-permute-start) | collective-permute-done | bytes 802848 | tf_op jit(solution)/shard_map/ppermute | solution.py:15
  50.7 0.0 collective-permute-done.1
  50.7 4.4 %fusion.20 = bf16[4,196,1024]{2,0,1:T(4,128)(2,1)S(1)} fusion(bf16[2,196,1024]{2,0,1:T(2,128)(2,1)} %collective-permute-done.1, bf16[2,196,1024]{2,0,1:T(2,128)(2,1)} %param.8, bf16[2,196,1024]{2,0,1:T(2,128)(2,1)} %collective-permute-done, s32[4]{0:T(128)S(1)} %fusion.53), kind=kOutput, calls=%fused_computation.34 | convolution fusion | flops 17661976 | bytes 4014096 | tf_op jit(solution)/shard_map/js,std->jtd/dot_general | solution.py:80
  55.2 2.2 %fusion.29 = bf16[4,196,384]{2,1,0:T(8,128)(2,1)S(1)} fusion(bf16[4,196,1024]{2,0,1:T(4,128)(2,1)S(1)} %fusion.20, bf16[128,8,384]{2,1,0:T(8,128)(2,1)} %all-to-all-done), kind=kOutput, calls=%fused_computation.43 | convolution fusion | flops 616863744 | bytes 2994176 | tf_op jit(solution)/shard_map/btd,de->bte/dot_general | solution.py:44
  57.4 0.0 collective-permute-done.2
  57.4 1.1 fusion.32
  58.5 0.4 convert_reduce_fusion
  58.9 1.5 %copy.74 = bf16[4,196,768]{2,0,1:T(4,128)(2,1)} copy(bf16[4,196,768]{2,1,0:T(8,128)(2,1)S(1)} %get-tuple-element.8) | data formatting | bytes 2408448 | tf_op jit(solution)/shard_map/jit(_where)/select_n | solution.py:90
  60.4 0.5 fusion.15
  60.9 0.0 copy-done
  60.9 3.4 %convolution_convert_fusion = bf16[4,196,2304]{2,1,0:T(8,128)(2,1)S(1)} fusion(bf16[1,768,2304]{2,1,0:T(8,128)(2,1)S(1)} %copy-done, bf16[4,196,768]{2,1,0:T(8,128)(2,1)S(1)} %get-tuple-element.8, f32[4,196]{1,0:T(4,128)S(1)} %add_rsqrt_fusion.2, f32[4,196]{1,0:T(4,128)S(1)} %broadcast_multiply_fusion.2), kind=kOutput, calls=%fused_computation.6 | convolution fusion | flops 2778746880 | bytes 8362112 | tf_op jit(solution)/shard_map/btd,de->bte/dot_general | solution.py:44
  64.4 0.0 copy-done.2
  64.4 1.9 %fusion.61 = (bf16[4,196,768]{2,1,0:T(8,128)(2,1)}, bf16[4,196,768]{2,1,0:T(8,128)(2,1)}, bf16[4,196,768]{2,1,0:T(8,128)(2,1)}) fusion(bf16[4,196,2304]{2,1,0:T(8,128)(2,1)S(1)} %convolution_convert_fusion), kind=kLoop, calls=%fused_computation.94 | loop fusion | bytes 7225344 | tf_op jit(solution)/shard_map/slice | solution.py:69
  66.2 1.6 %copy.70 = bf16[4,196,768]{1,2,0:T(8,128)(2,1)S(1)} copy(bf16[4,196,768]{2,1,0:T(8,128)(2,1)} %get-tuple-element.10) | data formatting | bytes 2408448 | tf_op jit(solution)/shard_map/slice | solution.py:68
  67.9 2.5 %copy.71 = bf16[4,196,768]{1,2,0:T(8,128)(2,1)} copy(bf16[4,196,768]{2,1,0:T(8,128)(2,1)} %get-tuple-element.9) | data formatting | bytes 2408448 | tf_op jit(solution)/shard_map/slice | solution.py:69
  70.4 2.5 %copy.69 = bf16[4,196,768]{1,2,0:T(8,128)(2,1)} copy(bf16[4,196,768]{2,1,0:T(8,128)(2,1)} %get-tuple-element.11) | data formatting | bytes 2408448 | tf_op jit(solution)/shard_map/slice | solution.py:70
  73.0 0.0 collective-permute-start.3
  73.0 3.6 %fusion = (f32[4,12,196]{2,1,0:T(8,128)S(1)}, f32[4,12,196,196]{2,3,1,0:T(8,128)S(1)}) fusion(bf16[4,196,12,64]{1,3,2,0:T(8,128)(2,1)S(1)} %bitcast.76, bf16[4,196,12,64]{1,3,2,0:T(8,128)(2,1)} %bitcast.77), kind=kOutput, calls=%fused_computation.4 | convolution fusion | flops 239706432 | bytes 9821952 | tf_op jit(solution)/shard_map/bqhd,bkhd->bhqk/dot_general | solution.py:53
  76.6 0.0 copy-done.6
  76.6 0.0 copy-start.3
  76.6 0.0 copy-start.10
  76.6 2.2 %fusion.24 = bf16[4,12,64,196]{3,2,1,0:T(8,128)(2,1)S(1)} fusion(bf16[4,196,12,64]{1,3,2,0:T(8,128)(2,1)S(1)} %bitcast.79, f32[4,12,196,196]{2,3,1,0:T(8,128)S(1)} %get-tuple-element.27, f32[4,12,196]{2,1,0:T(8,128)S(1)} %get-tuple-element.26), kind=kOutput, calls=%fused_computation.37 | convolution fusion | flops 242161920 | bytes 9821952 | tf_op jit(solution)/shard_map/bhqk,bkhd->bqhd/dot_general | solution.py:58
  78.8 0.0 copy-done.3
  78.8 0.0 copy-done.10
  78.8 1.3 %fusion.64 = (f32[4,196]{1,0:T(4,128)S(1)}, f32[4,196,768]{2,1,0:T(8,128)S(1)}) fusion(bf16[4,196,768]{1,2,0:T(8,128)(2,1)S(1)} %bitcast.82, bf16[1,768,768]{2,1,0:T(8,128)(2,1)S(1)} %copy-done.10, bf16[4,196,768]{2,1,0:T(8,128)(2,1)S(1)} %copy-done.3), kind=kOutput, calls=%fused_computation.97 | convolution fusion | flops 926649600 | bytes 5999680 | tf_op jit(solution)/shard_map/btd,de->bte/dot_general | solution.py:44
  80.2 0.0 copy-start.11
  80.2 0.4 multiply_reduce_fusion
  80.6 1.0 copy-done.4
  81.6 0.7 copy-done.11
  82.3 2.3 %convolution_convert_fusion.2 = bf16[4,196,768]{2,1,0:T(8,128)(2,1)} fusion(f32[4,196,768]{2,1,0:T(8,128)S(1)} %get-tuple-element.29, f32[4,196]{1,0:T(4,128)S(1)} %add_rsqrt_fusion.1, f32[4,196]{1,0:T(4,128)S(1)} %broadcast_multiply_fusion.1, bf16[1,768,768]{2,1,0:T(8,128)(2,1)S(1)} %copy-done.11), kind=kOutput, calls=%fused_computation.38 | convolution fusion | flops 927252480 | bytes 4798592 | tf_op jit(solution)/shard_map/btd,de->bte/dot_general | solution.py:44
  84.6 1.6 %copy.81 = bf16[4,196,768]{1,2,0:T(8,128)(2,1)S(1)} copy(bf16[4,196,768]{2,1,0:T(8,128)(2,1)} %convolution_convert_fusion.2) | data formatting | bytes 2408448 | tf_op jit(solution)/shard_map/convert_element_type | solution.py:73
  86.2 0.0 collective-permute-done.3
  86.2 0.5 convert_reduce_fusion.1
  86.8 0.0 copy-start.9
  86.8 1.2 fusion.17
  88.0 0.9 fusion.18
  88.9 2.1 %convolution_convert_fusion.1 = bf16[4,196,1536]{2,1,0:T(8,128)(2,1)S(1)} fusion(bf16[1,768,1536]{2,1,0:T(8,128)(2,1)S(1)} %copy-done.9, bf16[4,196,768]{2,0,1:T(4,128)(2,1)S(1)} %fusion.18), kind=kOutput, calls=%fused_computation.14 | convolution fusion | flops 1850892288 | bytes 5971968 | tf_op jit(solution)/shard_map/btd,de->bte/dot_general | solution.py:44
  91.0 1.6 %fusion.62 = (bf16[4,196,768]{2,1,0:T(8,128)(2,1)}, bf16[4,196,768]{2,1,0:T(8,128)(2,1)}) fusion(bf16[4,196,1536]{2,1,0:T(8,128)(2,1)S(1)} %convolution_convert_fusion.1), kind=kLoop, calls=%fused_computation.95 | loop fusion | bytes 4816896 | tf_op jit(solution)/shard_map/slice | solution.py:75
  92.6 2.5 %copy.82 = bf16[4,196,768]{1,2,0:T(8,128)(2,1)} copy(bf16[4,196,768]{2,1,0:T(8,128)(2,1)} %get-tuple-element.18) | data formatting | bytes 2408448 | tf_op jit(solution)/shard_map/slice | solution.py:75
  95.1 2.5 %copy.80 = bf16[4,196,768]{1,2,0:T(8,128)(2,1)} copy(bf16[4,196,768]{2,1,0:T(8,128)(2,1)} %get-tuple-element.19) | data formatting | bytes 2408448 | tf_op jit(solution)/shard_map/slice | solution.py:75
  97.7 3.7 %fusion.1 = (f32[4,12,196]{2,1,0:T(8,128)S(1)}, f32[4,12,196,196]{2,3,1,0:T(8,128)S(1)}) fusion(bf16[4,196,12,64]{1,3,2,0:T(8,128)(2,1)S(1)} %bitcast.75, bf16[4,196,12,64]{1,3,2,0:T(8,128)(2,1)} %bitcast.78), kind=kOutput, calls=%fused_computation.5 | convolution fusion | flops 239706432 | bytes 9821952 | tf_op jit(solution)/shard_map/bqhd,bkhd->bhqk/dot_general | solution.py:53
  101.3 0.0 copy-start.8
  101.3 2.4 %fusion.23 = bf16[4,12,64,196]{3,2,1,0:T(8,128)(2,1)S(1)} fusion(bf16[4,196,12,64]{1,3,2,0:T(8,128)(2,1)S(1)} %bitcast.80, f32[4,12,196,196]{2,3,1,0:T(8,128)S(1)} %get-tuple-element.31, f32[4,12,196]{2,1,0:T(8,128)S(1)} %get-tuple-element.30), kind=kOutput, calls=%fused_computation.36 | convolution fusion | flops 242161920 | bytes 9821952 | tf_op jit(solution)/shard_map/bhqk,bkhd->bqhd/dot_general | solution.py:58
  103.7 1.2 convolution_add_fusion
  105.0 0.2 slice_bitcast_fusion.3
  105.2 1.8 %fusion.59 = (bf16[6,196,768]{2,0,1:T(8,128)(2,1)S(1)}, f32[6,196,768]{2,0,1:T(8,128)S(1)}) fusion(f32[196,768]{1,0:T(8,128)S(1)} %get-tuple-element.15, pred[6]{0:T(512)(128)(4,1)S(1)} %get-tuple-element.23, f32[196,768]{1,0:T(8,128)S(1)} %get-tuple-element.16, pred[6]{0:T(512)(128)(4,1)S(1)} %get-tuple-element.24, f32[196,768]{1,0:T(8,128)S(1)} %get-tuple-element.17, ...), kind=kLoop, calls=%fused_computation.93 | loop fusion | flops 7225344 | bytes 7827480 | tf_op jit(solution)/shard_map/convert.1
  106.9 0.0 copy-start.1
  106.9 0.8 fusion.63
  107.8 2.1 %collective-permute-start.4 = (bf16[2,196,768]{2,0,1:T(2,128)(2,1)S(1)}, bf16[2,196,768]{2,0,1:T(2,128)(2,1)S(1)}, u32[]{:S(2)}, u32[]{:S(2)}) collective-permute-start(bf16[2,196,768]{2,0,1:T(2,128)(2,1)S(1)} %get-tuple-element.20), channel_id=1, source_target_pairs={{128,129},{129,130},{130,131},{131,132},{132,133},{133,134},{134,1... | collective-permute-start | bytes 1806344 | tf_op jit(solution)/shard_map/ppermute | solution.py:142
  109.9 8.8 %collective-permute-start.5 = (bf16[2,196,768]{2,0,1:T(2,128)(2,1)S(1)}, bf16[2,196,768]{2,0,1:T(2,128)(2,1)S(1)}, u32[]{:S(2)}, u32[]{:S(2)}) collective-permute-start(bf16[2,196,768]{2,0,1:T(2,128)(2,1)S(1)} %get-tuple-element.21), channel_id=1, source_target_pairs={{129,128},{130,129},{131,130},{132,131},{133,132},{134,133},{135,1... | collective-permute-start | bytes 1806344 | tf_op jit(solution)/shard_map/ppermute | solution.py:143
  118.7 5.5 %collective-permute-done.4 = bf16[2,196,768]{2,0,1:T(2,128)(2,1)S(1)} collective-permute-done((bf16[2,196,768]{2,0,1:T(2,128)(2,1)S(1)}, bf16[2,196,768]{2,0,1:T(2,128)(2,1)S(1)}, u32[]{:S(2)}, u32[]{:S(2)}) %collective-permute-start.4) | collective-permute-done | bytes 602144 | tf_op jit(solution)/shard_map/ppermute | solution.py:142
  124.1 1.5 %collective-permute-done.5 = bf16[2,196,768]{2,0,1:T(2,128)(2,1)S(1)} collective-permute-done((bf16[2,196,768]{2,0,1:T(2,128)(2,1)S(1)}, bf16[2,196,768]{2,0,1:T(2,128)(2,1)S(1)}, u32[]{:S(2)}, u32[]{:S(2)}) %collective-permute-start.5) | collective-permute-done | bytes 602144 | tf_op jit(solution)/shard_map/ppermute | solution.py:143
  125.6 2.2 %fusion.42 = f32[1,2,196,768]{3,1,2,0:T(2,128)} fusion(f32[6,196,768]{2,0,1:T(8,128)S(1)} %get-tuple-element.13, bf16[2,196,768]{2,0,1:T(2,128)(2,1)S(1)} %collective-permute-done.5, bf16[2,196,768]{2,0,1:T(2,128)(2,1)S(1)} %collective-permute-done.4), kind=kLoop, calls=%fused_computation.53 | loop fusion | flops 1204224 | bytes 3612672 | tf_op jit(solution)/shard_map/reshape | solution.py:147
  (17 shorter events, 0.1 us)
Async XLA Ops:
  0.0 60.9 %copy-start = (bf16[1,768,2304]{2,1,0:T(8,128)(2,1)S(1)}, bf16[1,768,2304]{2,1,0:T(8,128)(2,1)}, u32[]{:S(2)}) copy-start(bf16[1,768,2304]{2,1,0:T(8,128)(2,1)} %param.11) | copy-start | bytes 10616836
  1.8 41.2 %all-to-all-start = ((bf16[128,8,384]{2,1,0:T(8,128)(2,1)}), bf16[128,8,384]{2,1,0:T(8,128)(2,1)}, u32[]{:S(2)}, u32[]{:S(2)}) async-start(bf16[128,8,384]{2,1,0:T(8,128)(2,1)} %broadcast_in_dim.80), calls=%async_computation | async-start | bytes 1572864 | tf_op jit(solution)/shard_map/all_to_all | solution.py:24
  18.6 32.1 %collective-permute-start = (bf16[2,196,1024]{2,0,1:T(2,128)(2,1)}, bf16[2,196,1024]{2,0,1:T(2,128)(2,1)}, u32[]{:S(2)}, u32[]{:S(2)}) collective-permute-start(bf16[2,196,1024]{2,0,1:T(2,128)(2,1)} %param.8), channel_id=1, source_target_pairs={{0,129},{1,130},{2,131},{3,132},{4,133},{5,134},{6,135},{7,136},{8... | collective-permute-start | bytes 2408456 | tf_op jit(solution)/shard_map/ppermute | solution.py:15
  19.9 30.8 %collective-permute-start.1 = (bf16[2,196,1024]{2,0,1:T(2,128)(2,1)}, bf16[2,196,1024]{2,0,1:T(2,128)(2,1)}, u32[]{:S(2)}, u32[]{:S(2)}) collective-permute-start(bf16[2,196,1024]{2,0,1:T(2,128)(2,1)} %param.8), channel_id=1, source_target_pairs={{129,128},{130,129},{131,130},{132,131},{133,132},{134,133},{135,1... | collective-permute-start | bytes 2408456 | tf_op jit(solution)/shard_map/ppermute | solution.py:16
  43.0 14.4 %collective-permute-start.2 = (bf16[1024,384]{1,0:T(8,128)(2,1)}, bf16[1024,384]{1,0:T(8,128)(2,1)S(1)}, u32[]{:S(2)}, u32[]{:S(2)}) collective-permute-start(bf16[1024,384]{1,0:T(8,128)(2,1)} %bitcast.4), channel_id=1, source_target_pairs={{0,128},{128,0},{1,129},{129,1},{2,130},{130,2},{3,131},{131,3},{4... | collective-permute-start | bytes 2359304 | tf_op jit(solution)/shard_map/ppermute | solution.py:25
  58.9 5.5 %copy-start.2 = (bf16[4,196,768]{2,1,0:T(8,128)(2,1)}, bf16[4,196,768]{2,1,0:T(8,128)(2,1)S(1)}, u32[]{:S(2)}) copy-start(bf16[4,196,768]{2,1,0:T(8,128)(2,1)S(1)} %get-tuple-element.8) | copy-start | bytes 3612676
  73.0 13.3 %collective-permute-start.3 = (bf16[4,196,768]{2,0,1:T(4,128)(2,1)}, bf16[4,196,768]{2,0,1:T(4,128)(2,1)S(1)}, u32[]{:S(2)}, u32[]{:S(2)}) collective-permute-start(bf16[4,196,768]{2,0,1:T(4,128)(2,1)} %copy.74), channel_id=1, source_target_pairs={{0,128},{128,0},{1,129},{129,1},{2,130},{130,2},{3,131},{131,3},{4... | collective-permute-start | bytes 3612680 | tf_op jit(solution)/shard_map/ppermute | solution.py:32
  73.0 3.7 %copy-start.6 = (bf16[4,196,768]{1,2,0:T(8,128)(2,1)S(1)}, bf16[4,196,768]{1,2,0:T(8,128)(2,1)}, u32[]{:S(2)}) copy-start(bf16[4,196,768]{1,2,0:T(8,128)(2,1)} %copy.69) | copy-start | bytes 3612676
  76.6 2.2 %copy-start.3 = (bf16[4,196,768]{2,1,0:T(8,128)(2,1)S(1)}, bf16[4,196,768]{2,1,0:T(8,128)(2,1)}, u32[]{:S(2)}) copy-start(bf16[4,196,768]{2,1,0:T(8,128)(2,1)} %copy-done.2) | copy-start | bytes 3612676
  76.6 2.2 %copy-start.10 = (bf16[1,768,768]{2,1,0:T(8,128)(2,1)S(1)}, bf16[1,768,768]{2,1,0:T(8,128)(2,1)}, u32[]{:S(2)}) copy-start(bf16[1,768,768]{2,1,0:T(8,128)(2,1)} %param.12) | copy-start | bytes 3538948
  80.2 1.5 %copy-start.4 = (f32[4,196,768]{2,1,0:T(8,128)}, f32[4,196,768]{2,1,0:T(8,128)S(1)}, u32[]{:S(2)}) copy-start(f32[4,196,768]{2,1,0:T(8,128)S(1)} %get-tuple-element.29) | copy-start | bytes 7225348
  80.2 2.1 %copy-start.11 = (bf16[1,768,768]{2,1,0:T(8,128)(2,1)S(1)}, bf16[1,768,768]{2,1,0:T(8,128)(2,1)}, u32[]{:S(2)}) copy-start(bf16[1,768,768]{2,1,0:T(8,128)(2,1)} %param.13) | copy-start | bytes 3538948
  86.8 2.1 %copy-start.9 = (bf16[1,768,1536]{2,1,0:T(8,128)(2,1)S(1)}, bf16[1,768,1536]{2,1,0:T(8,128)(2,1)}, u32[]{:S(2)}) copy-start(bf16[1,768,1536]{2,1,0:T(8,128)(2,1)} %param.14) | copy-start | bytes 7077892
  97.6 3.7 %copy-start.7 = (bf16[4,196,768]{1,2,0:T(8,128)(2,1)S(1)}, bf16[4,196,768]{1,2,0:T(8,128)(2,1)}, u32[]{:S(2)}) copy-start(bf16[4,196,768]{1,2,0:T(8,128)(2,1)} %copy.80) | copy-start | bytes 3612676
  101.3 2.4 %copy-start.5 = (f32[4,196,768]{2,1,0:T(8,128)S(1)}, f32[4,196,768]{2,1,0:T(8,128)}, u32[]{:S(2)}) copy-start(f32[4,196,768]{2,1,0:T(8,128)} %copy-done.4) | copy-start | bytes 7225348
  101.3 2.4 %copy-start.8 = (bf16[1,768,768]{2,1,0:T(8,128)(2,1)S(1)}, bf16[1,768,768]{2,1,0:T(8,128)(2,1)}, u32[]{:S(2)}) copy-start(bf16[1,768,768]{2,1,0:T(8,128)(2,1)} %param.15) | copy-start | bytes 3538948
  106.9 20.9 %copy-start.1 = (bf16[1,768,2304]{2,1,0:T(8,128)(2,1)S(1)}, bf16[1,768,2304]{2,1,0:T(8,128)(2,1)}, u32[]{:S(2)}) copy-start(bf16[1,768,2304]{2,1,0:T(8,128)(2,1)} %param.11) | copy-start | bytes 10616836
  107.8 16.3 %collective-permute-start.4 = (bf16[2,196,768]{2,0,1:T(2,128)(2,1)S(1)}, bf16[2,196,768]{2,0,1:T(2,128)(2,1)S(1)}, u32[]{:S(2)}, u32[]{:S(2)}) collective-permute-start(bf16[2,196,768]{2,0,1:T(2,128)(2,1)S(1)} %get-tuple-element.20), channel_id=1, source_target_pairs={{128,129},{129,130},{130,131},{131,132},{132,133},{133,134},{134,1... | collective-permute-start | bytes 1806344 | tf_op jit(solution)/shard_map/ppermute | solution.py:142
  109.9 15.7 %collective-permute-start.5 = (bf16[2,196,768]{2,0,1:T(2,128)(2,1)S(1)}, bf16[2,196,768]{2,0,1:T(2,128)(2,1)S(1)}, u32[]{:S(2)}, u32[]{:S(2)}) collective-permute-start(bf16[2,196,768]{2,0,1:T(2,128)(2,1)S(1)} %get-tuple-element.21), channel_id=1, source_target_pairs={{129,128},{130,129},{131,130},{132,131},{133,132},{134,133},{135,1... | collective-permute-start | bytes 1806344 | tf_op jit(solution)/shard_map/ppermute | solution.py:143
